TPU v7x, 32 devices: a whole 2x2x4 slice. The times are simulated.
32 devices in a mesh: seq: 16 (over z, y, x), feat: 2 (over core).
Axes of the slice: x: 2, y: 2, z: 4, core: 2. Of those that a mesh axis runs over, the one named last changes fastest.
Arguments:
- layer_input: bfloat16 [16384, 768], P(('seq', 'feat')), may hold values from -6 to 6
- ln1_gain: bfloat16 [768], replicated, may hold values from 0.25 to 1.75
- ln1_bias: bfloat16 [768], replicated, may hold values from -1.75 to 1.75
- w_qkv: bfloat16 [768, 2304], replicated, may hold values from -0.21875 to 0.21875
- b_qkv: bfloat16 [2304], replicated, may hold values from -1.75 to 1.75
- w_out: bfloat16 [768, 768], replicated, may hold values from -0.875 to 0.875
- b_out: bfloat16 [768], replicated, may hold values from -1.75 to 1.75
- ln2_gain: bfloat16 [768], replicated, may hold values from 0.25 to 1.75
- ln2_bias: bfloat16 [768], replicated, may hold values from -1.75 to 1.75
- w_up: bfloat16 [768, 3072], P(None, 'feat'), may hold values from -0.21875 to 0.21875
- b_up: bfloat16 [3072], P('feat'), may hold values from -1.75 to 1.75
- w_down: bfloat16 [3072, 768], P('feat'), may hold values from -0.109375 to 0.109375
- b_down: bfloat16 [768], replicated, may hold values from -1.75 to 1.75
- feature_signs: int32 [12, 64, 256], P(None, None, 'feat'), may hold values from 0 to 1
- match_blocks: int32 [16, 12, 16, 4], P('seq'), may hold values from 0 to 15, as said below
- match_count: int32 [16, 12, 16], P('seq'), may hold values from 1 to 4, as said below
- out_grad: bfloat16 [16384, 768], P(('seq', 'feat')), may hold values from -12 to 12
Outputs:
- layer_output: bfloat16 [16384, 768], P(('seq', 'feat'))
- d_input: float32 [16384, 768], P(('seq', 'feat'))
- d_ln1_gain: float32 [768], P(('seq', 'feat'))
- d_ln1_bias: float32 [768], P(('seq', 'feat'))
- d_w_qkv: float32 [768, 2304], P(('seq', 'feat'))
- d_b_qkv: float32 [2304], P(('seq', 'feat'))
- d_w_out: float32 [768, 768], P(('seq', 'feat'))
- d_b_out: float32 [768], P(('seq', 'feat'))
- d_ln2_gain: float32 [768], P(('seq', 'feat'))
- d_ln2_bias: float32 [768], P(('seq', 'feat'))
- d_w_up: float32 [768, 3072], P('seq', 'feat')
- d_b_up: float32 [3072], P(('feat', 'seq'))
- d_w_down: float32 [3072, 768], P('feat', 'seq')
- d_b_down: float32 [768], P(('seq', 'feat'))
Inputs may be any that keep to these rules, and one draw needn't show every extreme that they name: `match_blocks`: each list names distinct key blocks of the query block's own sequence; entries from match_count on are not used. `match_count`: some list holds 4 used entries in every draw.
All inputs are finite; a program needn't handle non-finite values.
Results may differ from a plain program's by a relative error of at most 0.025.
Values may be sent and summed in bfloat16 or wider, within the bound.
A program may use at most 192 MiB of HBM per device.

v0:
```python
import jax
import jax.numpy as jnp
from jax import lax
from jax.sharding import PartitionSpec as P

HEADS = 12
HEAD_DIM = 64
FEATS = 256
BLOCK = 64
MATCH = 4
SEQLEN = 1024
NB = 16


exact_mode = lax.Precision.HIGHEST
norm_epsilon = 1e-05


def norm_rows(values, gain, shift):
    center = values - jnp.mean(values, axis=-1, keepdims=True)
    inverse = lax.rsqrt(jnp.mean(center * center, axis=-1, keepdims=True) + norm_epsilon)
    normed = center * inverse
    return (normed * gain + shift, normed, inverse)


def norm_back(grad_out, normed, inverse, gain):
    scaled = grad_out * gain
    grad_in = inverse * (
        scaled
        - jnp.mean(scaled, axis=-1, keepdims=True)
        - normed * jnp.mean(scaled * normed, axis=-1, keepdims=True)
    )
    return (grad_in, jnp.sum(grad_out * normed, axis=0), jnp.sum(grad_out, axis=0))


def gelu_piece(values):
    return jax.nn.gelu(values, approximate=True)


def lift(tokens, sign_table):
    lifted = jnp.einsum(
        "ghd,hdf->ghf", tokens, sign_table, preferred_element_type=jnp.float32
    ) * HEAD_DIM ** (-0.25)
    widened = tokens.astype(jnp.float32)
    square = jnp.sum(widened * widened, axis=-1, keepdims=True) * (0.5 * HEAD_DIM ** (-0.5))
    return jnp.exp(lifted - square) * FEATS ** (-0.5)


def lift_back(tokens, raw_feats, grad_feats, sign_table):
    grad_lift = grad_feats * raw_feats
    grad_square = -jnp.sum(grad_lift, axis=-1, keepdims=True)
    grad_tokens = jnp.einsum(
        "ghf,hdf->ghd",
        grad_lift.astype(jnp.bfloat16),
        sign_table,
        preferred_element_type=jnp.float32,
    ) * HEAD_DIM ** (-0.25)
    return grad_tokens + grad_square * HEAD_DIM ** (-0.5) * tokens.astype(jnp.float32)


def body(
    layer_input,
    ln1_gain,
    ln1_bias,
    w_qkv,
    b_qkv,
    w_out,
    b_out,
    ln2_gain,
    ln2_bias,
    w_up,
    b_up,
    w_down,
    b_down,
    feature_signs,
    match_blocks,
    match_count,
    out_grad,
):
    tok_rows, model_width = layer_input.shape
    seq_here = match_blocks.shape[0]
    group_rows = seq_here * SEQLEN
    group_blocks = seq_here * NB
    own_blocks = tok_rows // BLOCK
    feat_index = lax.axis_index("feat")
    first_block = feat_index * own_blocks
    half_feats = feature_signs.shape[2]
    sign_table = (2 * feature_signs - 1).astype(jnp.bfloat16)
    score_scale = HEAD_DIM ** (-0.5)
    head_shape = (group_rows, HEADS, HEAD_DIM)
    input_wide = layer_input.astype(jnp.float32)
    ln_one, normed_one, inverse_one = norm_rows(
        input_wide, ln1_gain.astype(jnp.float32), ln1_bias.astype(jnp.float32)
    )
    h_one = ln_one.astype(jnp.bfloat16)
    qkv_own = (
        jnp.dot(h_one, w_qkv, preferred_element_type=jnp.float32) + b_qkv.astype(jnp.float32)
    ).astype(jnp.bfloat16)
    qkv_group = lax.all_gather(qkv_own, "feat", axis=0, tiled=True)
    queries = qkv_group[:, :model_width].reshape(head_shape)
    key_rows = qkv_group[:, model_width : 2 * model_width].reshape(head_shape)
    value_rows = qkv_group[:, 2 * model_width :].reshape(head_shape)
    raw_q = lift(queries, sign_table)
    raw_k = lift(key_rows, sign_table)
    split_feat = (seq_here, NB, BLOCK, HEADS, half_feats)
    split_head = (seq_here, NB, BLOCK, HEADS, HEAD_DIM)
    q_feats = raw_q.astype(jnp.bfloat16).reshape(split_feat)
    k_feats = raw_k.astype(jnp.bfloat16).reshape(split_feat)
    v_blocks = value_rows.reshape(split_head)
    key_state = jnp.einsum(
        "snkhf,snkhd->snhfd", k_feats, v_blocks, preferred_element_type=jnp.float32
    )
    key_sum = jnp.sum(k_feats.astype(jnp.float32), axis=2)
    slot_iota = lax.broadcasted_iota(jnp.int32, match_blocks.shape, 3)
    in_use = (slot_iota < match_count[..., None]).astype(jnp.float32)
    block_iota = jnp.arange(NB, dtype=jnp.int32)
    matched = jnp.sum(
        in_use[..., None] * (match_blocks[..., None] == block_iota).astype(jnp.float32), axis=3
    )
    unmatched = 1.0 - matched
    low_state = jnp.einsum("shbm,smhfd->sbhfd", unmatched, key_state, precision=exact_mode).astype(
        jnp.bfloat16
    )
    low_sum = jnp.einsum("shbm,smhf->sbhf", unmatched, key_sum, precision=exact_mode).astype(
        jnp.bfloat16
    )
    num_part = jnp.einsum(
        "sbqhf,sbhfd->sbqhd", q_feats, low_state, preferred_element_type=jnp.float32
    ).reshape(group_rows, model_width)
    den_part = jnp.einsum(
        "sbqhf,sbhf->sbqh", q_feats, low_sum, preferred_element_type=jnp.float32
    ).reshape(group_rows, HEADS)
    num_sum, den_sum = (
        lax.psum_scatter(
            num_part.astype(jnp.bfloat16), "feat", scatter_dimension=0, tiled=True
        ).astype(jnp.float32),
        lax.psum_scatter(
            den_part.astype(jnp.bfloat16), "feat", scatter_dimension=0, tiled=True
        ).astype(jnp.float32),
    )
    seq_base = jnp.arange(group_blocks, dtype=jnp.int32) // NB * NB
    list_group = (
        match_blocks.transpose(1, 0, 2, 3).reshape(HEADS, group_blocks, MATCH)
        + seq_base[None, :, None]
    )
    use_group = in_use.transpose(1, 0, 2, 3).reshape(HEADS, group_blocks, MATCH)
    own_lists = lax.dynamic_slice_in_dim(list_group, first_block, own_blocks, 1)
    own_use = lax.dynamic_slice_in_dim(use_group, first_block, own_blocks, 1)
    key_table = key_rows.reshape(group_blocks, BLOCK, HEADS, HEAD_DIM).transpose(2, 0, 1, 3)
    value_table = value_rows.reshape(group_blocks, BLOCK, HEADS, HEAD_DIM).transpose(2, 0, 1, 3)
    pick_rows = jax.vmap(lambda lookup_table, row_index: lookup_table[row_index])
    key_pick = pick_rows(key_table, own_lists)
    value_pick = pick_rows(value_table, own_lists)
    query_own = (
        qkv_own[:, :model_width].reshape(own_blocks, BLOCK, HEADS, HEAD_DIM).transpose(2, 0, 1, 3)
    )
    exp_scores = jnp.exp(
        jnp.einsum("hoqd,hojkd->hojqk", query_own, key_pick, preferred_element_type=jnp.float32)
        * score_scale
    )
    slot_mask = own_use[..., None, None].astype(jnp.bfloat16)
    exact_probs = exp_scores.astype(jnp.bfloat16) * slot_mask
    exact_num = (
        jnp.einsum("hojqk,hojkd->hoqd", exact_probs, value_pick, preferred_element_type=jnp.float32)
        .transpose(1, 2, 0, 3)
        .reshape(tok_rows, HEADS, HEAD_DIM)
    )
    exact_den = (
        jnp.sum(exact_probs.astype(jnp.float32), axis=(2, 4))
        .transpose(1, 2, 0)
        .reshape(tok_rows, HEADS)
    )
    numerator = num_sum.reshape(tok_rows, HEADS, HEAD_DIM) + exact_num
    denominator = den_sum + exact_den
    attended = (
        (numerator / denominator[..., None]).reshape(tok_rows, model_width).astype(jnp.bfloat16)
    )
    mixed = (
        input_wide
        + jnp.dot(attended, w_out, preferred_element_type=jnp.float32)
        + b_out.astype(jnp.float32)
    )
    ln_two, normed_two, inverse_two = norm_rows(
        mixed, ln2_gain.astype(jnp.float32), ln2_bias.astype(jnp.float32)
    )
    h_two = ln_two.astype(jnp.bfloat16)
    grad_wide = out_grad.astype(jnp.float32)
    up_full, down_full, bias_full = (
        lax.all_gather(w_up, "feat", axis=1, tiled=True),
        lax.all_gather(w_down, "feat", axis=0, tiled=True),
        lax.all_gather(b_up, "feat", axis=0, tiled=True),
    )
    pre_act = jnp.dot(h_two, up_full, preferred_element_type=jnp.float32) + bias_full.astype(
        jnp.float32
    )
    activation, gelu_back = jax.vjp(gelu_piece, pre_act)
    act_low = activation.astype(jnp.bfloat16)
    hidden_out = jnp.dot(act_low, down_full, preferred_element_type=jnp.float32)
    grad_act = jnp.einsum("rd,fd->rf", out_grad, down_full, preferred_element_type=jnp.float32)
    grad_pre = gelu_back(grad_act)[0].astype(jnp.bfloat16)
    up_terms = jnp.einsum("rd,rf->df", h_two, grad_pre, preferred_element_type=jnp.float32)
    down_terms = jnp.einsum("rf,rd->fd", act_low, out_grad, preferred_element_type=jnp.float32)
    bias_terms = jnp.sum(grad_pre.astype(jnp.float32), axis=0)
    grad_h_two = jnp.einsum("rf,df->rd", grad_pre, up_full, preferred_element_type=jnp.float32)
    up_grad, down_grad, up_bias_grad = (
        lax.psum_scatter(
            up_terms.astype(jnp.bfloat16), "feat", scatter_dimension=1, tiled=True
        ).astype(jnp.float32),
        lax.psum_scatter(
            down_terms.astype(jnp.bfloat16), "feat", scatter_dimension=0, tiled=True
        ).astype(jnp.float32),
        lax.psum_scatter(
            bias_terms.astype(jnp.bfloat16), "feat", scatter_dimension=0, tiled=True
        ).astype(jnp.float32),
    )
    layer_output = (mixed + hidden_out + b_down.astype(jnp.float32)).astype(jnp.bfloat16)
    grad_mixed_norm, ln2_gain_grad, ln2_bias_grad = norm_back(
        grad_h_two, normed_two, inverse_two, ln2_gain.astype(jnp.float32)
    )
    grad_mixed = grad_wide + grad_mixed_norm
    down_bias_grad = jnp.sum(grad_wide, axis=0)
    grad_branch = grad_mixed.astype(jnp.bfloat16)
    out_w_grad = jnp.einsum("rd,re->de", attended, grad_branch, preferred_element_type=jnp.float32)
    out_b_grad = jnp.sum(grad_branch.astype(jnp.float32), axis=0)
    grad_att = jnp.einsum(
        "re,de->rd", grad_branch, w_out, preferred_element_type=jnp.float32
    ).reshape(tok_rows, HEADS, HEAD_DIM)
    grad_num = (grad_att / denominator[..., None]).astype(jnp.bfloat16)
    grad_den = (-jnp.sum(grad_att * numerator, axis=-1) / (denominator * denominator)).astype(
        jnp.bfloat16
    )
    num_group, den_group = (
        lax.all_gather(grad_num.reshape(tok_rows, model_width), "feat", axis=0, tiled=True),
        lax.all_gather(grad_den, "feat", axis=0, tiled=True),
    )
    num_own = grad_num.reshape(own_blocks, BLOCK, HEADS, HEAD_DIM).transpose(2, 0, 1, 3)
    den_own = grad_den.reshape(own_blocks, BLOCK, HEADS).transpose(2, 0, 1).astype(jnp.float32)
    grad_probs = (
        jnp.einsum("hoqd,hojkd->hojqk", num_own, value_pick, preferred_element_type=jnp.float32)
        + den_own[:, :, None, :, None]
    ) * own_use[..., None, None]
    grad_scores = (grad_probs * exp_scores).astype(jnp.bfloat16)
    query_exact = (
        jnp.einsum("hojqk,hojkd->hoqd", grad_scores, key_pick, preferred_element_type=jnp.float32)
        .transpose(1, 2, 0, 3)
        .reshape(tok_rows, model_width)
        * score_scale
    )
    key_exact_pick = (
        jnp.einsum("hojqk,hoqd->hojkd", grad_scores, query_own, preferred_element_type=jnp.float32)
        * score_scale
    )
    value_exact_pick = jnp.einsum(
        "hojqk,hoqd->hojkd", exact_probs, num_own, preferred_element_type=jnp.float32
    )
    block_onehot = (own_lists[..., None] == jnp.arange(group_blocks, dtype=jnp.int32)).astype(
        jnp.float32
    )
    key_exact = jnp.einsum(
        "hojg,hojkd->gkhd", block_onehot, key_exact_pick, precision=exact_mode
    ).reshape(head_shape)
    value_exact = jnp.einsum(
        "hojg,hojkd->gkhd", block_onehot, value_exact_pick, precision=exact_mode
    ).reshape(head_shape)
    num_blocks = num_group.reshape(split_head)
    den_blocks = den_group.reshape(seq_here, NB, BLOCK, HEADS)
    grad_phi_q = (
        jnp.einsum("sbqhd,sbhfd->sbqhf", num_blocks, low_state, preferred_element_type=jnp.float32)
        + den_blocks.astype(jnp.float32)[..., None] * low_sum.astype(jnp.float32)[:, :, None]
    ).reshape(group_rows, HEADS, half_feats)
    grad_low_state = jnp.einsum(
        "sbqhf,sbqhd->sbhfd", q_feats, num_blocks, preferred_element_type=jnp.float32
    )
    grad_low_sum = jnp.einsum(
        "sbqhf,sbqh->sbhf", q_feats, den_blocks, preferred_element_type=jnp.float32
    )
    grad_key_state = jnp.einsum(
        "shbm,sbhfd->smhfd", unmatched, grad_low_state, precision=exact_mode
    ).astype(jnp.bfloat16)
    grad_key_sum = jnp.einsum("shbm,sbhf->smhf", unmatched, grad_low_sum, precision=exact_mode)
    grad_phi_k = (
        jnp.einsum(
            "snkhd,snhfd->snkhf", v_blocks, grad_key_state, preferred_element_type=jnp.float32
        )
        + grad_key_sum[:, :, None]
    ).reshape(group_rows, HEADS, half_feats)
    value_low = jnp.einsum(
        "snkhf,snhfd->snkhd", k_feats, grad_key_state, preferred_element_type=jnp.float32
    ).reshape(head_shape)
    grad_q = lift_back(queries, raw_q, grad_phi_q, sign_table)
    grad_k = lift_back(key_rows, raw_k, grad_phi_k, sign_table) + key_exact
    grad_v = value_low + value_exact
    q_summed, k_summed, v_summed = (
        lax.psum_scatter(
            grad_q.reshape(group_rows, model_width).astype(jnp.bfloat16),
            "feat",
            scatter_dimension=0,
            tiled=True,
        ).astype(jnp.float32),
        lax.psum_scatter(
            grad_k.reshape(group_rows, model_width).astype(jnp.bfloat16),
            "feat",
            scatter_dimension=0,
            tiled=True,
        ).astype(jnp.float32),
        lax.psum_scatter(
            grad_v.reshape(group_rows, model_width).astype(jnp.bfloat16),
            "feat",
            scatter_dimension=0,
            tiled=True,
        ).astype(jnp.float32),
    )
    grad_qkv = jnp.concatenate([q_summed + query_exact, k_summed, v_summed], axis=1).astype(
        jnp.bfloat16
    )
    qkv_w_grad = jnp.einsum("rd,re->de", h_one, grad_qkv, preferred_element_type=jnp.float32)
    qkv_b_grad = jnp.sum(grad_qkv.astype(jnp.float32), axis=0)
    grad_h_one = jnp.einsum("re,de->rd", grad_qkv, w_qkv, preferred_element_type=jnp.float32)
    grad_in_norm, ln1_gain_grad, ln1_bias_grad = norm_back(
        grad_h_one, normed_one, inverse_one, ln1_gain.astype(jnp.float32)
    )
    d_input = grad_mixed + grad_in_norm
    shared = (
        lax.psum_scatter(qkv_w_grad, ("seq", "feat"), scatter_dimension=0, tiled=True),
        lax.psum_scatter(qkv_b_grad, ("seq", "feat"), scatter_dimension=0, tiled=True),
        lax.psum_scatter(out_w_grad, ("seq", "feat"), scatter_dimension=0, tiled=True),
        lax.psum_scatter(out_b_grad, ("seq", "feat"), scatter_dimension=0, tiled=True),
        lax.psum_scatter(ln1_gain_grad, ("seq", "feat"), scatter_dimension=0, tiled=True),
        lax.psum_scatter(ln1_bias_grad, ("seq", "feat"), scatter_dimension=0, tiled=True),
        lax.psum_scatter(ln2_gain_grad, ("seq", "feat"), scatter_dimension=0, tiled=True),
        lax.psum_scatter(ln2_bias_grad, ("seq", "feat"), scatter_dimension=0, tiled=True),
        lax.psum_scatter(down_bias_grad, ("seq", "feat"), scatter_dimension=0, tiled=True),
    )
    hidden = (
        lax.psum_scatter(up_grad, "seq", scatter_dimension=0, tiled=True),
        lax.psum_scatter(down_grad, "seq", scatter_dimension=1, tiled=True),
        lax.psum_scatter(up_bias_grad, "seq", scatter_dimension=0, tiled=True),
    )
    return (
        layer_output,
        d_input,
        shared[4],
        shared[5],
        shared[0],
        shared[1],
        shared[2],
        shared[3],
        shared[6],
        shared[7],
        hidden[0],
        hidden[2],
        hidden[1],
        shared[8],
    )


def solution(mesh):
    return jax.shard_map(
        body,
        mesh=mesh,
        in_specs=(
            P(("seq", "feat"), None),
            P(),
            P(),
            P(),
            P(),
            P(),
            P(),
            P(),
            P(),
            P(None, "feat"),
            P("feat"),
            P("feat", None),
            P(),
            P(None, None, "feat"),
            P("seq", None, None, None),
            P("seq", None, None),
            P(("seq", "feat"), None),
        ),
        out_specs=(
            P(("seq", "feat"), None),
            P(("seq", "feat"), None),
            P(("seq", "feat")),
            P(("seq", "feat")),
            P(("seq", "feat"), None),
            P(("seq", "feat")),
            P(("seq", "feat"), None),
            P(("seq", "feat")),
            P(("seq", "feat")),
            P(("seq", "feat")),
            P("seq", "feat"),
            P(("feat", "seq")),
            P("feat", "seq"),
            P(("seq", "feat")),
        ),
        check_vma=False,
    )
```

profile of v0, /device:TPU:0, one launch (start us, length us, event | category | flops | bytes accessed | tf_op | source)
XLA Modules:
  0.0 1016.9 jit_solution(3722970176871566917)
XLA Ops:
  12.3 4.7 fusion.28
  21.2 13.2 %all-gather.6.cloned.1.call-done = bf16[1024,2304]{1,0:T(8,128)(2,1)} async-done(((bf16[512,2304]{1,0:T(8,128)(2,1)}), bf16[1024,2304]{1,0:T(8,128)(2,1)}) %all-gather.6.cloned.1.call-update) | async-done | bytes 4718608 | tf_op jit(solution)/shard_map/all_gather | solution.py:99
  34.4 4.7 fusion.156
  46.9 5.3 reshape.351
  57.1 5.0 copy.205
  62.2 6.7 fusion.25
  68.9 4.7 copy.167
  80.9 9.4 convert_bitcast_fusion.2
  90.3 5.3 fusion.27
  95.6 4.7 copy.173
  106.1 4.7 convert_bitcast_fusion.1
  110.8 4.1 copy.176
  115.0 5.4 convert_element_type.279
  134.4 4.2 reshape.407
  139.4 6.0 reshape.406
  145.5 5.4 copy.182
  150.8 4.7 copy.321
  155.5 7.1 gather_fusion.1
  162.6 6.4 gather_fusion
  170.6 9.9 fusion.100
  180.5 10.0 convert_reduce_fusion
  192.0 8.5 fusion.158
  207.2 3.9 reshape.356
  223.8 8.2 fusion.152
  232.1 9.8 fusion.153
  269.0 11.0 %fusion.14 = bf16[12,8,4,64,64]{3,4,2,1,0:T(8,128)(2,1)} fusion(f32[12,8,4,64,64]{4,3,2,1,0:T(8,128)} %fusion.100, f32[12,8,4]{2,1,0:T(8,128)} %get-tuple-element.97, f32[12,8,64]{2,1,0:T(8,128)} %bitcast.297, bf16[12,8,4,64,64]{4,3,2,1,0:T(8,128)(2,1)} %bitcast.272, bf16[12,8,64,64,1]{3,2,4,1,0:T(8,128)(2,1)} %copy.227), kind=kOutput, calls=%fused_computation.21 | convolution fusion | flops 209190912 | bytes 13395456 | tf_op jit(solution)/shard_map/hoqd,hojkd->hojqk/dot_general | solution.py:239
  286.6 4.7 broadcast_multiply_fusion
  291.3 11.3 %fusion.61 = f32[16,64,12,64]{3,0,1,2:T(8,128)} fusion(f32[12,8,4,64,64]{4,3,2,1,0:T(8,128)S(1)} %broadcast_multiply_fusion, s32[12,8,4]{1,2,0:T(4,128)S(1)} %copy-done.32), kind=kOutput, calls=%fused_computation.82 | convolution fusion | flops 301996032 | bytes 9438720 | tf_op jit(solution)/shard_map/hojg,hojkd->gkhd/dot_general | solution.py:259
  302.6 7.7 copy.212
  310.2 6.3 reshape.368
  316.5 5.9 reshape.413
  322.4 6.9 copy.201
  329.3 5.0 bitcast_add_fusion
  337.6 6.6 copy.194
  344.2 6.6 fusion.103
  351.0 6.1 fusion.35
  361.1 8.1 convert_bitcast_fusion
  375.9 6.7 copy.209
  382.6 6.7 fusion.105
  390.3 6.3 fusion.32
  396.7 4.6 fusion.159
  401.3 11.3 %fusion.64 = f32[16,64,12,64]{3,0,1,2:T(8,128)} fusion(f32[12,8,4,64,64]{4,3,2,1,0:T(8,128)S(1)} %fusion.159, s32[12,8,4]{1,2,0:T(4,128)S(1)} %copy-done.33), kind=kOutput, calls=%fused_computation.83 | convolution fusion | flops 301996032 | bytes 9438720 | tf_op jit(solution)/shard_map/hojg,hojkd->gkhd/dot_general | solution.py:262
  412.6 7.6 copy.218
  420.1 6.7 reshape.370
  426.8 4.7 fusion.56
  431.5 6.9 copy.215
  438.5 6.3 reshape.369
  444.8 4.5 add_convert_fusion
  449.4 7.4 convolution_convert_fusion.1
  457.5 9.1 convolution_convert_fusion
  466.7 3.9 fusion.136
  470.6 10.1 fusion.36
  484.3 4.3 mul.388
  491.7 7.0 fusion.148
  498.9 4.5 convert_element_type.329
  503.5 4.6 copy.249
  515.8 43.5 %all-reduce.7 = f32[1536]{0:T(1024)} all-reduce(f32[1536]{0:T(1024)S(1)} %dynamic-slice_convert_fusion), channel_id=18, replica_groups=mesh['seq'=16,'feat'=2] {'seq'}, use_global_device_ids=true, to_apply=%region_39.40.clone | all-reduce | flops 1536 | bytes 12288
  560.7 9.6 add_convert_fusion.2
  570.7 4.2 fusion.96
  574.8 38.4 %all-reduce.9 = (f32[768]{0:T(1024)}, f32[768]{0:T(1024)}, f32[2304]{0:T(1024)}, f32[768]{0:T(1024)}, f32[768]{0:T(1024)}, /*index=5*/f32[768]{0:T(1024)}, f32[768]{0:T(1024)}) all-reduce(f32[768]{0:T(1024)} %get-tuple-element.72, f32[768]{0:T(1024)} %get-tuple-element.77, ...), channel_id=7, replica_groups=mesh['seq'=16,'feat'=2] {'seq','feat'}, use_global_device_ids=true, to_apply=%region_22.23.clone | all-reduce | flops 6912 | bytes 55296
  623.4 3.9 fusion.95
  627.4 96.1 %reduce-scatter.24.cloned.1.call-done = f32[24,2304]{1,0:T(8,128)} async-done(((f32[768,2304]{1,0:T(8,128)}), f32[24,2304]{1,0:T(8,128)}) %reduce-scatter.24.cloned.1.call-update) | async-done | bytes 221200 | tf_op jit(solution)/shard_map/reduce_scatter | solution.py:324
  723.5 143.5 %reduce-scatter.30.cloned.1.call-done = f32[48,1536]{1,0:T(8,128)} async-done(((f32[768,1536]{1,0:T(8,128)}), f32[48,1536]{1,0:T(8,128)}) %reduce-scatter.30.cloned.1.call-update) | async-done | bytes 294928 | tf_op jit(solution)/shard_map/reduce_scatter | solution.py:335
  867.0 143.1 %reduce-scatter.34.cloned.1.call-done = f32[48,1536]{1,0:T(8,128)} async-done(((f32[768,1536]{1,0:T(8,128)}), f32[48,1536]{1,0:T(8,128)}) %reduce-scatter.34.cloned.1.call-update) | async-done | bytes 294928
  (258 shorter events, 147.2 us)
Async XLA Ops:
  7.2 5.2 copy-start
  7.2 27.2 %all-gather.6.cloned.1.call-start = ((), (), s32[]{:S(2)}) async-start(), calls=%async_computation.11 | async-start | bytes 7077888 | tf_op jit(solution)/shard_map/all_gather | solution.py:99
  8.7 3.6 copy-start.36
  17.1 194.1 %reduce-scatter.16.cloned.1.call-start = ((), (), s32[]{:S(2)}) async-start(), calls=%async_computation.13 | async-start | bytes 49152 | tf_op jit(solution)/shard_map/reduce_scatter | solution.py:137
  73.6 3.2 copy-start.21
  73.6 4.1 copy-start.3
  80.8 9.4 copy-start.8
  80.8 9.4 copy-start.16
  80.8 9.4 copy-start.25
  106.1 113.1 %reduce-scatter.14.cloned.1.call-start = ((), (), s32[]{:S(2)}) async-start(), calls=%async_computation.12 | async-start | bytes 2359296 | tf_op jit(solution)/shard_map/reduce_scatter | solution.py:134
  120.4 7.1 copy-start.56
  120.4 103.5 %all-gather.8.cloned.1.call-start = ((), (), s32[]{:S(2)}) async-start(), calls=%async_computation.14 | async-start | bytes 7077888 | tf_op jit(solution)/shard_map/all_gather | solution.py:189
  121.0 111.1 %all-gather.10.cloned.1.call-start = ((), (), s32[]{:S(2)}) async-start(), calls=%async_computation.15 | async-start | bytes 7077888 | tf_op jit(solution)/shard_map/all_gather | solution.py:190
  121.5 195.0 %all-gather.12.cloned.1.call-start = ((), (), s32[]{:S(2)}) async-start(), calls=%async_computation.16 | async-start | bytes 2359296 | tf_op jit(solution)/shard_map/all_gather | solution.py:233
  124.9 120.6 %copy-start.43 = (f32[768]{0:T(1024)}, f32[768]{0:T(1024)S(1)}, u32[]{:S(2)}) copy-start(f32[768]{0:T(1024)S(1)} %convert_element_type.296) | copy-start | bytes 9220
  170.6 9.9 copy-start.34
  216.1 5.1 copy-start.55
  222.4 23.1 %copy-start.38 = (f32[512]{0:T(512)}, f32[512]{0:T(512)S(1)}, u32[]{:S(2)}) copy-start(f32[512]{0:T(512)S(1)} %broadcast_multiply_fusion.7) | copy-start | bytes 6148
  223.8 21.7 %copy-start.49 = (f32[512]{0:T(512)}, f32[512]{0:T(512)S(1)}, u32[]{:S(2)}) copy-start(f32[512]{0:T(512)S(1)} %add_rsqrt_fusion) | copy-start | bytes 6148
  232.1 9.9 copy-start.15
  232.1 9.9 copy-start.57
  241.9 3.5 copy-start.61
  241.9 3.6 copy-start.28
  246.8 2.6 copy-start.10
  261.3 227.2 %reduce-scatter.18.cloned.1.call-start = ((), (), s32[]{:S(2)}) async-start(), calls=%async_computation.17 | async-start | bytes 2359296 | tf_op jit(solution)/shard_map/reduce_scatter | solution.py:294
  269.0 11.0 %copy-start.5 = (bf16[1024,12,128]{2,0,1:T(8,128)(2,1)S(1)}, bf16[1024,12,128]{2,0,1:T(8,128)(2,1)}, u32[]{:S(2)}) copy-start(bf16[1024,12,128]{2,0,1:T(8,128)(2,1)} %copy.173) | copy-start | bytes 9437188
  269.0 11.0 %copy-start.35 = (bf16[16,64,12,1]{1,0,2,3:T(8,128)(2,1)S(1)}, bf16[16,64,12,1]{1,0,2,3:T(8,128)(2,1)}, u32[]{:S(2)}) copy-start(bf16[16,64,12,1]{1,0,2,3:T(8,128)(2,1)} %reshape.400) | copy-start | bytes 73732
  286.6 4.7 copy-start.32
  344.1 6.7 copy-start.2
  344.1 6.9 copy-start.9
  344.1 6.9 copy-start.17
  344.1 6.9 copy-start.26
  357.1 134.5 %reduce-scatter.20.cloned.1.call-start = ((), (), s32[]{:S(2)}) async-start(), calls=%async_computation.18 | async-start | bytes 2359296 | tf_op jit(solution)/shard_map/reduce_scatter | solution.py:300
  357.2 3.9 copy-start.22
  361.0 9.8 copy-start.4
  361.1 9.8 copy-start.31
  382.5 6.7 copy-start.1
  382.5 6.9 copy-start.7
  382.5 7.8 copy-start.11
  382.5 7.8 copy-start.18
  382.6 7.8 copy-start.24
  396.7 95.0 %reduce-scatter.22.cloned.1.call-start = ((), (), s32[]{:S(2)}) async-start(), calls=%async_computation.19 | async-start | bytes 2359296 | tf_op jit(solution)/shard_map/reduce_scatter | solution.py:306
  396.7 4.6 copy-start.33
  444.8 4.6 copy-start.39
  444.8 4.6 copy-start.44
  444.8 4.6 copy-start.50
  444.8 4.6 copy-start.54
  449.3 49.5 %reduce-scatter.28.cloned.1.call-start = ((), (), s32[]{:S(2)}) async-start(), calls=%async_computation.22 | async-start | bytes 7077888 | tf_op jit(solution)/shard_map/reduce_scatter | solution.py:206
  456.8 46.7 %reduce-scatter.32.cloned.1.call-start = ((), (), s32[]{:S(2)}) async-start(), calls=%async_computation.24 | async-start | bytes 7077888 | tf_op jit(solution)/shard_map/reduce_scatter | solution.py:209
  466.6 160.8 %reduce-scatter.26.cloned.1.call-start = ((), (), s32[]{:S(2)}) async-start(), calls=%async_computation.21 | async-start | bytes 2433024 | tf_op jit(solution)/shard_map/reduce_scatter | solution.py:326
  470.6 252.9 %reduce-scatter.24.cloned.1.call-start = ((), (), s32[]{:S(2)}) async-start(), calls=%async_computation.20 | async-start | bytes 7299072 | tf_op jit(solution)/shard_map/reduce_scatter | solution.py:324
  484.2 7.4 copy-start.37
  484.2 7.4 copy-start.41
  484.3 7.4 copy-start.47
  484.3 7.4 copy-start.53
  498.8 368.2 %reduce-scatter.30.cloned.1.call-start = ((), (), s32[]{:S(2)}) async-start(), calls=%async_computation.23 | async-start | bytes 5013504 | tf_op jit(solution)/shard_map/reduce_scatter | solution.py:335
  503.4 506.7 %reduce-scatter.34.cloned.1.call-start = ((), (), s32[]{:S(2)}) async-start(), calls=%async_computation.25 | async-start | bytes 5013504
  508.1 3.9 copy-start.51
  560.6 9.6 copy-start.20
  560.6 9.6 copy-start.29
  560.6 9.6 copy-start.30
  560.6 10.0 copy-start.13
  560.6 10.0 copy-start.42
  560.6 10.0 copy-start.48
  (13 other events, 21.4 us)
Sparse Core Ops, SparseCore 0:
  17.2 17.1 all-gather.5
  106.2 8.6 reduce-scatter.15
  120.5 10.0 reduce-scatter.13
  132.0 15.7 all-gather.7
  149.2 15.5 all-gather.9
  261.5 11.0 all-gather.11
  357.3 10.1 reduce-scatter.17
  396.8 10.1 reduce-scatter.19
  449.4 10.1 reduce-scatter.21
  461.8 13.6 reduce-scatter.27
  477.8 13.7 reduce-scatter.31
  497.4 101.1 reduce-scatter.25
  604.9 118.5 reduce-scatter.23
  729.1 137.8 reduce-scatter.29
  872.6 137.5 reduce-scatter.33
where the time goes:
time: 1020 us
  waiting for transfers between devices  397 us (39%)
  local copies, waits for them, and re-layouts  223 us (22%)
  matrix products  214 us (21%)
  blocking collectives  88.8 us (9%)
  other arithmetic  76.6 us (8%)
  between operations  16.2 us (2%)
    unnamed x16, waiting for transfers between devices  144 us
    reduce_scatter x1, waiting for transfers between devices, body(): lax.psum_scatter(up_grad, 'seq', scatter_dimension=0, tiled=True)  144 us
    reduce_scatter x1, waiting for transfers between devices, body(): lax.psum_scatter(qkv_w_grad, ('seq', 'feat'), scatter_dimension=0, tiled=...  96.1 us
    unnamed x3, blocking collectives  85 us
    another operation x5, local copies, waits for them, and re-layouts  28.4 us
    unnamed x137, local copies, waits for them, and re-layouts  22.6 us
  transfers between devices with their start and end apart: 15, of which 4 were waited for; matrix products, arithmetic and copies ran while one was open for 35% of the time, Pallas kernels for 0%

commit v1 on v0

v1 whole, which is shorter than its diff:
```python
import functools
import math

import jax
import jax.numpy as jnp
from jax import lax
from jax.experimental import pallas as pl
from jax.experimental.pallas import tpu as pltpu
from jax.sharding import PartitionSpec as P

HEADS = 12
HEAD_DIM = 64
BLOCK = 64
NB = 16
SEQLEN = NB * BLOCK
BF = jnp.bfloat16
F32 = jnp.float32
EPS = 1e-05
TILE = 256
GELU_A = math.sqrt(2.0 / math.pi)
GELU_B = 0.044715
VMEM = pl.BlockSpec(memory_space=pltpu.VMEM)
ANY = pl.BlockSpec(memory_space=pl.ANY)


def nn(a, b):
    return lax.dot_general(a, b, (((1,), (0,)), ((), ())), preferred_element_type=F32)


def nt(a, b):
    return lax.dot_general(a, b, (((1,), (1,)), ((), ())), preferred_element_type=F32)


def tn(a, b):
    return lax.dot_general(a, b, (((0,), (0,)), ((), ())), preferred_element_type=F32)


def ds(i, n):
    return pl.ds(i * n if isinstance(i, int) else pl.multiple_of(i * n, n), n)


def norm(x):
    c = x - jnp.mean(x, axis=-1, keepdims=True)
    inv = lax.rsqrt(jnp.mean(c * c, axis=-1, keepdims=True) + EPS)
    return c * inv, inv


def norm_back(g, normed, inv, gain):
    a = g * gain
    return inv * (
        a
        - jnp.mean(a, axis=-1, keepdims=True)
        - normed * jnp.mean(a * normed, axis=-1, keepdims=True)
    )


def call(body, outs, ins, specs=None, scratch=(), name=None):
    return pl.pallas_call(
        body,
        out_shape=[jax.ShapeDtypeStruct(s, d) for s, d in outs],
        in_specs=specs or [VMEM] * len(ins),
        out_specs=[VMEM] * len(outs),
        scratch_shapes=list(scratch),
        compiler_params=pltpu.CompilerParams(vmem_limit_bytes=64000 * 1024),
        name=name,
    )(*ins)


def qkv_body(x_ref, g_ref, s_ref, w_ref, b_ref, h_ref, qkv_ref):
    gain = g_ref[...].astype(F32)
    shift = s_ref[...].astype(F32)
    bias = b_ref[...].astype(F32)

    def step(i, _):
        rows = ds(i, TILE)
        normed, _inv = norm(x_ref[rows, :].astype(F32))
        h = (normed * gain + shift).astype(BF)
        h_ref[rows, :] = h
        qkv_ref[rows, :] = (nn(h, w_ref[...]) + bias).astype(BF)
        return 0

    lax.fori_loop(0, x_ref.shape[0] // TILE, step, 0)


def head_parts(qkv_ref, h):
    own = qkv_ref.shape[1] // 3
    p, e = h // 2, h % 2
    lane = lax.broadcasted_iota(jnp.int32, (1, 128), 1)
    mine = (lane // HEAD_DIM) == e

    def cols(part):
        return pl.ds(pl.multiple_of(part * own + p * 128, 128), 128)

    return p, e, lane, mine, cols


def lift_all(qkv_ref, s_ref, h, pq_ref, pk_ref):
    p, e, lane, mine, cols = head_parts(qkv_ref, h)
    feats = pq_ref.shape[1]
    signs = s_ref[p, :, ds(e, feats)]

    def step(i, _):
        rows = ds(i, TILE)
        for part, out in ((0, pq_ref), (1, pk_ref)):
            t = qkv_ref[rows, cols(part)]
            w = jnp.where(mine, t.astype(F32), 0.0)
            sq = jnp.sum(w * w, axis=-1, keepdims=True) * (0.5 * HEAD_DIM ** (-0.5))
            lifted = nn(t, signs) * HEAD_DIM ** (-0.25)
            out[rows, :] = (jnp.exp(lifted - sq) * feats ** (-0.5)).astype(BF)
        return 0

    lax.fori_loop(0, qkv_ref.shape[0] // TILE, step, 0)


def att_body(qkv_ref, s_ref, m_ref, att_ref, den_ref, pq_ref, pk_ref):
    def head(h, _):
        p, e, lane, mine, cols = head_parts(qkv_ref, h)
        lift_all(qkv_ref, s_ref, h, pq_ref, pk_ref)
        zero = jnp.zeros((), BF)
        v_one = jnp.where(mine, qkv_ref[:, cols(2)], jnp.ones((), BF))

        def step(i, _):
            rows = ds(i, TILE)
            q = jnp.where(mine, qkv_ref[rows, cols(0)] * BF(HEAD_DIM ** (-0.5)), zero)
            ex = jnp.exp(nt(q, qkv_ref[:, cols(1)]))
            low = nt(pq_ref[rows, :], pk_ref[...])
            per = TILE // BLOCK
            marks = m_ref[h, i]
            probs = jnp.concatenate(
                [
                    jnp.where(
                        marks[j : j + 1, :] > 0.5,
                        ex[j * BLOCK : (j + 1) * BLOCK],
                        low[j * BLOCK : (j + 1) * BLOCK],
                    )
                    for j in range(per)
                ],
                axis=0,
            ).astype(BF)
            both = nn(probs, v_one)
            den = pltpu.roll(both, HEAD_DIM, 1)
            out_cols = ds(p, 128)
            att = (both / den).astype(BF)
            att_ref[rows, out_cols] = jnp.where(mine, att, att_ref[rows, out_cols])
            den_ref[rows, out_cols] = jnp.where(mine, den, den_ref[rows, out_cols])
            return 0

        lax.fori_loop(0, qkv_ref.shape[0] // TILE, step, 0)
        return 0

    lax.fori_loop(0, qkv_ref.shape[1] // (3 * HEAD_DIM), head, 0)


def mix_body(x_ref, mine_ref, other_ref, w_ref, b_ref, g_ref, s_ref, mixed_ref, h_ref):
    f = lax.axis_index("feat")
    half = mine_ref.shape[1]

    def step(i, _):
        rows = ds(i, TILE)
        mixed = (
            x_ref[rows, :].astype(F32)
            + nn(mine_ref[rows, :], w_ref[ds(f, half), :])
            + nn(other_ref[rows, :], w_ref[ds(1 - f, half), :])
            + b_ref[...].astype(F32)
        )
        mixed_ref[rows, :] = mixed
        normed, _inv = norm(mixed)
        h_ref[rows, :] = (normed * g_ref[...].astype(F32) + s_ref[...].astype(F32)).astype(BF)
        return 0

    lax.fori_loop(0, x_ref.shape[0] // TILE, step, 0)


def ff_body(h_ref, og_ref, up_ref, down_ref, b_ref, act_ref, gp_ref, hid_ref, gh_ref, db_ref):
    db_ref[...] = jnp.zeros_like(db_ref)

    def step(i, _):
        rows = ds(i, TILE)
        v = nn(h_ref[rows, :], up_ref[...]) + b_ref[...].astype(F32)
        vv = v * v
        th = jnp.tanh(GELU_A * v * (1.0 + GELU_B * vv))
        half = 0.5 + 0.5 * th
        act = (v * half).astype(BF)
        slope = half + (0.5 * GELU_A) * v * (1.0 - th * th) * (1.0 + (3.0 * GELU_B) * vv)
        act_ref[rows, :] = act
        hid_ref[rows, :] = nn(act, down_ref[...]).astype(BF)
        gp = nt(og_ref[rows, :], down_ref[...]) * slope
        gpl = gp.astype(BF)
        gp_ref[rows, :] = gpl
        db_ref[...] += jnp.sum(gpl.astype(F32), axis=0, keepdims=True)
        gh_ref[rows, :] = nt(gpl, up_ref[...]).astype(BF)
        return 0

    lax.fori_loop(0, h_ref.shape[0] // TILE, step, 0)


def ffw_body(h_ref, og_ref, act_ref, gp_ref, up_ref, down_ref):
    def step(i, _):
        rows = ds(i, TILE)
        up_ref[rows, :] = tn(h_ref[:, rows], gp_ref[...]).astype(BF)
        down_ref[rows, :] = tn(og_ref[:, rows], act_ref[...]).astype(BF)
        return 0

    lax.fori_loop(0, h_ref.shape[1] // TILE, step, 0)


def outb_body(
    gh_ref, gho_ref, mixed_ref, og_ref, hid_ref, hido_ref, bd_ref, g_ref, w_ref, mine_ref, other_ref,
    gm_ref, gatt_ref, dw_ref, y_ref, vec_ref, gb_ref,
):
    f = lax.axis_index("feat")
    half = mine_ref.shape[1]
    tiles = mixed_ref.shape[0] // TILE
    own = tiles // 2
    gain = g_ref[...].astype(F32)
    vec_ref[...] = jnp.zeros_like(vec_ref)

    def step(i, _):
        rows = ds(i, TILE)
        mixed = mixed_ref[rows, :]
        og = og_ref[rows, :].astype(F32)
        normed, inv = norm(mixed)
        g = gh_ref[rows, :].astype(F32) + gho_ref[rows, :].astype(F32)
        gm = og + norm_back(g, normed, inv, gain)
        gm_ref[rows, :] = gm
        gb = gm.astype(BF)
        gb_ref[rows, :] = gb
        gatt_ref[rows, :] = nt(gb, w_ref[ds(f, half), :])

        @pl.when(i < own)
        def _():
            y_ref[rows, :] = (
                mixed + hid_ref[rows, :].astype(F32) + hido_ref[rows, :].astype(F32) + bd_ref[...].astype(F32)
            ).astype(BF)
            for j, term in enumerate((g * normed, g, gb.astype(F32), og)):
                vec_ref[j : j + 1, :] += jnp.sum(term, axis=0, keepdims=True)

        return 0

    lax.fori_loop(0, tiles, step, 0)
    gb_own = gb_ref[:, ds(f, half)]
    dw_ref[ds(f, half), :] = tn(mine_ref[...], gb_own).astype(BF)
    dw_ref[ds(1 - f, half), :] = tn(other_ref[...], gb_own).astype(BF)


def attb_body(
    qkv_ref, s_ref, m_ref, att_ref, den_ref, gatt_ref,
    gqkv_ref, pq_ref, pk_ref, gn_ref, gq_ref, gpq_ref,
):
    rows_all = qkv_ref.shape[0]
    scale = HEAD_DIM ** (-0.5)

    def head(h, _):
        p, e, lane, mine, cols = head_parts(qkv_ref, h)
        feats = pq_ref.shape[1]
        zero = jnp.zeros((), BF)
        lift_all(qkv_ref, s_ref, h, pq_ref, pk_ref)
        first_other = (1 - e) * HEAD_DIM

        def prep(i, _):
            rows = ds(i, TILE)
            inv = 1.0 / den_ref[rows, ds(p, 128)]
            ga = jnp.where(mine, gatt_ref[rows, ds(p, 128)] * inv, 0.0)
            gd = -jnp.sum(ga * att_ref[rows, ds(p, 128)].astype(F32), axis=-1, keepdims=True)
            gn_ref[rows, :] = jnp.where(lane == first_other, gd, ga).astype(BF)
            return 0

        lax.fori_loop(0, rows_all // TILE, prep, 0)
        gq_ref[...] = jnp.zeros_like(gq_ref)
        gpq_ref[...] = jnp.zeros_like(gpq_ref)
        signs = s_ref[p, :, ds(e, feats)]

        def lift_back(t, raw, g_phi):
            gl = g_phi * raw.astype(F32)
            gt = nt(gl.astype(BF), signs) * HEAD_DIM ** (-0.25)
            return gt - jnp.sum(gl, axis=-1, keepdims=True) * (scale * t.astype(F32))

        def put(part, rows, value):
            gqkv_ref[rows, cols(part)] = jnp.where(mine, value.astype(BF), gqkv_ref[rows, cols(part)])

        def step(i, _):
            rows = ds(i, TILE)
            k = jnp.where(mine, qkv_ref[rows, cols(1)] * BF(scale), zero)
            v_one = jnp.where(mine, qkv_ref[rows, cols(2)], jnp.ones((), BF))
            q_all = qkv_ref[:, cols(0)]
            pk = pk_ref[rows, :]
            ex = jnp.exp(nt(k, q_all))
            low = nt(pk, pq_ref[...])
            da = nt(v_one, gn_ref[...])
            per = TILE // BLOCK
            marks = m_ref[h, i]
            probs, dl, gs = [], [], []
            for j in range(per):
                part = slice(j * BLOCK, (j + 1) * BLOCK)
                on = marks[j : j + 1, :] > 0.5
                exj, daj = ex[part], da[part]
                probs.append(jnp.where(on, exj, low[part]))
                dl.append(jnp.where(on, 0.0, daj))
                gs.append(jnp.where(on, daj * exj, 0.0))
            probs = jnp.concatenate(probs, axis=0).astype(BF)
            dl = jnp.concatenate(dl, axis=0).astype(BF)
            gs = jnp.concatenate(gs, axis=0).astype(BF)
            put(2, rows, nn(probs, gn_ref[...]))
            g_phi_k = nn(dl, pq_ref[...])
            gk = nn(gs, q_all) * scale + lift_back(qkv_ref[rows, cols(1)], pk, g_phi_k)
            put(1, rows, gk)
            gpq_ref[...] += tn(dl, pk)
            gq_ref[...] += tn(gs, k)
            return 0

        lax.fori_loop(0, rows_all // TILE, step, 0)

        def last(i, _):
            rows = ds(i, TILE)
            gq = gq_ref[rows, :] + lift_back(qkv_ref[rows, cols(0)], pq_ref[rows, :], gpq_ref[rows, :])
            put(0, rows, gq)
            return 0

        lax.fori_loop(0, rows_all // TILE, last, 0)
        return 0

    lax.fori_loop(0, qkv_ref.shape[1] // (3 * HEAD_DIM), head, 0)


def qkvb_body(gqkv_ref, h_ref, w_ref, gh_ref, dw_ref, db_ref):
    db_ref[...] = jnp.zeros_like(db_ref)

    def step(i, _):
        rows = ds(i, TILE)
        g = gqkv_ref[rows, :]
        db_ref[...] += jnp.sum(g.astype(F32), axis=0, keepdims=True)
        gh_ref[rows, :] = nt(g, w_ref[...]).astype(BF)
        return 0

    lax.fori_loop(0, gqkv_ref.shape[0] // TILE, step, 0)

    def weight(i, _):
        rows = ds(i, TILE)
        dw_ref[rows, :] = tn(h_ref[:, rows], gqkv_ref[...]).astype(BF)
        return 0

    lax.fori_loop(0, h_ref.shape[1] // TILE, weight, 0)


def ln1b_body(gh_ref, gho_ref, x_ref, g_ref, gm_ref, dx_ref, vec_ref):
    gain = g_ref[...].astype(F32)
    vec_ref[...] = jnp.zeros_like(vec_ref)

    def step(i, _):
        rows = ds(i, TILE)
        normed, inv = norm(x_ref[rows, :].astype(F32))
        g = gh_ref[rows, :].astype(F32) + gho_ref[rows, :].astype(F32)
        dx_ref[rows, :] = gm_ref[rows, :] + norm_back(g, normed, inv, gain)
        vec_ref[0:1, :] += jnp.sum(g * normed, axis=0, keepdims=True)
        vec_ref[1:2, :] += jnp.sum(g, axis=0, keepdims=True)
        return 0

    lax.fori_loop(0, dx_ref.shape[0] // TILE, step, 0)


def body(
    layer_input, ln1_gain, ln1_bias, w_qkv, b_qkv, w_out, b_out, ln2_gain, ln2_bias,
    w_up, b_up, w_down, b_down, feature_signs, match_blocks, match_count, out_grad,
):
    rows, width = layer_input.shape
    half_width = width // 2
    half_heads = HEADS // 2
    hidden = w_up.shape[1]
    f = lax.axis_index("feat")
    tokens = 2 * rows
    assert lax.axis_size("feat") == 2 and match_blocks.shape[0] == 1 and tokens == SEQLEN

    def swap(a):
        return lax.ppermute(a, "feat", [(0, 1), (1, 0)])

    def row(a):
        return a.reshape(1, -1)

    x = jnp.concatenate([layer_input, swap(layer_input)], axis=0)
    og = jnp.concatenate([out_grad, swap(out_grad)], axis=0)
    signs = (2 * feature_signs - 1).astype(BF)
    own_signs = lax.dynamic_slice_in_dim(signs, f * half_heads, half_heads, 0)
    far_signs = swap(lax.dynamic_slice_in_dim(signs, (1 - f) * half_heads, half_heads, 0))
    signs = jnp.concatenate([own_signs, far_signs], axis=2)
    feats = signs.shape[2]
    pairs = signs.reshape(half_heads // 2, 2, HEAD_DIM, feats)
    table = jnp.concatenate(
        [
            jnp.pad(pairs[:, 0], ((0, 0), (0, HEAD_DIM), (0, 0))),
            jnp.pad(pairs[:, 1], ((0, 0), (HEAD_DIM, 0), (0, 0))),
        ],
        axis=2,
    )
    lists = lax.dynamic_slice_in_dim(match_blocks[0], f * half_heads, half_heads, 0)
    counts = lax.dynamic_slice_in_dim(match_count[0], f * half_heads, half_heads, 0)
    used = jnp.arange(lists.shape[2], dtype=jnp.int32) < counts[..., None]
    shift = f * (NB // 2)
    block = (jnp.arange(NB, dtype=jnp.int32) + shift) % NB
    matched = jnp.any(used[..., None] & (lists[..., None] == block), axis=2)
    matched = jnp.where(f == 0, matched, jnp.roll(matched, NB // 2, axis=1)).astype(F32)
    tiled = (half_heads, tokens // TILE, TILE // BLOCK, tokens)
    marks = jnp.repeat(matched, BLOCK, axis=2).reshape(tiled)
    marks_t = jnp.repeat(matched.transpose(0, 2, 1), BLOCK, axis=2).reshape(tiled)

    def own_cols(a):
        return jnp.concatenate(
            [lax.dynamic_slice_in_dim(a, i * width + f * half_width, half_width, 1) for i in range(3)], axis=1
        )

    w_own, b_own = own_cols(w_qkv), own_cols(row(b_qkv))
    h1, qkv = call(
        qkv_body, [((tokens, width), BF), ((tokens, 3 * half_width), BF)],
        [x, row(ln1_gain), row(ln1_bias), w_own, b_own], name="qkv",
    )
    phi = pltpu.VMEM((tokens, feats), BF)
    att, den = call(
        att_body, [((tokens, half_width), BF), ((tokens, half_width), F32)], [qkv, table, marks],
        scratch=[phi, phi], name="att",
    )
    far = swap(att)
    att_far = jnp.concatenate([far[rows:], far[:rows]], axis=0)
    mixed, h2 = call(
        mix_body, [((tokens, width), F32), ((tokens, width), BF)],
        [x, att, att_far, w_out, row(b_out), row(ln2_gain), row(ln2_bias)], name="mix",
    )
    act, gp, hid, gh2, d_bup = call(
        ff_body,
        [((tokens, hidden), BF), ((tokens, hidden), BF), ((tokens, width), BF), ((tokens, width), BF), ((1, hidden), F32)],
        [h2, og, w_up, w_down, row(b_up)], name="ff",
    )
    gh_far = swap(gh2)
    gh_far = jnp.concatenate([gh_far[rows:], gh_far[:rows]], axis=0)
    hid_far = swap(hid[rows:])
    d_up, d_down = call(
        ffw_body, [((width, hidden), BF), ((width, hidden), BF)], [h2, og, act, gp], name="ffw"
    )
    gm, gatt, d_out, y, vec2 = call(
        outb_body,
        [
            ((tokens, width), F32), ((tokens, half_width), F32), ((width, half_width), BF),
            ((rows, width), BF), ((8, width), F32),
        ],
        [gh2, gh_far, mixed, og, hid, hid_far, row(b_down), row(ln2_gain), w_out, att, att_far],
        scratch=[pltpu.VMEM((tokens, width), BF)], name="outb",
    )
    gqkv, = call(
        attb_body, [((tokens, 3 * half_width), BF)], [qkv, table, marks_t, att, den, gatt],
        scratch=[phi, phi, pltpu.VMEM((tokens, 128), BF), pltpu.VMEM((tokens, 128), F32), pltpu.VMEM((tokens, feats), F32)],
        name="attb",
    )
    gh1, d_qkv, d_bqkv = call(
        qkvb_body, [((tokens, width), BF), ((width, 3 * half_width), BF), ((1, 3 * half_width), F32)],
        [gqkv, h1, w_own], name="qkvb",
    )
    gh1_far = swap(gh1[rows:])
    dx, vec1 = call(
        ln1b_body, [((rows, width), F32), ((8, width), F32)],
        [gh1, gh1_far, layer_input, row(ln1_gain), gm], name="ln1b",
    )

    def over_seq(a):
        return lax.psum_scatter(a, "seq", scatter_dimension=0, tiled=True).astype(F32)

    up = over_seq(d_up)
    down = over_seq(d_down).T
    both = over_seq(jnp.concatenate([d_qkv, d_out], axis=1))
    keep = both.shape[0] // 2
    mine = lax.dynamic_slice_in_dim(both, f * keep, keep, 0)
    theirs = swap(lax.dynamic_slice_in_dim(both, (1 - f) * keep, keep, 0))
    low = jnp.where(f == 0, mine, theirs).reshape(keep, 4, 1, half_width)
    high = jnp.where(f == 0, theirs, mine).reshape(keep, 4, 1, half_width)
    full = jnp.concatenate([low, high], axis=2).reshape(keep, 4 * width)

    def scatter(v):
        return lax.psum_scatter(v.reshape(-1), ("seq", "feat"), scatter_dimension=0, tiled=True)

    d_b = jnp.zeros((1, 3 * width), F32)
    for i in range(3):
        d_b = lax.dynamic_update_slice(
            d_b, d_bqkv[:, i * half_width : (i + 1) * half_width], (0, i * width + f * half_width)
        )
    return (
        y, dx, scatter(vec1[0]), scatter(vec1[1]), full[:, : 3 * width], scatter(d_b), full[:, 3 * width :],
        scatter(vec2[2]), scatter(vec2[0]), scatter(vec2[1]), up, over_seq(d_bup.reshape(-1)), down, scatter(vec2[3]),
    )


def solution(mesh):
    both = ("seq", "feat")
    return jax.shard_map(
        body,
        mesh=mesh,
        in_specs=(
            P(both, None), P(), P(), P(), P(), P(), P(), P(), P(), P(None, "feat"), P("feat"), P("feat", None), P(),
            P(None, None, "feat"), P("seq", None, None, None), P("seq", None, None), P(both, None),
        ),
        out_specs=(
            P(both, None), P(both, None), P(both), P(both), P(both, None), P(both), P(both, None), P(both), P(both),
            P(both), P("seq", "feat"), P(("feat", "seq")), P("feat", "seq"), P(both),
        ),
        check_vma=False,
    )
```

time: 1020 us -> 583 us (0.57)
  matrix products: 214 us -> 0 us
  local copies, waits for them, and re-layouts: 223 us -> 28.8 us
  Pallas kernels: 0 us -> 152 us
  waiting for transfers between devices: 397 us -> 288 us
  other arithmetic: 76.6 us -> 14.7 us
    dot_general x36 -> x0, matrix products: 214 us -> none  [the longest x2 12.4 us: lift_back(): jnp.einsum('ghf,hdf->ghd', grad_lift.astype(jnp.bfloat16), sign_table, pr...]
    pallas_call x0 -> x9, Pallas kernels: none -> 152 us  [call(): pl.pallas_call(body, out_shape=[jax.ShapeDtypeStruct(s, d) for s, d in ou...]
    unnamed x16 -> x3, waiting for transfers between devices: 144 us -> 0.66 us
    reduce_scatter x10 -> x3, waiting for transfers between devices: 240 us -> 288 us  [over_seq(): lax.psum_scatter(a, 'seq', scatter_dimension=0, tiled=True).astype(F32)]
    reshape x12 -> x11, local copies, waits for them, and re-layouts: 51.9 us -> 4.45 us  [the longest x7 4.1 us: row(): return a.reshape(1, -1)]
    reduce_sum x13 -> x0, other arithmetic: 39.3 us -> none  [the longest x2 13.3 us: lift_back(): grad_square = -jnp.sum(grad_lift, axis=-1, keepdims=True)]
    another operation x7 -> x3, local copies, waits for them, and re-layouts: 39.1 us -> 2.23 us  [the longest x1 1.06 us: body(): jnp.repeat(matched.transpose(0, 2, 1), BLOCK, axis=2).reshape(tiled)]
    transpose x5 -> x1, local copies, waits for them, and re-layouts: 28.5 us -> 0.07 us  [body(): matched.transpose(0, 2, 1)]
  transfers between devices with their start and end apart: 15 -> 11, of which waited for: 4 -> 3; matrix products, arithmetic and copies ran while one was open for 35% -> 6% of each run, Pallas kernels for 0% -> 9%
where the time goes in v1:
time: 583 us
  waiting for transfers between devices  288 us (49%)
  Pallas kernels  152 us (26%)
  blocking collectives  81.9 us (14%)
  local copies, waits for them, and re-layouts  28.8 us (5%)
  other arithmetic  14.7 us (3%)
  between operations  14.7 us (3%)
    reduce_scatter x3, waiting for transfers between devices, over_seq(): lax.psum_scatter(a, 'seq', scatter_dimension=0, tiled=True).astype(F32)  288 us
    pallas_call x9, Pallas kernels, call(): pl.pallas_call(body, out_shape=[jax.ShapeDtypeStruct(s, d) for s, d in ou...  152 us
    unnamed x2, blocking collectives  81.9 us
  transfers between devices with their start and end apart: 11, of which 3 were waited for; matrix products, arithmetic and copies ran while one was open for 6% of the time, Pallas kernels for 9%

profile of v1, /device:TPU:0, one launch (start us, length us, event | category | flops | bytes accessed | tf_op | source)
XLA Modules:
  0.0 582.9 jit_solution(7112383256461173600)
XLA Ops:
  7.2 0.6 collective-permute-start
  7.8 1.1 add_convert_fusion
  8.9 0.7 constant_dynamic-slice_fusion.3
  9.5 0.5 collective-permute-start.3
  10.0 1.6 constant_dynamic-slice_fusion.6
  11.8 0.6 reshape.109.g_ref
  12.4 0.6 reshape.110.s_ref
  13.5 1.1 reshape_reshape.6.m_ref
  14.6 1.4 pad_maximum_fusion.1.w_ref
  16.0 0.6 pad_maximum_fusion.6.b_ref
  16.6 0.9 constant_dynamic-update-slice_fusion.1
  17.5 0.9 pad_maximum_fusion.5
  18.5 0.8 fusion.2.s_ref
  19.3 0.9 constant_dynamic-update-slice_fusion.x_ref
  20.2 7.0 %qkv.1 = (bf16[1024,768]{1,0:T(8,128)(2,1)}, bf16[1024,1152]{1,0:T(8,128)(2,1)}) custom-call(bf16[1024,768]{1,0:T(8,128)(2,1)} %constant_dynamic-update-slice_fusion.x_ref, bf16[1,768]{1,0:T(2,128)(2,1)} %reshape.109.g_ref, bf16[1,768]{1,0:T(2,128)(2,1)} %reshape.110.s_ref, bf16[768,1152]{1,0:T(8,128)(2,1)} %pad_maximum_fusion.1.w_ref, ...), custom_call_target="tpu_custom_call" | custom-call | tf_op jit(solution)/shard_map/qkv/pallas_call | solution.py:58
  27.2 26.8 %att.1 = (bf16[1024,384]{1,0:T(8,128)(2,1)}, f32[1024,384]{1,0:T(8,128)}) custom-call(bf16[1024,1152]{1,0:T(8,128)(2,1)} %get-tuple-element.37.qkv_ref, bf16[3,128,512]{2,1,0:T(8,128)(2,1)} %fusion.2.s_ref, f32[6,4,4,1024]{3,2,1,0:T(4,128)} %reshape_reshape.6.m_ref), custom_call_target="tpu_custom_call" | custom-call | tf_op jit(solution)/shard_map/att/pallas_call | solution.py:58
  54.1 0.6 reshape.113.g_ref
  54.7 0.6 reshape.112.b_ref
  55.2 0.6 reshape.114.s_ref
  55.8 0.6 reshape.115.b_ref
  56.4 0.9 constant_dynamic-update-slice_fusion.3
  57.4 2.1 constant_dynamic-update-slice_fusion.2.og_ref
  59.5 1.0 pad_maximum_fusion.3.other_ref
  60.5 7.4 %mix.1 = (f32[1024,768]{1,0:T(8,128)}, bf16[1024,768]{1,0:T(8,128)(2,1)}) custom-call(bf16[1024,768]{1,0:T(8,128)(2,1)} %constant_dynamic-update-slice_fusion.x_ref, bf16[1024,384]{1,0:T(8,128)(2,1)} %get-tuple-element.38.mine_ref.att_ref, bf16[1024,384]{1,0:T(8,128)(2,1)} %pad_maximum_fusion.3.other_ref, bf16[768,768]{1,0:T(8,128)(2,1)} %w_ref.3, ...), custom_call_target="tpu_custom_call" | custom-call | tf_op jit(solution)/shard_map/mix/pallas_call | solution.py:58
  67.9 17.8 %ff.1 = (bf16[1024,1536]{1,0:T(8,128)(2,1)}, bf16[1024,1536]{1,0:T(8,128)(2,1)}, bf16[1024,768]{1,0:T(8,128)(2,1)}, bf16[1024,768]{1,0:T(8,128)(2,1)}, f32[1,1536]{1,0:T(1,128)}) custom-call(bf16[1024,768]{1,0:T(8,128)(2,1)} %get-tuple-element.39.h_ref, bf16[1024,768]{1,0:T(8,128)(2,1)} %constant_dynamic-update-slice_fusion.2.og_ref, ...), custom_call_target="tpu_custom_call" | custom-call | tf_op jit(solution)/shard_map/ff/pallas_call | solution.py:58
  85.7 0.5 collective-permute-start.4
  86.2 2.1 slice.73
  88.3 0.6 reshape.116.bd_ref
  89.0 0.3 broadcast_in_dim.5
  89.3 1.1 reshape_reshape.7.m_ref
  90.4 1.3 pad_maximum_fusion.2.gho_ref
  91.8 0.9 copy-done.5
  92.7 11.8 %outb.1 = (f32[1024,768]{1,0:T(8,128)}, f32[1024,384]{1,0:T(8,128)}, bf16[768,384]{1,0:T(8,128)(2,1)}, bf16[512,768]{1,0:T(8,128)(2,1)}, f32[8,768]{1,0:T(8,128)}) custom-call(bf16[1024,768]{1,0:T(8,128)(2,1)} %get-tuple-element.40.gh_ref, bf16[1024,768]{1,0:T(8,128)(2,1)} %pad_maximum_fusion.2.gho_ref, f32[1024,768]{1,0:T(8,128)} %get-tuple-element.41.mixed_ref, ...), custom_call_target="tpu_custom_call" | custom-call | tf_op jit(solution)/shard_map/outb/pallas_call | solution.py:58
  104.5 55.6 %attb.1.gqkv_ref = bf16[1024,1152]{1,0:T(8,128)(2,1)} custom-call(bf16[1024,1152]{1,0:T(8,128)(2,1)} %get-tuple-element.37.qkv_ref, bf16[3,128,512]{2,1,0:T(8,128)(2,1)} %fusion.2.s_ref, f32[6,4,4,1024]{3,2,1,0:T(4,128)} %reshape_reshape.7.m_ref, bf16[1024,384]{1,0:T(8,128)(2,1)} %get-tuple-element.38.mine_ref.att_ref, ...), custom_call_target="tpu_custom_call" | custom-call | tf_op jit(solution)/shard_map/attb/pallas_call | solution.py:58
  160.1 9.6 %qkvb.1 = (bf16[1024,768]{1,0:T(8,128)(2,1)}, bf16[768,1152]{1,0:T(8,128)(2,1)}, f32[1,1152]{1,0:T(1,128)}) custom-call(bf16[1024,1152]{1,0:T(8,128)(2,1)} %attb.1.gqkv_ref, bf16[1024,768]{1,0:T(8,128)(2,1)} %get-tuple-element.46.h_ref, bf16[768,1152]{1,0:T(8,128)(2,1)} %pad_maximum_fusion.1.w_ref), custom_call_target="tpu_custom_call" | custom-call | tf_op jit(solution)/shard_map/qkvb/pallas_call | solution.py:58
  169.8 3.1 pad_maximum_fusion
  172.9 10.6 %ffw.1 = (bf16[768,1536]{1,0:T(8,128)(2,1)}, bf16[768,1536]{1,0:T(8,128)(2,1)}) custom-call(bf16[1024,768]{1,0:T(8,128)(2,1)} %get-tuple-element.39.h_ref, bf16[1024,768]{1,0:T(8,128)(2,1)} %constant_dynamic-update-slice_fusion.2.og_ref, bf16[1024,1536]{1,0:T(8,128)(2,1)} %get-tuple-element.55.act_ref, bf16[1024,1536]{1,0:T(8,128)(2,1)} %get-tuple-element.56.gp_ref), custom_call_target="tpu_custom_call" | custom-call | tf_op jit(solution)/shard_map/ffw/pallas_call | solution.py:58
  183.7 0.6 reduce-scatter.6.cloned.1.call-update
  184.3 0.7 copy-done.2
  185.0 0.9 slice.74
  185.9 0.5 collective-permute-start.6
  186.4 0.6 dynamic-slice.20
  187.6 44.0 %all-reduce.8 = f32[1536]{0:T(1024)S(1)} all-reduce(f32[1536]{0:T(1024)S(1)} %reduce.8), channel_id=10, replica_groups=mesh['seq'=16,'feat'=2] {'seq'}, use_global_device_ids=true, to_apply=%region_9.10.clone | all-reduce | flops 1536 | bytes 12288
  231.7 0.6 dynamic-slice.21
  232.3 0.3 dynamic_update_slice.12
  233.1 0.9 copy-done.4
  234.0 5.4 ln1b.1
  239.5 0.8 slice_reduce_fusion.4
  240.3 37.9 %all-reduce.10 = (f32[768]{0:T(1024)S(1)}, f32[768]{0:T(1024)S(1)}, f32[2304]{0:T(1024)S(1)}, f32[768]{0:T(1024)S(1)}, f32[768]{0:T(1024)S(1)}, /*index=5*/f32[768]{0:T(1024)S(1)}, f32[768]{0:T(1024)S(1)}) all-reduce(f32[768]{0:T(1024)S(1)} %get-tuple-element.65, ...), channel_id=2, replica_groups=mesh['seq'=16,'feat'=2] {'seq','feat'}, use_global_device_ids=true, to_apply=%region_1.2.clone | all-reduce | flops 6912 | bytes 55296
  278.2 0.6 dynamic-slice.14
  278.8 0.6 dynamic-slice.15
  279.3 0.6 dynamic-slice.17
  279.9 0.6 dynamic-slice.18
  280.5 0.6 dynamic-slice.19
  281.1 0.6 dynamic-slice.22
  281.7 0.6 dynamic-slice.16
  282.3 23.4 %reduce-scatter.4.cloned.1.call-done = bf16[48,1536]{1,0:T(8,128)(2,1)} async-done(((bf16[768,1536]{1,0:T(8,128)(2,1)}), bf16[48,1536]{1,0:T(8,128)(2,1)}) %reduce-scatter.4.cloned.1.call-update) | async-done | bytes 147472 | tf_op jit(solution)/shard_map/reduce_scatter | solution.py:462
  305.7 0.9 convert_element_type.19
  306.7 132.3 %reduce-scatter.8.cloned.1.call-done = bf16[48,1536]{1,0:T(8,128)(2,1)} async-done(((bf16[768,1536]{1,0:T(8,128)(2,1)}), bf16[48,1536]{1,0:T(8,128)(2,1)}) %reduce-scatter.8.cloned.1.call-update) | async-done | bytes 147472 | tf_op jit(solution)/shard_map/reduce_scatter | solution.py:462
  439.0 1.6 convert_bitcast_fusion
  440.7 132.0 %reduce-scatter.6.cloned.1.call-done = bf16[48,1536]{1,0:T(8,128)(2,1)} async-done(((bf16[768,1536]{1,0:T(8,128)(2,1)}), bf16[48,1536]{1,0:T(8,128)(2,1)}) %reduce-scatter.6.cloned.1.call-update) | async-done | bytes 147472 | tf_op jit(solution)/shard_map/reduce_scatter | solution.py:462
  572.6 1.6 convert_element_type.20
  575.0 0.7 slice.94
  575.7 0.6 slice.95
  (86 shorter events, 2.6 us)
Async XLA Ops:
  7.2 5.8 copy-start
  7.2 298.5 %reduce-scatter.4.cloned.1.call-start = ((), (), s32[]{:S(2)}) async-start(), calls=%async_computation.3 | async-start | bytes 2506752 | tf_op jit(solution)/shard_map/reduce_scatter | solution.py:462
  7.2 12.0 %collective-permute-start = (bf16[512,768]{1,0:T(8,128)(2,1)}, bf16[512,768]{1,0:T(8,128)(2,1)S(1)}, u32[]{:S(2)}, u32[]{:S(2)}) collective-permute-start(bf16[512,768]{1,0:T(8,128)(2,1)} %x_ref.1), channel_id=1, source_target_pairs={{0,1},{1,0},{2,3},{3,2},{4,5},{5,4},{6,7},{7,6},{8,9},{9,8},{10,11... | collective-permute-start | bytes 2359304 | tf_op jit(solution)/shard_map/ppermute | solution.py:374
  9.5 8.0 %collective-permute-start.1 = (bf16[6,64,128]{2,1,0:T(8,128)(2,1)}, bf16[6,64,128]{2,1,0:T(8,128)(2,1)}, u32[]{:S(2)}, u32[]{:S(2)}) collective-permute-start(bf16[6,64,128]{2,1,0:T(8,128)(2,1)} %get-tuple-element.88), channel_id=1, source_target_pairs={{0,1},{1,0},{2,3},{3,2},{4,5},{5,4},{6,7},{7,6},{8,9},{9,8},{10,11... | collective-permute-start | bytes 294920 | tf_op jit(solution)/shard_map/ppermute | solution.py:374
  9.5 47.8 %collective-permute-start.3 = (bf16[512,768]{1,0:T(8,128)(2,1)}, bf16[512,768]{1,0:T(8,128)(2,1)}, u32[]{:S(2)}, u32[]{:S(2)}) collective-permute-start(bf16[512,768]{1,0:T(8,128)(2,1)} %param.33), channel_id=1, source_target_pairs={{0,1},{1,0},{2,3},{3,2},{4,5},{5,4},{6,7},{7,6},{8,9},{9,8},{10,11... | collective-permute-start | bytes 2359304 | tf_op jit(solution)/shard_map/ppermute | solution.py:374
  10.0 1.7 copy-start.18
  10.0 1.8 copy-start.12
  10.0 2.4 copy-start.13
  10.0 3.0 copy-start.19
  14.6 2.0 copy-start.3
  27.2 26.9 %copy-start.14 = (bf16[768]{0:T(1024)(128)(2,1)S(1)}, bf16[768]{0:T(1024)(128)(2,1)}, u32[]{:S(2)}) copy-start(bf16[768]{0:T(1024)(128)(2,1)} %param.24) | copy-start | bytes 4612
  27.2 27.5 %copy-start.15 = (bf16[768]{0:T(1024)(128)(2,1)S(1)}, bf16[768]{0:T(1024)(128)(2,1)}, u32[]{:S(2)}) copy-start(bf16[768]{0:T(1024)(128)(2,1)} %param.23) | copy-start | bytes 4612
  27.2 28.1 %copy-start.16 = (bf16[768]{0:T(1024)(128)(2,1)S(1)}, bf16[768]{0:T(1024)(128)(2,1)}, u32[]{:S(2)}) copy-start(bf16[768]{0:T(1024)(128)(2,1)} %param.25) | copy-start | bytes 4612
  27.2 28.7 %copy-start.11 = (bf16[1536]{0:T(1024)(128)(2,1)S(1)}, bf16[1536]{0:T(1024)(128)(2,1)}, u32[]{:S(2)}) copy-start(bf16[1536]{0:T(1024)(128)(2,1)} %param.27) | copy-start | bytes 9220
  27.2 29.2 %copy-start.6 = (bf16[512,768]{1,0:T(8,128)(2,1)S(1)}, bf16[512,768]{1,0:T(8,128)(2,1)}, u32[]{:S(2)}) copy-start(bf16[512,768]{1,0:T(8,128)(2,1)} %param.33) | copy-start | bytes 2359300
  54.0 5.4 collective-permute-start.2
  67.9 20.4 %copy-start.17 = (bf16[768]{0:T(1024)(128)(2,1)S(1)}, bf16[768]{0:T(1024)(128)(2,1)}, u32[]{:S(2)}) copy-start(bf16[768]{0:T(1024)(128)(2,1)} %param.29) | copy-start | bytes 4612
  85.7 4.6 collective-permute-start.4
  88.3 3.5 collective-permute-start.5
  91.8 0.9 copy-start.5
  160.1 9.7 %copy-start.7 = (bf16[768,384]{1,0:T(8,128)(2,1)S(1)}, bf16[768,384]{1,0:T(8,128)(2,1)}, u32[]{:S(2)}) copy-start(bf16[768,384]{1,0:T(8,128)(2,1)} %get-tuple-element.52) | copy-start | bytes 1769476
  172.8 266.2 %reduce-scatter.8.cloned.1.call-start = ((), (), s32[]{:S(2)}) async-start(), calls=%async_computation.5 | async-start | bytes 2506752 | tf_op jit(solution)/shard_map/reduce_scatter | solution.py:462
  183.6 1.4 copy-start.2
  183.6 389.1 %reduce-scatter.6.cloned.1.call-start = ((), (), s32[]{:S(2)}) async-start(), calls=%async_computation.4 | async-start | bytes 2506752 | tf_op jit(solution)/shard_map/reduce_scatter | solution.py:462
  183.6 2.7 copy-start.20
  183.6 4.0 copy-start.9
  183.6 48.6 %copy-start.10 = (f32[1,1152]{1,0:T(1,128)S(1)}, f32[1,1152]{1,0:T(1,128)}, u32[]{:S(2)}) copy-start(f32[1,1152]{1,0:T(1,128)} %get-tuple-element.53) | copy-start | bytes 13828
  183.7 49.4 %copy-start.8 = (f32[8,768]{1,0:T(8,128)S(1)}, f32[8,768]{1,0:T(8,128)}, u32[]{:S(2)}) copy-start(f32[8,768]{1,0:T(8,128)} %get-tuple-element.54) | copy-start | bytes 73732
  185.9 47.2 %collective-permute-start.6 = (bf16[512,768]{1,0:T(8,128)(2,1)}, bf16[512,768]{1,0:T(8,128)(2,1)S(1)}, u32[]{:S(2)}, u32[]{:S(2)}) collective-permute-start(bf16[512,768]{1,0:T(8,128)(2,1)} %slice.74), channel_id=1, source_target_pairs={{0,1},{1,0},{2,3},{3,2},{4,5},{5,4},{6,7},{7,6},{8,9},{9,8},{10,11... | collective-permute-start | bytes 2359304 | tf_op jit(solution)/shard_map/ppermute | solution.py:374
  233.1 0.9 copy-start.4
  306.6 267.6 %collective-permute-start.7 = (f32[24,1536]{1,0:T(8,128)S(1)}, f32[24,1536]{1,0:T(8,128)S(1)}, u32[]{:S(2)}, u32[]{:S(2)}) collective-permute-start(f32[24,1536]{1,0:T(8,128)S(1)} %constant_dynamic-slice_fusion), channel_id=1, source_target_pairs={{0,1},{1,0},{2,3},{3,2},{4,5},{5,4},{6,7},{7,6},{8,9},{9,8},{10,11... | collective-permute-start | bytes 442376 | tf_op jit(solution)/shard_map/ppermute | solution.py:374
  572.6 3.7 copy-start.1
Sparse Core Ops, SparseCore 0:
  173.0 132.6 reduce-scatter.3
  310.6 128.3 reduce-scatter.7
  444.0 128.6 reduce-scatter.5

commit v2 on v1

--- a/solution.py
+++ b/solution.py
@@ -19,6 +19,7 @@
 TILE = 256
 GELU_A = math.sqrt(2.0 / math.pi)
 GELU_B = 0.044715
+MESH = pl.DeviceIdType.MESH
 VMEM = pl.BlockSpec(memory_space=pltpu.VMEM)
 ANY = pl.BlockSpec(memory_space=pl.ANY)
 
@@ -54,14 +55,243 @@
     )
 
 
-def call(body, outs, ins, specs=None, scratch=(), name=None):
+def split(n):
+    p = 1
+    while 2 * (2 * p) ** 3 <= n:
+        p *= 2
+    assert n % (p * p) == 0
+    return p, n // (p * p)
+
+
+class Net:
+    def __init__(self, n):
+        p, self.nz = split(n)
+        self.p = p
+        self.s, self.f = lax.axis_index("seq"), lax.axis_index("feat")
+        x, y = lax.rem(self.s, p), lax.rem(self.s // p, p)
+        f = self.f
+        self.sizes = (p, p, self.nz)
+        self.at = (x + f * (y - x), y + f * (x - y), self.s // (p * p))
+        self.strides = (1 + f * (p - 1), p + f * (1 - p), p * p)
+
+    def place(self, dest):
+        p = self.p
+        x, y, z = lax.rem(dest, p), lax.rem(dest // p, p), dest // (p * p)
+        f = self.f
+        return ((x + f * (y - x)) * p + y + f * (x - y)) * self.nz + z
+
+    def peer(self, phase, d):
+        j = lax.rem(self.at[phase] + d, self.sizes[phase])
+        return j, self.s + (j - self.at[phase]) * self.strides[phase]
+
+    def barrier(self):
+        sem = pltpu.get_barrier_semaphore()
+        count = 1
+        for phase in range(3):
+            for d in range(1, self.sizes[phase]):
+                pl.semaphore_signal(sem, inc=1, device_id={"seq": self.peer(phase, d)[1]}, device_id_type=MESH)
+                count += 1
+        pl.semaphore_signal(sem, inc=1, device_id={"feat": 1 - self.f}, device_id_type=MESH)
+        pl.semaphore_wait(sem, count)
+
+    def slot(self, phase, d):
+        return sum(size - 1 for size in self.sizes[:phase]) + d - 1
+
+    def slots(self):
+        return self.slot(3, 1) + 1
+
+
+def scatter_bufs(n, rows, cols):
+    p, nz = split(n)
+    return [
+        pltpu.VMEM((p - 1, p * nz, rows, cols), BF),
+        pltpu.VMEM((p * nz, rows, cols), BF),
+        pltpu.VMEM((p - 1, nz, rows, cols), BF),
+        pltpu.VMEM((nz, rows, cols), BF),
+        pltpu.VMEM((nz - 1, 1, rows, cols), BF),
+    ]
+
+
+class Scatter:
+    def __init__(self, net, src, bufs, send, recv):
+        self.net, self.send, self.recv = net, send, recv
+        self.hold = (src, bufs[1], bufs[3])
+        self.got = (bufs[0], bufs[2], bufs[4])
+
+    def block(self, phase, j):
+        size = self.got[phase].shape[1]
+        return pl.ds(j * size, size)
+
+    def copies(self, phase):
+        net, out = self.net, []
+        for d in range(1, net.sizes[phase]):
+            j, device = net.peer(phase, d)
+            k = net.slot(phase, d)
+            out.append(
+                pltpu.make_async_remote_copy(
+                    src_ref=self.hold[phase].at[self.block(phase, j)],
+                    dst_ref=self.got[phase].at[d - 1],
+                    send_sem=self.send.at[k],
+                    recv_sem=self.recv.at[k],
+                    device_id={"seq": device},
+                    device_id_type=MESH,
+                )
+            )
+        return out
+
+    def start(self, phase):
+        for copy in self.copies(phase):
+            copy.start()
+
+    def finish(self, phase, put=None):
+        for copy in self.copies(phase):
+            copy.wait()
+        got, own = self.got[phase], self.hold[phase]
+        size = got.shape[1]
+        base = self.net.at[phase] * size
+
+        def add(i, _):
+            total = own[base + i].astype(F32)
+            for d in range(got.shape[0]):
+                total = total + got[d, i].astype(F32)
+            if put is None:
+                self.hold[phase + 1][i] = total.astype(BF)
+            else:
+                put(total)
+            return 0
+
+        lax.fori_loop(0, size, add, 0)
+
+
+class Vector:
+    def __init__(self, net, bufs, send, recv, both):
+        self.net, self.bufs, self.send, self.recv, self.both = net, bufs, send, recv, both
+
+    def copies(self, phase):
+        net, out = self.net, []
+        peers = [({"feat": 1 - net.f}, net.slots() - 1)]
+        if phase < 3:
+            peers = [({"seq": net.peer(phase, d)[1]}, net.slot(phase, d)) for d in range(1, net.sizes[phase])]
+        for device, k in peers:
+            out.append(
+                pltpu.make_async_remote_copy(
+                    src_ref=self.bufs.at[phase],
+                    dst_ref=self.bufs.at[4 + k],
+                    send_sem=self.send.at[k],
+                    recv_sem=self.recv.at[k],
+                    device_id=device,
+                    device_id_type=MESH,
+                )
+            )
+        return out
+
+    def start(self, phase):
+        for copy in self.copies(phase):
+            copy.start()
+
+    def finish(self, phase):
+        for copy in self.copies(phase):
+            copy.wait()
+        first, count = (self.net.slots() - 1, 1) if phase == 3 else (self.net.slot(phase, 1), self.net.sizes[phase] - 1)
+        total = self.bufs[phase]
+        for k in range(count):
+            total = total + self.bufs[4 + first + k]
+        if phase < 3:
+            self.bufs[phase + 1] = total
+        return total
+
+
+def grads_body(
+    n, up_ref, down_ref, out_ref, qkv_ref, rows_ref, bqkv_ref, bup_ref,
+    oup_ref, odown_ref, oout_ref, oqkv_ref, orows_ref, obqkv_ref, obup_ref, *scratch,
+):
+    net = Net(n)
+    bufs, tail = scratch[:20], scratch[20:]
+    sout, sqkv, gout, gqkv, vrows, vbqkv, vbup, send, recv = tail
+    parts = []
+    for i, src in enumerate((down_ref, up_ref, out_ref, qkv_ref)):
+        parts.append(Scatter(net, src, bufs[5 * i : 5 * i + 5], send.at[i], recv.at[i]))
+    vectors = [Vector(net, ref, send.at[4 + i], recv.at[4 + i], i < 2) for i, ref in enumerate((vrows, vbqkv, vbup))]
+    vrows[0], vbqkv[0], vbup[0] = rows_ref[...], bqkv_ref[...], bup_ref[...]
+    half = sout.shape[1]
+
+    def whole(ref):
+        def put(total):
+            ref[...] = total
+
+        return put
+
+    def halves(ref):
+        def put(total):
+            ref[0], ref[1] = total[:half], total[half:]
+
+        return put
+
+    net.barrier()
+    for part in parts:
+        part.start(0)
+    for v in vectors:
+        v.start(0)
+    for phase in (0, 1):
+        for part in parts:
+            part.finish(phase)
+            part.start(phase + 1)
+        for v in vectors:
+            v.finish(phase)
+            v.start(phase + 1)
+    for part, put in zip(parts, (whole(odown_ref), whole(oup_ref), halves(sout), halves(sqkv))):
+        part.finish(2, put)
+    last = net.slots() - 1
+    swaps = []
+    for i, (src, dst) in enumerate(((sout, gout), (sqkv, gqkv))):
+        swaps.append(
+            pltpu.make_async_remote_copy(
+                src_ref=src.at[1 - net.f], dst_ref=dst, send_sem=send.at[2 + i, last], recv_sem=recv.at[2 + i, last],
+                device_id={"feat": 1 - net.f}, device_id_type=MESH,
+            )
+        )
+    for swap in swaps:
+        swap.start()
+    rows = vectors[0].finish(2)
+    bqkv = vectors[1].finish(2)
+    bup = vectors[2].finish(2)
+    vectors[0].start(3)
+    vectors[1].start(3)
+    width = rows.shape[1]
+    lanes = orows_ref.shape[1]
+    where = 2 * net.s + net.f
+
+    def cut(value, per, index, size):
+        shift = lax.rem(size - index * per, size)
+        return pltpu.roll(value, shift, 1)[:, :lanes]
+
+    obup_ref[...] = cut(bup, bup.shape[1] // n, net.s, bup.shape[1])
+    rows = vectors[0].finish(3)
+    bqkv = vectors[1].finish(3)
+    orows_ref[...] = cut(rows, width // (2 * n), where, width)
+    obqkv_ref[...] = cut(bqkv, bqkv.shape[1] // (2 * n), where, bqkv.shape[1])
+    for swap in swaps:
+        swap.wait()
+    own = sout.shape[2]
+    f = net.f
+    oout_ref[:, ds(f, own)] = sout[f]
+    oout_ref[:, ds(1 - f, own)] = gout[...]
+    for i in range(3):
+        part = slice(i * own, (i + 1) * own)
+        oqkv_ref[:, ds(2 * i + f, own)] = sqkv[f, :, part]
+        oqkv_ref[:, ds(2 * i + 1 - f, own)] = gqkv[:, part]
+
+
+def call(body, outs, ins, specs=None, scratch=(), name=None, net=None):
     return pl.pallas_call(
         body,
         out_shape=[jax.ShapeDtypeStruct(s, d) for s, d in outs],
         in_specs=specs or [VMEM] * len(ins),
         out_specs=[VMEM] * len(outs),
         scratch_shapes=list(scratch),
-        compiler_params=pltpu.CompilerParams(vmem_limit_bytes=64000 * 1024),
+        compiler_params=pltpu.CompilerParams(
+            vmem_limit_bytes=64000 * 1024, collective_id=net, has_side_effects=net is not None
+        ),
         name=name,
     )(*ins)
 
@@ -194,18 +424,28 @@
     lax.fori_loop(0, h_ref.shape[0] // TILE, step, 0)
 
 
-def ffw_body(h_ref, og_ref, act_ref, gp_ref, up_ref, down_ref):
+def put_chunks(out_ref, first, value, net):
+    rows = out_ref.shape[1]
+    for i in range(value.shape[0] // rows):
+        out_ref[net.place(first + i)] = value[i * rows : (i + 1) * rows].astype(BF)
+
+
+def ffw_body(n, h_ref, og_ref, act_ref, gp_ref, up_ref, down_ref):
+    net = Net(n)
+    wide = h_ref.shape[1] // 2
+    per = wide // up_ref.shape[1]
+
     def step(i, _):
-        rows = ds(i, TILE)
-        up_ref[rows, :] = tn(h_ref[:, rows], gp_ref[...]).astype(BF)
-        down_ref[rows, :] = tn(og_ref[:, rows], act_ref[...]).astype(BF)
-        return 0
-
-    lax.fori_loop(0, h_ref.shape[1] // TILE, step, 0)
+        rows = ds(i, wide)
+        put_chunks(up_ref, i * per, tn(h_ref[:, rows], gp_ref[...]), net)
+        put_chunks(down_ref, i * per, tn(og_ref[:, rows], act_ref[...]), net)
+        return 0
+
+    lax.fori_loop(0, 2, step, 0)
 
 
 def outb_body(
-    gh_ref, gho_ref, mixed_ref, og_ref, hid_ref, hido_ref, bd_ref, g_ref, w_ref, mine_ref, other_ref,
+    n, gh_ref, gho_ref, mixed_ref, og_ref, hid_ref, hido_ref, bd_ref, g_ref, w_ref, mine_ref, other_ref,
     gm_ref, gatt_ref, dw_ref, y_ref, vec_ref, gb_ref,
 ):
     f = lax.axis_index("feat")
@@ -239,8 +479,10 @@
 
     lax.fori_loop(0, tiles, step, 0)
     gb_own = gb_ref[:, ds(f, half)]
-    dw_ref[ds(f, half), :] = tn(mine_ref[...], gb_own).astype(BF)
-    dw_ref[ds(1 - f, half), :] = tn(other_ref[...], gb_own).astype(BF)
+    net = Net(n)
+    per = half // dw_ref.shape[1]
+    put_chunks(dw_ref, f * per, tn(mine_ref[...], gb_own), net)
+    put_chunks(dw_ref, (1 - f) * per, tn(other_ref[...], gb_own), net)
 
 
 def attb_body(
@@ -322,7 +564,7 @@
     lax.fori_loop(0, qkv_ref.shape[1] // (3 * HEAD_DIM), head, 0)
 
 
-def qkvb_body(gqkv_ref, h_ref, w_ref, gh_ref, dw_ref, db_ref):
+def qkvb_body(n, gqkv_ref, h_ref, w_ref, gh_ref, dw_ref, db_ref):
     db_ref[...] = jnp.zeros_like(db_ref)
 
     def step(i, _):
@@ -334,12 +576,16 @@
 
     lax.fori_loop(0, gqkv_ref.shape[0] // TILE, step, 0)
 
+    net = Net(n)
+    wide = h_ref.shape[1] // 2
+    per = wide // dw_ref.shape[1]
+
     def weight(i, _):
-        rows = ds(i, TILE)
-        dw_ref[rows, :] = tn(h_ref[:, rows], gqkv_ref[...]).astype(BF)
-        return 0
-
-    lax.fori_loop(0, h_ref.shape[1] // TILE, weight, 0)
+        rows = ds(i, wide)
+        put_chunks(dw_ref, i * per, tn(h_ref[:, rows], gqkv_ref[...]), net)
+        return 0
+
+    lax.fori_loop(0, 2, weight, 0)
 
 
 def ln1b_body(gh_ref, gho_ref, x_ref, g_ref, gm_ref, dx_ref, vec_ref):
@@ -368,6 +614,8 @@
     hidden = w_up.shape[1]
     f = lax.axis_index("feat")
     tokens = 2 * rows
+    n = lax.axis_size("seq")
+    chunk = width // n
     assert lax.axis_size("feat") == 2 and match_blocks.shape[0] == 1 and tokens == SEQLEN
 
     def swap(a):
@@ -432,12 +680,13 @@
     gh_far = jnp.concatenate([gh_far[rows:], gh_far[:rows]], axis=0)
     hid_far = swap(hid[rows:])
     d_up, d_down = call(
-        ffw_body, [((width, hidden), BF), ((width, hidden), BF)], [h2, og, act, gp], name="ffw"
+        functools.partial(ffw_body, n), [((n, chunk, hidden), BF), ((n, chunk, hidden), BF)], [h2, og, act, gp],
+        name="ffw",
     )
     gm, gatt, d_out, y, vec2 = call(
-        outb_body,
+        functools.partial(outb_body, n),
         [
-            ((tokens, width), F32), ((tokens, half_width), F32), ((width, half_width), BF),
+            ((tokens, width), F32), ((tokens, half_width), F32), ((n, chunk, half_width), BF),
             ((rows, width), BF), ((8, width), F32),
         ],
         [gh2, gh_far, mixed, og, hid, hid_far, row(b_down), row(ln2_gain), w_out, att, att_far],
@@ -449,7 +698,8 @@
         name="attb",
     )
     gh1, d_qkv, d_bqkv = call(
-        qkvb_body, [((tokens, width), BF), ((width, 3 * half_width), BF), ((1, 3 * half_width), F32)],
+        functools.partial(qkvb_body, n),
+        [((tokens, width), BF), ((n, chunk, 3 * half_width), BF), ((1, 3 * half_width), F32)],
         [gqkv, h1, w_own], name="qkvb",
     )
     gh1_far = swap(gh1[rows:])
@@ -457,31 +707,42 @@
         ln1b_body, [((rows, width), F32), ((8, width), F32)],
         [gh1, gh1_far, layer_input, row(ln1_gain), gm], name="ln1b",
     )
-
-    def over_seq(a):
-        return lax.psum_scatter(a, "seq", scatter_dimension=0, tiled=True).astype(F32)
-
-    up = over_seq(d_up)
-    down = over_seq(d_down).T
-    both = over_seq(jnp.concatenate([d_qkv, d_out], axis=1))
-    keep = both.shape[0] // 2
-    mine = lax.dynamic_slice_in_dim(both, f * keep, keep, 0)
-    theirs = swap(lax.dynamic_slice_in_dim(both, (1 - f) * keep, keep, 0))
-    low = jnp.where(f == 0, mine, theirs).reshape(keep, 4, 1, half_width)
-    high = jnp.where(f == 0, theirs, mine).reshape(keep, 4, 1, half_width)
-    full = jnp.concatenate([low, high], axis=2).reshape(keep, 4 * width)
-
-    def scatter(v):
-        return lax.psum_scatter(v.reshape(-1), ("seq", "feat"), scatter_dimension=0, tiled=True)
 
     d_b = jnp.zeros((1, 3 * width), F32)
     for i in range(3):
         d_b = lax.dynamic_update_slice(
             d_b, d_bqkv[:, i * half_width : (i + 1) * half_width], (0, i * width + f * half_width)
         )
+    vecs = jnp.concatenate([vec1[:2], vec2[:4], jnp.zeros((2, width), F32)], axis=0)
+    slots = sum(split(n)) + split(n)[0] - 3 + 1
+    bufs = []
+    for cols in (hidden, hidden, half_width, 3 * half_width):
+        bufs += scatter_bufs(n, chunk, cols)
+    half_chunk = chunk // 2
+    sems = pltpu.SemaphoreType.DMA((7, slots))
+    up, down, out, full, vecs, d_b, d_bup = call(
+        functools.partial(grads_body, n),
+        [
+            ((chunk, hidden), F32), ((chunk, hidden), F32), ((half_chunk, width), F32), ((half_chunk, 3 * width), F32),
+            ((8, 128), F32), ((1, 128), F32), ((1, 128), F32),
+        ],
+        [d_up, d_down, d_out, d_qkv, vecs, d_b, d_bup],
+        scratch=bufs + [
+            pltpu.VMEM((2, half_chunk, half_width), F32), pltpu.VMEM((2, half_chunk, 3 * half_width), F32),
+            pltpu.VMEM((half_chunk, half_width), F32), pltpu.VMEM((half_chunk, 3 * half_width), F32),
+            pltpu.VMEM((4 + slots, 8, width), F32), pltpu.VMEM((4 + slots, 1, 3 * width), F32),
+            pltpu.VMEM((4 + slots, 1, hidden), F32), sems, sems,
+        ],
+        name="grads", net=1,
+    )
+    own = width // (2 * n)
+
+    def vec(i):
+        return vecs[i, :own]
+
     return (
-        y, dx, scatter(vec1[0]), scatter(vec1[1]), full[:, : 3 * width], scatter(d_b), full[:, 3 * width :],
-        scatter(vec2[2]), scatter(vec2[0]), scatter(vec2[1]), up, over_seq(d_bup.reshape(-1)), down, scatter(vec2[3]),
+        y, dx, vec(0), vec(1), full, d_b[0, : 3 * own], out, vec(4), vec(2), vec(3), up, d_bup[0, : hidden // n],
+        down.T, vec(5),
     )
 
 

time: 583 us -> 306 us (0.52)
  waiting for transfers between devices: 288 us -> 0.02 us
  Pallas kernels: 152 us -> 261 us
  blocking collectives: 81.9 us -> 0 us
  between operations: 14.7 us -> 0.87 us
  other arithmetic: 14.7 us -> 6.98 us
    reduce_scatter x3 -> x0, waiting for transfers between devices: 288 us -> none  [over_seq(): lax.psum_scatter(a, 'seq', scatter_dimension=0, tiled=True).astype(F32)]
    pallas_call x9 -> x10, Pallas kernels: 152 us -> 261 us  [call(): pl.pallas_call(body, out_shape=[jax.ShapeDtypeStruct(s, d) for s, d in ou...]
    unnamed x2 -> x0, blocking collectives: 81.9 us -> none
  transfers between devices with their start and end apart: 11 -> 7, of which waited for: 3 -> 0; matrix products, arithmetic and copies ran while one was open for 6% -> 8% of each run, Pallas kernels for 9% -> 15%
where the time goes in v2:
time: 306 us; the launch traced here: 305 us
  Pallas kernels  261 us (85%)
  local copies, waits for them, and re-layouts  33.7 us (11%)
  other arithmetic  6.98 us (2%)
    pallas_call x10, Pallas kernels, call(): pl.pallas_call(body, out_shape=[jax.ShapeDtypeStruct(s, d) for s, d in ou...  261 us
    unnamed x35, local copies, waits for them, and re-layouts  10.3 us
  transfers between devices with their start and end apart: 7, of which 0 were waited for; matrix products, arithmetic and copies ran while one was open for 8% of the time, Pallas kernels for 15%

profile of v2, /device:TPU:0, one launch (start us, length us, event | category | flops | bytes accessed | tf_op | source)
XLA Modules:
  0.0 305.1 jit_solution(2317840493121857117)
XLA Ops:
  0.6 0.0 copy-start
  0.7 1.1 add_convert_fusion
  1.8 0.6 collective-permute-start.1
  2.3 0.1 collective-permute-start.3
  2.4 0.4 collective-permute-start
  2.8 1.3 reshape.82.g_ref
  4.1 1.3 reshape.83.s_ref
  5.4 0.7 constant_dynamic-slice_fusion
  6.1 0.9 fusion.9
  7.0 0.2 and_reduce_fusion
  7.2 0.3 broadcast_in_dim.8
  7.5 1.1 reshape_reshape.6.m_ref
  8.5 1.6 constant_dynamic-slice_fusion.5
  10.2 0.0 copy-start.2
  10.2 1.4 pad_maximum_fusion.w_ref
  11.6 0.6 pad_maximum_fusion.4.b_ref
  12.2 0.9 constant_dynamic-update-slice_fusion.1
  13.1 0.8 fusion.2.s_ref
  13.9 0.9 constant_dynamic-update-slice_fusion.x_ref
  14.9 7.0 %qkv.1 = (bf16[1024,768]{1,0:T(8,128)(2,1)}, bf16[1024,1152]{1,0:T(8,128)(2,1)}) custom-call(bf16[1024,768]{1,0:T(8,128)(2,1)} %constant_dynamic-update-slice_fusion.x_ref, bf16[1,768]{1,0:T(2,128)(2,1)} %reshape.82.g_ref, bf16[1,768]{1,0:T(2,128)(2,1)} %reshape.83.s_ref, bf16[768,1152]{1,0:T(8,128)(2,1)} %pad_maximum_fusion.w_ref, ...), custom_call_target="tpu_custom_call" | custom-call | tf_op jit(solution)/shard_map/qkv/pallas_call | solution.py:286
  21.8 0.0 copy-start.9
  21.9 0.0 copy-start.5
  21.9 26.9 %att.1 = (bf16[1024,384]{1,0:T(8,128)(2,1)}, f32[1024,384]{1,0:T(8,128)}) custom-call(bf16[1024,1152]{1,0:T(8,128)(2,1)} %get-tuple-element.44.qkv_ref, bf16[3,128,512]{2,1,0:T(8,128)(2,1)} %fusion.2.s_ref, f32[6,4,4,1024]{3,2,1,0:T(4,128)} %reshape_reshape.6.m_ref), custom_call_target="tpu_custom_call" | custom-call | tf_op jit(solution)/shard_map/att/pallas_call | solution.py:286
  48.7 0.1 collective-permute-start.2
  48.8 0.6 reshape.86.g_ref
  49.4 0.6 reshape.85.b_ref
  50.0 0.6 reshape.87.s_ref
  50.6 0.6 reshape.88.b_ref
  51.2 0.9 constant_dynamic-update-slice_fusion.3
  52.1 2.1 constant_dynamic-update-slice_fusion.2.og_ref
  54.2 0.1 fusion.7
  54.3 1.0 pad_maximum_fusion.2.other_ref
  55.3 7.3 %mix.1 = (f32[1024,768]{1,0:T(8,128)}, bf16[1024,768]{1,0:T(8,128)(2,1)}) custom-call(bf16[1024,768]{1,0:T(8,128)(2,1)} %constant_dynamic-update-slice_fusion.x_ref, bf16[1024,384]{1,0:T(8,128)(2,1)} %get-tuple-element.45.mine_ref.att_ref, bf16[1024,384]{1,0:T(8,128)(2,1)} %pad_maximum_fusion.2.other_ref, bf16[768,768]{1,0:T(8,128)(2,1)} %w_ref.3, ...), custom_call_target="tpu_custom_call" | custom-call | tf_op jit(solution)/shard_map/mix/pallas_call | solution.py:286
  62.6 17.8 %ff.1 = (bf16[1024,1536]{1,0:T(8,128)(2,1)}, bf16[1024,1536]{1,0:T(8,128)(2,1)}, bf16[1024,768]{1,0:T(8,128)(2,1)}, bf16[1024,768]{1,0:T(8,128)(2,1)}, f32[1,1536]{1,0:T(1,128)}) custom-call(bf16[1024,768]{1,0:T(8,128)(2,1)} %get-tuple-element.46.h_ref, bf16[1024,768]{1,0:T(8,128)(2,1)} %constant_dynamic-update-slice_fusion.2.og_ref, ...), custom_call_target="tpu_custom_call" | custom-call | tf_op jit(solution)/shard_map/ff/pallas_call | solution.py:286
  80.4 0.4 collective-permute-start.4
  80.9 2.1 slice.79
  82.9 0.1 collective-permute-start.5
  83.0 0.6 reshape.89.bd_ref
  83.6 0.1 copy.41
  83.7 0.3 broadcast_in_dim.18
  83.9 1.1 reshape_reshape.7.m_ref
  85.0 0.1 fusion.6
  85.1 1.3 pad_maximum_fusion.1.gho_ref
  86.4 0.9 copy-done.3
  87.3 12.7 %outb.1 = (f32[1024,768]{1,0:T(8,128)}, f32[1024,384]{1,0:T(8,128)}, bf16[16,48,384]{2,1,0:T(8,128)(2,1)}, bf16[512,768]{1,0:T(8,128)(2,1)}, f32[8,768]{1,0:T(8,128)}) custom-call(bf16[1024,768]{1,0:T(8,128)(2,1)} %get-tuple-element.47.gh_ref, bf16[1024,768]{1,0:T(8,128)(2,1)} %pad_maximum_fusion.1.gho_ref, f32[1024,768]{1,0:T(8,128)} %get-tuple-element.48.mixed_ref, ...), custom_call_target="tpu_custom_call" | custom-call | tf_op jit(solution)/shard_map/outb/pallas_call | solution.py:286
  100.0 55.7 %attb.1.gqkv_ref = bf16[1024,1152]{1,0:T(8,128)(2,1)} custom-call(bf16[1024,1152]{1,0:T(8,128)(2,1)} %get-tuple-element.44.qkv_ref, bf16[3,128,512]{2,1,0:T(8,128)(2,1)} %fusion.2.s_ref, f32[6,4,4,1024]{3,2,1,0:T(4,128)} %reshape_reshape.7.m_ref, bf16[1024,384]{1,0:T(8,128)(2,1)} %get-tuple-element.45.mine_ref.att_ref, ...), custom_call_target="tpu_custom_call" | custom-call | tf_op jit(solution)/shard_map/attb/pallas_call | solution.py:286
  155.7 9.7 %qkvb.1 = (bf16[1024,768]{1,0:T(8,128)(2,1)}, bf16[16,48,1152]{2,1,0:T(8,128)(2,1)}, f32[1,1152]{1,0:T(1,128)}) custom-call(bf16[1024,1152]{1,0:T(8,128)(2,1)} %attb.1.gqkv_ref, bf16[1024,768]{1,0:T(8,128)(2,1)} %get-tuple-element.53.h_ref, bf16[768,1152]{1,0:T(8,128)(2,1)} %pad_maximum_fusion.w_ref), custom_call_target="tpu_custom_call" | custom-call | tf_op jit(solution)/shard_map/qkvb/pallas_call | solution.py:286
  165.5 2.1 slice.80
  167.5 0.4 collective-permute-start.6
  168.0 0.1 pad.12.clone
  168.0 10.5 %ffw.1 = (bf16[16,48,1536]{2,1,0:T(8,128)(2,1)}, bf16[16,48,1536]{2,1,0:T(8,128)(2,1)}) custom-call(bf16[1024,768]{1,0:T(8,128)(2,1)} %get-tuple-element.46.h_ref, bf16[1024,768]{1,0:T(8,128)(2,1)} %constant_dynamic-update-slice_fusion.2.og_ref, bf16[1024,1536]{1,0:T(8,128)(2,1)} %get-tuple-element.57.act_ref, bf16[1024,1536]{1,0:T(8,128)(2,1)} %get-tuple-element.58.gp_ref), custom_call_target="tpu_custom_call" | custom-call | tf_op jit(solution)/shard_map/ffw/pallas_call | solution.py:286
  178.6 0.0 copy-start.6
  178.6 0.9 copy-done.4
  179.6 5.4 %ln1b.1 = (f32[512,768]{1,0:T(8,128)}, f32[8,768]{1,0:T(8,128)}) custom-call(bf16[1024,768]{1,0:T(8,128)(2,1)} %get-tuple-element.54.gh_ref, bf16[512,768]{1,0:T(8,128)(2,1)} %copy-done.4, bf16[512,768]{1,0:T(8,128)(2,1)} %x_ref.1, bf16[1,768]{1,0:T(2,128)(2,1)} %reshape.82.g_ref, f32[1024,768]{1,0:T(8,128)} %get-tuple-element.55.gm_ref), custom_call_target="tpu_custom_call" | custom-call | tf_op jit(solution)/shard_map/ln1b/pallas_call | solution.py:286
  185.0 0.7 slice.81
  185.7 0.7 maximum_maximum_fusion.rows_ref
  186.4 108.5 %grads.1 = (f32[48,1536]{1,0:T(8,128)}, f32[48,1536]{1,0:T(8,128)}, f32[24,768]{1,0:T(8,128)}, f32[24,2304]{1,0:T(8,128)}, f32[8,128]{1,0:T(8,128)}, /*index=5*/f32[1,128]{1,0:T(1,128)}, f32[1,128]{1,0:T(1,128)}) custom-call(bf16[16,48,1536]{2,1,0:T(8,128)(2,1)} %get-tuple-element.59.up_ref, bf16[16,48,1536]{2,1,0:T(8,128)(2,1)} %get-tuple-element.60.down_ref, ...), custom_call_target="tpu_custom_call" | custom-call | tf_op jit(solution)/shard_map/grads/pallas_call | solution.py:286
  294.9 1.4 slice_bitcast_fusion.2
  296.3 1.1 slice_bitcast_fusion.7
  297.4 1.2 slice_bitcast_fusion.3
  298.6 1.6 copy.56
  300.2 1.5 copy.57
  301.7 1.7 copy.58
  303.4 1.7 copy.59
  (46 shorter events, 0.2 us)
Async XLA Ops:
  0.6 6.3 %copy-start = (s32[1,12,16,4]{2,3,1,0:T(4,128)S(1)}, s32[1,12,16,4]{2,3,1,0:T(4,128)}, u32[]{:S(2)}) copy-start(s32[1,12,16,4]{2,3,1,0:T(4,128)} %param.31) | copy-start | bytes 9220
  1.8 11.3 %collective-permute-start.1 = (bf16[6,64,128]{2,1,0:T(8,128)(2,1)S(1)}, bf16[6,64,128]{2,1,0:T(8,128)(2,1)S(1)}, u32[]{:S(2)}, u32[]{:S(2)}) collective-permute-start(bf16[6,64,128]{2,1,0:T(8,128)(2,1)S(1)} %get-tuple-element.84), channel_id=1, source_target_pairs={{0,1},{1,0},{2,3},{3,2},{4,5},{5,4},{6,7},{7,6},{8,9},{9,8},{10,11... | collective-permute-start | bytes 294920 | tf_op jit(solution)/shard_map/ppermute | solution.py:622
  2.3 49.8 %collective-permute-start.3 = (bf16[512,768]{1,0:T(8,128)(2,1)}, bf16[512,768]{1,0:T(8,128)(2,1)}, u32[]{:S(2)}, u32[]{:S(2)}) collective-permute-start(bf16[512,768]{1,0:T(8,128)(2,1)} %param.33), channel_id=1, source_target_pairs={{0,1},{1,0},{2,3},{3,2},{4,5},{5,4},{6,7},{7,6},{8,9},{9,8},{10,11... | collective-permute-start | bytes 2359304 | tf_op jit(solution)/shard_map/ppermute | solution.py:622
  2.4 11.5 %collective-permute-start = (bf16[512,768]{1,0:T(8,128)(2,1)}, bf16[512,768]{1,0:T(8,128)(2,1)S(1)}, u32[]{:S(2)}, u32[]{:S(2)}) collective-permute-start(bf16[512,768]{1,0:T(8,128)(2,1)} %x_ref.1), channel_id=1, source_target_pairs={{0,1},{1,0},{2,3},{3,2},{4,5},{5,4},{6,7},{7,6},{8,9},{9,8},{10,11... | collective-permute-start | bytes 2359304 | tf_op jit(solution)/shard_map/ppermute | solution.py:622
  10.2 2.0 copy-start.2
  21.8 27.0 %copy-start.10 = (bf16[768]{0:T(1024)(128)(2,1)S(1)}, bf16[768]{0:T(1024)(128)(2,1)}, u32[]{:S(2)}) copy-start(bf16[768]{0:T(1024)(128)(2,1)} %param.24) | copy-start | bytes 4612
  21.8 27.6 %copy-start.11 = (bf16[768]{0:T(1024)(128)(2,1)S(1)}, bf16[768]{0:T(1024)(128)(2,1)}, u32[]{:S(2)}) copy-start(bf16[768]{0:T(1024)(128)(2,1)} %param.23) | copy-start | bytes 4612
  21.8 28.2 %copy-start.12 = (bf16[768]{0:T(1024)(128)(2,1)S(1)}, bf16[768]{0:T(1024)(128)(2,1)}, u32[]{:S(2)}) copy-start(bf16[768]{0:T(1024)(128)(2,1)} %param.25) | copy-start | bytes 4612
  21.8 28.7 %copy-start.9 = (bf16[1536]{0:T(1024)(128)(2,1)S(1)}, bf16[1536]{0:T(1024)(128)(2,1)}, u32[]{:S(2)}) copy-start(bf16[1536]{0:T(1024)(128)(2,1)} %param.27) | copy-start | bytes 9220
  21.9 29.3 %copy-start.5 = (bf16[512,768]{1,0:T(8,128)(2,1)S(1)}, bf16[512,768]{1,0:T(8,128)(2,1)}, u32[]{:S(2)}) copy-start(bf16[512,768]{1,0:T(8,128)(2,1)} %param.33) | copy-start | bytes 2359300
  48.7 5.5 %collective-permute-start.2 = (bf16[1024,384]{1,0:T(8,128)(2,1)}, bf16[1024,384]{1,0:T(8,128)(2,1)S(1)}, u32[]{:S(2)}, u32[]{:S(2)}) collective-permute-start(bf16[1024,384]{1,0:T(8,128)(2,1)} %get-tuple-element.45.mine_ref.att_ref), channel_id=1, source_target_pairs={{0,1},{1,0},{2,3},{3,2},{4,5},{5,4},{6,7},{7,6},{8,9},{9,8},{10,11... | collective-permute-start | bytes 2359304 | tf_op jit(solution)/shard_map/ppermute | solution.py:622
  80.4 2.6 copy-start.13
  80.4 4.6 %collective-permute-start.4 = (bf16[1024,768]{1,0:T(8,128)(2,1)}, bf16[1024,768]{1,0:T(8,128)(2,1)S(1)}, u32[]{:S(2)}, u32[]{:S(2)}) collective-permute-start(bf16[1024,768]{1,0:T(8,128)(2,1)} %get-tuple-element.47.gh_ref), channel_id=1, source_target_pairs={{0,1},{1,0},{2,3},{3,2},{4,5},{5,4},{6,7},{7,6},{8,9},{9,8},{10,11... | collective-permute-start | bytes 4718600 | tf_op jit(solution)/shard_map/ppermute | solution.py:622
  82.9 3.5 %collective-permute-start.5 = (bf16[512,768]{1,0:T(8,128)(2,1)}, bf16[512,768]{1,0:T(8,128)(2,1)S(1)}, u32[]{:S(2)}, u32[]{:S(2)}) collective-permute-start(bf16[512,768]{1,0:T(8,128)(2,1)} %slice.79), channel_id=1, source_target_pairs={{0,1},{1,0},{2,3},{3,2},{4,5},{5,4},{6,7},{7,6},{8,9},{9,8},{10,11... | collective-permute-start | bytes 2359304 | tf_op jit(solution)/shard_map/ppermute | solution.py:622
  86.4 0.9 copy-start.3
  167.5 11.1 %collective-permute-start.6 = (bf16[512,768]{1,0:T(8,128)(2,1)}, bf16[512,768]{1,0:T(8,128)(2,1)S(1)}, u32[]{:S(2)}, u32[]{:S(2)}) collective-permute-start(bf16[512,768]{1,0:T(8,128)(2,1)} %slice.80), channel_id=1, source_target_pairs={{0,1},{1,0},{2,3},{3,2},{4,5},{5,4},{6,7},{7,6},{8,9},{9,8},{10,11... | collective-permute-start | bytes 2359304 | tf_op jit(solution)/shard_map/ppermute | solution.py:622
  168.0 10.5 %copy-start.7 = (f32[8,768]{1,0:T(8,128)S(1)}, f32[8,768]{1,0:T(8,128)}, u32[]{:S(2)}) copy-start(f32[8,768]{1,0:T(8,128)} %get-tuple-element.64) | copy-start | bytes 73732
  168.0 10.5 %copy-start.8 = (f32[1,1152]{1,0:T(1,128)S(1)}, f32[1,1152]{1,0:T(1,128)}, u32[]{:S(2)}) copy-start(f32[1,1152]{1,0:T(1,128)} %get-tuple-element.65) | copy-start | bytes 13828
  178.6 7.8 %copy-start.6 = (f32[1,2304]{1,0:T(1,128)}, f32[1,2304]{1,0:T(1,128)S(1)}, u32[]{:S(2)}) copy-start(f32[1,2304]{1,0:T(1,128)S(1)} %constant_dynamic-update-slice_fusion.4.bqkv_ref) | copy-start | bytes 27652
  178.6 0.9 copy-start.4
  186.4 118.7 %copy-start.1 = (s32[1,12,16,4]{2,3,1,0:T(4,128)S(1)}, s32[1,12,16,4]{2,3,1,0:T(4,128)}, u32[]{:S(2)}) copy-start(s32[1,12,16,4]{2,3,1,0:T(4,128)} %param.31) | copy-start | bytes 9220

commit v3 on v2

--- a/solution.py
+++ b/solution.py
@@ -164,8 +164,8 @@
 
 
 class Vector:
-    def __init__(self, net, bufs, send, recv, both):
-        self.net, self.bufs, self.send, self.recv, self.both = net, bufs, send, recv, both
+    def __init__(self, net, bufs, send, recv):
+        self.net, self.bufs, self.send, self.recv = net, bufs, send, recv
 
     def copies(self, phase):
         net, out = self.net, []
@@ -199,87 +199,6 @@
         if phase < 3:
             self.bufs[phase + 1] = total
         return total
-
-
-def grads_body(
-    n, up_ref, down_ref, out_ref, qkv_ref, rows_ref, bqkv_ref, bup_ref,
-    oup_ref, odown_ref, oout_ref, oqkv_ref, orows_ref, obqkv_ref, obup_ref, *scratch,
-):
-    net = Net(n)
-    bufs, tail = scratch[:20], scratch[20:]
-    sout, sqkv, gout, gqkv, vrows, vbqkv, vbup, send, recv = tail
-    parts = []
-    for i, src in enumerate((down_ref, up_ref, out_ref, qkv_ref)):
-        parts.append(Scatter(net, src, bufs[5 * i : 5 * i + 5], send.at[i], recv.at[i]))
-    vectors = [Vector(net, ref, send.at[4 + i], recv.at[4 + i], i < 2) for i, ref in enumerate((vrows, vbqkv, vbup))]
-    vrows[0], vbqkv[0], vbup[0] = rows_ref[...], bqkv_ref[...], bup_ref[...]
-    half = sout.shape[1]
-
-    def whole(ref):
-        def put(total):
-            ref[...] = total
-
-        return put
-
-    def halves(ref):
-        def put(total):
-            ref[0], ref[1] = total[:half], total[half:]
-
-        return put
-
-    net.barrier()
-    for part in parts:
-        part.start(0)
-    for v in vectors:
-        v.start(0)
-    for phase in (0, 1):
-        for part in parts:
-            part.finish(phase)
-            part.start(phase + 1)
-        for v in vectors:
-            v.finish(phase)
-            v.start(phase + 1)
-    for part, put in zip(parts, (whole(odown_ref), whole(oup_ref), halves(sout), halves(sqkv))):
-        part.finish(2, put)
-    last = net.slots() - 1
-    swaps = []
-    for i, (src, dst) in enumerate(((sout, gout), (sqkv, gqkv))):
-        swaps.append(
-            pltpu.make_async_remote_copy(
-                src_ref=src.at[1 - net.f], dst_ref=dst, send_sem=send.at[2 + i, last], recv_sem=recv.at[2 + i, last],
-                device_id={"feat": 1 - net.f}, device_id_type=MESH,
-            )
-        )
-    for swap in swaps:
-        swap.start()
-    rows = vectors[0].finish(2)
-    bqkv = vectors[1].finish(2)
-    bup = vectors[2].finish(2)
-    vectors[0].start(3)
-    vectors[1].start(3)
-    width = rows.shape[1]
-    lanes = orows_ref.shape[1]
-    where = 2 * net.s + net.f
-
-    def cut(value, per, index, size):
-        shift = lax.rem(size - index * per, size)
-        return pltpu.roll(value, shift, 1)[:, :lanes]
-
-    obup_ref[...] = cut(bup, bup.shape[1] // n, net.s, bup.shape[1])
-    rows = vectors[0].finish(3)
-    bqkv = vectors[1].finish(3)
-    orows_ref[...] = cut(rows, width // (2 * n), where, width)
-    obqkv_ref[...] = cut(bqkv, bqkv.shape[1] // (2 * n), where, bqkv.shape[1])
-    for swap in swaps:
-        swap.wait()
-    own = sout.shape[2]
-    f = net.f
-    oout_ref[:, ds(f, own)] = sout[f]
-    oout_ref[:, ds(1 - f, own)] = gout[...]
-    for i in range(3):
-        part = slice(i * own, (i + 1) * own)
-        oqkv_ref[:, ds(2 * i + f, own)] = sqkv[f, :, part]
-        oqkv_ref[:, ds(2 * i + 1 - f, own)] = gqkv[:, part]
 
 
 def call(body, outs, ins, specs=None, scratch=(), name=None, net=None):
@@ -462,18 +381,18 @@
         normed, inv = norm(mixed)
         g = gh_ref[rows, :].astype(F32) + gho_ref[rows, :].astype(F32)
         gm = og + norm_back(g, normed, inv, gain)
-        gm_ref[rows, :] = gm
         gb = gm.astype(BF)
         gb_ref[rows, :] = gb
         gatt_ref[rows, :] = nt(gb, w_ref[ds(f, half), :])
 
         @pl.when(i < own)
         def _():
+            gm_ref[rows, :] = gm
             y_ref[rows, :] = (
                 mixed + hid_ref[rows, :].astype(F32) + hido_ref[rows, :].astype(F32) + bd_ref[...].astype(F32)
             ).astype(BF)
             for j, term in enumerate((g * normed, g, gb.astype(F32), og)):
-                vec_ref[j : j + 1, :] += jnp.sum(term, axis=0, keepdims=True)
+                vec_ref[j + 2 : j + 3, :] += jnp.sum(term, axis=0, keepdims=True)
 
         return 0
 
@@ -485,9 +404,8 @@
     put_chunks(dw_ref, (1 - f) * per, tn(other_ref[...], gb_own), net)
 
 
-def attb_body(
-    qkv_ref, s_ref, m_ref, att_ref, den_ref, gatt_ref,
-    gqkv_ref, pq_ref, pk_ref, gn_ref, gq_ref, gpq_ref,
+def heads_back(
+    qkv_ref, s_ref, m_ref, att_ref, den_ref, gatt_ref, gqkv_ref, pq_ref, pk_ref, gn_ref, gq_ref, gpq_ref, after
 ):
     rows_all = qkv_ref.shape[0]
     scale = HEAD_DIM ** (-0.5)
@@ -559,49 +477,186 @@
             return 0
 
         lax.fori_loop(0, rows_all // TILE, last, 0)
+        for k, then in after.items():
+            pl.when(h == k)(then)
         return 0
 
     lax.fori_loop(0, qkv_ref.shape[1] // (3 * HEAD_DIM), head, 0)
 
 
-def qkvb_body(n, gqkv_ref, h_ref, w_ref, gh_ref, dw_ref, db_ref):
-    db_ref[...] = jnp.zeros_like(db_ref)
-
-    def step(i, _):
-        rows = ds(i, TILE)
-        g = gqkv_ref[rows, :]
-        db_ref[...] += jnp.sum(g.astype(F32), axis=0, keepdims=True)
-        gh_ref[rows, :] = nt(g, w_ref[...]).astype(BF)
+def back_body(
+    n, qkv_ref, s_ref, m_ref, att_ref, den_ref, gatt_ref, h_ref, w_ref, x_ref, g_ref, gm_ref, up_ref, down_ref, out_ref,
+    vec_ref, bup_ref, dx_ref, oup_ref, odown_ref, oout_ref, oqkv_ref, orows_ref, obqkv_ref, obup_ref, *scratch,
+):
+    net = Net(n)
+    bufs, tail = scratch[:30], scratch[30:]
+    pq, pk, gn, gq, gpq, gqkv, gw, gh_send, gh_got, sout, rout, sqkv, rqkv, vrows, vbqkv, vbup, send, recv = tail
+    f = net.f
+    other = {"feat": 1 - f}
+    parts = [
+        Scatter(net, src, bufs[5 * i : 5 * i + 5], send.at[i], recv.at[i])
+        for i, src in enumerate((down_ref, up_ref, out_ref, gw.at[0], gw.at[1], gw.at[2]))
+    ]
+    down, up, out = parts[:3]
+    pairs = parts[3:]
+    vectors = [Vector(net, ref, send.at[6 + i], recv.at[6 + i]) for i, ref in enumerate((vrows, vbqkv, vbup))]
+    last = net.slots() - 1
+    half = sout.shape[1]
+    rows = x_ref.shape[0]
+    width = x_ref.shape[1]
+    own = width // 2
+    lanes = orows_ref.shape[1]
+
+    def whole(ref):
+        def put(total):
+            ref[...] = total
+
+        return put
+
+    def halves(ref):
+        def put(total):
+            ref[0], ref[1] = total[:half], total[half:]
+
+        return put
+
+    def swap(i, src, dst):
+        return pltpu.make_async_remote_copy(
+            src_ref=src, dst_ref=dst, send_sem=send.at[i, last], recv_sem=recv.at[i, last],
+            device_id=other, device_id_type=MESH,
+        )
+
+    def move(part, phase):
+        part.finish(phase)
+        part.start(phase + 1)
+
+    def weight(p):
+        g = jnp.concatenate([gqkv[:, i * own + p * 128 : i * own + (p + 1) * 128] for i in range(3)], axis=1)
+        per = own // gw.shape[2]
+        for i in range(2):
+            put_chunks(gw.at[p], i * per, tn(h_ref[:, i * own : (i + 1) * own], g), net)
+        pairs[p].start(0)
+
+    net.barrier()
+    for part in (down, up, out):
+        part.start(0)
+
+    def after1():
+        move(down, 0)
+        weight(0)
+
+    def after2():
+        move(up, 0)
+        move(out, 0)
+
+    def after3():
+        move(down, 1)
+        move(pairs[0], 0)
+        weight(1)
+
+    def after4():
+        move(up, 1)
+        move(out, 1)
+        move(pairs[0], 1)
+
+    heads_back(
+        qkv_ref, s_ref, m_ref, att_ref, den_ref, gatt_ref, gqkv, pq, pk, gn, gq, gpq,
+        {1: after1, 2: after2, 3: after3, 4: after4},
+    )
+    weight(2)
+    tiles = rows // TILE
+
+    def far(i, total):
+        g = gqkv[ds(tiles + i, TILE), :]
+        gh_send[ds(i, TILE), :] = nt(g, w_ref[...]).astype(BF)
+        return total + jnp.sum(g.astype(F32), axis=0, keepdims=True)
+
+    total = lax.fori_loop(0, tiles, far, jnp.zeros((1, 3 * own), F32))
+    gh_swap = swap(9, gh_send, gh_got)
+    gh_swap.start()
+    move(pairs[1], 0)
+
+    def sums(i, total):
+        return total + jnp.sum(gqkv[ds(i, TILE), :].astype(F32), axis=0, keepdims=True)
+
+    total = lax.fori_loop(0, tiles, sums, total)
+    vbqkv[0] = jnp.zeros_like(vbqkv[0])
+    for i in range(3):
+        vbqkv[0, :, ds(2 * i + f, own)] = total[:, i * own : (i + 1) * own]
+    vbup[0] = bup_ref[...]
+    down.finish(2, whole(odown_ref))
+    out.finish(2, halves(sout))
+    out_swap = swap(2, sout.at[1 - f], rout)
+    out_swap.start()
+    up.finish(2, whole(oup_ref))
+    move(pairs[1], 1)
+    move(pairs[2], 0)
+    gh_swap.wait()
+    gain = g_ref[...].astype(F32)
+    vrows[0] = vec_ref[...]
+
+    def norm1(i, _):
+        r = ds(i, TILE)
+        normed, inv = norm(x_ref[r, :].astype(F32))
+        g = nt(gqkv[r, :], w_ref[...]) + gh_got[r, :].astype(F32)
+        dx_ref[r, :] = gm_ref[r, :] + norm_back(g, normed, inv, gain)
+        vrows[0, 0:1, :] += jnp.sum(g * normed, axis=0, keepdims=True)
+        vrows[0, 1:2, :] += jnp.sum(g, axis=0, keepdims=True)
         return 0
 
-    lax.fori_loop(0, gqkv_ref.shape[0] // TILE, step, 0)
-
-    net = Net(n)
-    wide = h_ref.shape[1] // 2
-    per = wide // dw_ref.shape[1]
-
-    def weight(i, _):
-        rows = ds(i, wide)
-        put_chunks(dw_ref, i * per, tn(h_ref[:, rows], gqkv_ref[...]), net)
-        return 0
-
-    lax.fori_loop(0, 2, weight, 0)
-
-
-def ln1b_body(gh_ref, gho_ref, x_ref, g_ref, gm_ref, dx_ref, vec_ref):
-    gain = g_ref[...].astype(F32)
-    vec_ref[...] = jnp.zeros_like(vec_ref)
-
-    def step(i, _):
-        rows = ds(i, TILE)
-        normed, inv = norm(x_ref[rows, :].astype(F32))
-        g = gh_ref[rows, :].astype(F32) + gho_ref[rows, :].astype(F32)
-        dx_ref[rows, :] = gm_ref[rows, :] + norm_back(g, normed, inv, gain)
-        vec_ref[0:1, :] += jnp.sum(g * normed, axis=0, keepdims=True)
-        vec_ref[1:2, :] += jnp.sum(g, axis=0, keepdims=True)
-        return 0
-
-    lax.fori_loop(0, dx_ref.shape[0] // TILE, step, 0)
+    lax.fori_loop(0, tiles, norm1, 0)
+    for v in vectors:
+        v.start(0)
+    move(pairs[2], 1)
+    for p in (0, 1):
+        pairs[p].finish(2, halves(sqkv.at[p]))
+    for v in vectors:
+        v.finish(0)
+        v.start(1)
+    swaps = [swap(3 + p, sqkv.at[p, 1 - f], rqkv.at[p]) for p in range(3)]
+    swaps[0].start()
+    swaps[1].start()
+    for v in vectors:
+        v.finish(1)
+        v.start(2)
+    pairs[2].finish(2, halves(sqkv.at[2]))
+    swaps[2].start()
+    vecs, bqkv, bup = [v.finish(2) for v in vectors]
+    vectors[0].start(3)
+    vectors[1].start(3)
+    where = 2 * net.s + f
+
+    def cut(value, per, index, size):
+        return pltpu.roll(value, lax.rem(size - index * per, size), 1)[:, :lanes]
+
+    obup_ref[...] = cut(bup, bup.shape[1] // n, net.s, bup.shape[1])
+    out_swap.wait()
+    oout_ref[:, ds(f, own)] = sout[f]
+    oout_ref[:, ds(1 - f, own)] = rout[...]
+
+    def cols(i, p, side):
+        return pl.ds(pl.multiple_of(i * width + side * own + p * 128, 128), 128)
+
+    for p in range(3):
+        swaps[p].wait()
+        for i in range(3):
+            part = slice(i * 128, (i + 1) * 128)
+            oqkv_ref[:, cols(i, p, f)] = sqkv[p, f, :, part]
+            oqkv_ref[:, cols(i, p, 1 - f)] = rqkv[p, :, part]
+    vecs = vectors[0].finish(3)
+    bqkv = vectors[1].finish(3)
+    orows_ref[...] = cut(vecs, width // (2 * n), where, width)
+    obqkv_ref[...] = cut(bqkv, bqkv.shape[1] // (2 * n), where, bqkv.shape[1])
+
+
+def emit_body(dx_ref, up_ref, down_ref, out_ref, qkv_ref, rows_ref, bqkv_ref, bup_ref, *outs):
+    odx, oup, odown, oout, oqkv, obqkv, obup = outs[:7]
+    odx[...], oup[...], oout[...], oqkv[...] = dx_ref[...], up_ref[...], out_ref[...], qkv_ref[...]
+    down = down_ref[...]
+    odown[...] = down if odown.shape == down.shape else down.T
+    obqkv[...] = bqkv_ref[:, : obqkv.shape[1]]
+    obup[...] = bup_ref[:, : obup.shape[1]]
+    for i, ref in enumerate(outs[7:]):
+        ref[...] = rows_ref[i : i + 1, : ref.shape[1]]
 
 
 def body(
@@ -686,63 +741,52 @@
     gm, gatt, d_out, y, vec2 = call(
         functools.partial(outb_body, n),
         [
-            ((tokens, width), F32), ((tokens, half_width), F32), ((n, chunk, half_width), BF),
+            ((rows, width), F32), ((tokens, half_width), F32), ((n, chunk, half_width), BF),
             ((rows, width), BF), ((8, width), F32),
         ],
         [gh2, gh_far, mixed, og, hid, hid_far, row(b_down), row(ln2_gain), w_out, att, att_far],
         scratch=[pltpu.VMEM((tokens, width), BF)], name="outb",
     )
-    gqkv, = call(
-        attb_body, [((tokens, 3 * half_width), BF)], [qkv, table, marks_t, att, den, gatt],
-        scratch=[phi, phi, pltpu.VMEM((tokens, 128), BF), pltpu.VMEM((tokens, 128), F32), pltpu.VMEM((tokens, feats), F32)],
-        name="attb",
-    )
-    gh1, d_qkv, d_bqkv = call(
-        functools.partial(qkvb_body, n),
-        [((tokens, width), BF), ((n, chunk, 3 * half_width), BF), ((1, 3 * half_width), F32)],
-        [gqkv, h1, w_own], name="qkvb",
-    )
-    gh1_far = swap(gh1[rows:])
-    dx, vec1 = call(
-        ln1b_body, [((rows, width), F32), ((8, width), F32)],
-        [gh1, gh1_far, layer_input, row(ln1_gain), gm], name="ln1b",
-    )
-
-    d_b = jnp.zeros((1, 3 * width), F32)
-    for i in range(3):
-        d_b = lax.dynamic_update_slice(
-            d_b, d_bqkv[:, i * half_width : (i + 1) * half_width], (0, i * width + f * half_width)
-        )
-    vecs = jnp.concatenate([vec1[:2], vec2[:4], jnp.zeros((2, width), F32)], axis=0)
     slots = sum(split(n)) + split(n)[0] - 3 + 1
     bufs = []
-    for cols in (hidden, hidden, half_width, 3 * half_width):
+    for cols in (hidden, hidden, half_width, half_width, half_width, half_width):
         bufs += scatter_bufs(n, chunk, cols)
     half_chunk = chunk // 2
-    sems = pltpu.SemaphoreType.DMA((7, slots))
-    up, down, out, full, vecs, d_b, d_bup = call(
-        functools.partial(grads_body, n),
+    sems = pltpu.SemaphoreType.DMA((10, slots))
+    sums = call(
+        functools.partial(back_body, n),
         [
-            ((chunk, hidden), F32), ((chunk, hidden), F32), ((half_chunk, width), F32), ((half_chunk, 3 * width), F32),
-            ((8, 128), F32), ((1, 128), F32), ((1, 128), F32),
+            ((rows, width), F32), ((chunk, hidden), F32), ((chunk, hidden), F32), ((half_chunk, width), F32),
+            ((half_chunk, 3 * width), F32), ((8, 128), F32), ((1, 128), F32), ((1, 128), F32),
         ],
-        [d_up, d_down, d_out, d_qkv, vecs, d_b, d_bup],
+        [
+            qkv, table, marks_t, att, den, gatt, h1, w_own, layer_input, row(ln1_gain), gm, d_up, d_down, d_out, vec2, d_bup,
+        ],
         scratch=bufs + [
-            pltpu.VMEM((2, half_chunk, half_width), F32), pltpu.VMEM((2, half_chunk, 3 * half_width), F32),
-            pltpu.VMEM((half_chunk, half_width), F32), pltpu.VMEM((half_chunk, 3 * half_width), F32),
+            phi, phi, pltpu.VMEM((tokens, 128), BF), pltpu.VMEM((tokens, 128), F32), pltpu.VMEM((tokens, feats), F32),
+            pltpu.VMEM((tokens, 3 * half_width), BF), pltpu.VMEM((3, n, chunk, half_width), BF),
+            pltpu.VMEM((rows, width), BF), pltpu.VMEM((rows, width), BF),
+            pltpu.VMEM((2, half_chunk, half_width), F32), pltpu.VMEM((half_chunk, half_width), F32),
+            pltpu.VMEM((3, 2, half_chunk, half_width), F32), pltpu.VMEM((3, half_chunk, half_width), F32),
             pltpu.VMEM((4 + slots, 8, width), F32), pltpu.VMEM((4 + slots, 1, 3 * width), F32),
             pltpu.VMEM((4 + slots, 1, hidden), F32), sems, sems,
         ],
-        name="grads", net=1,
+        name="back", net=1,
     )
     own = width // (2 * n)
-
-    def vec(i):
-        return vecs[i, :own]
-
+    turn = chunk % 8 == 0
+    dx, up, down, out, full, d_b, d_bup, *vec = call(
+        emit_body,
+        [
+            ((rows, width), F32), ((chunk, hidden), F32), ((hidden, chunk) if turn else (chunk, hidden), F32),
+            ((half_chunk, width), F32), ((half_chunk, 3 * width), F32), ((1, 3 * own), F32), ((1, hidden // n), F32),
+        ] + [((1, own), F32)] * 6,
+        sums, name="emit",
+    )
+    vec = [v.reshape(-1) for v in vec]
     return (
-        y, dx, vec(0), vec(1), full, d_b[0, : 3 * own], out, vec(4), vec(2), vec(3), up, d_bup[0, : hidden // n],
-        down.T, vec(5),
+        y, dx, vec[0], vec[1], full, d_b.reshape(-1), out, vec[4], vec[2], vec[3], up, d_bup.reshape(-1),
+        down if turn else down.T, vec[5],
     )
 
 

time: 306 us -> 222 us (0.73)
  Pallas kernels: 261 us -> 191 us
  local copies, waits for them, and re-layouts: 33.7 us -> 20.9 us
    pallas_call x10 -> x8, Pallas kernels: 261 us -> 191 us  [call(): pl.pallas_call(body, out_shape=[jax.ShapeDtypeStruct(s, d) for s, d in ou...]
    unnamed x35 -> x32, local copies, waits for them, and re-layouts: 10.3 us -> 4.96 us
    squeeze x3 -> x0, local copies, waits for them, and re-layouts: 3.7 us -> none  [the longest x1 1.44 us: vec(): return vecs[i, :own]]
  transfers between devices with their start and end apart: 7 -> 6, of which waited for: 0 -> 0; matrix products, arithmetic and copies ran while one was open for 8% -> 11% of each run, Pallas kernels for 15% -> 20%
where the time goes in v3:
time: 222 us
  Pallas kernels  191 us (86%)
  local copies, waits for them, and re-layouts  20.9 us (9%)
  other arithmetic  7.25 us (3%)
    pallas_call x8, Pallas kernels, call(): pl.pallas_call(body, out_shape=[jax.ShapeDtypeStruct(s, d) for s, d in ou...  191 us
    unnamed x32, local copies, waits for them, and re-layouts  4.96 us
  transfers between devices with their start and end apart: 6, of which 0 were waited for; matrix products, arithmetic and copies ran while one was open for 11% of the time, Pallas kernels for 20%

profile of v3, /device:TPU:0, one launch (start us, length us, event | category | flops | bytes accessed | tf_op | source)
XLA Modules:
  0.0 221.7 jit_solution(8684102246941525467)
XLA Ops:
  0.6 0.0 copy-start
  0.7 0.6 collective-permute-start
  1.2 1.1 add_convert_fusion
  2.3 0.7 constant_dynamic-slice_fusion.2
  2.9 0.0 collective-permute-start.1
  3.0 0.5 collective-permute-start.3
  3.5 1.6 constant_dynamic-slice_fusion.5
  5.1 0.0 copy-done.12
  5.1 0.1 fusion.9
  5.2 0.0 copy-done.6
  5.3 0.6 reshape.106.g_ref
  5.8 0.0 copy-done.7
  5.8 0.6 reshape.107.s_ref
  6.4 0.0 copy-done
  6.4 0.0 copy-done.13
  6.5 0.2 and_reduce_fusion
  6.7 0.3 broadcast_in_dim.4
  7.0 1.1 reshape_reshape.6.m_ref
  8.0 1.4 pad_maximum_fusion.w_ref
  9.4 0.6 pad_maximum_fusion.4.b_ref
  10.0 0.0 copy-done.2
  10.0 0.9 constant_dynamic-update-slice_fusion.1
  11.0 0.0 collective-permute-done.1
  11.0 0.9 pad_maximum_fusion.3
  11.9 0.8 fusion.2.s_ref
  12.8 0.0 collective-permute-done
  12.8 0.9 constant_dynamic-update-slice_fusion.x_ref
  13.7 6.9 %qkv.1 = (bf16[1024,768]{1,0:T(8,128)(2,1)}, bf16[1024,1152]{1,0:T(8,128)(2,1)}) custom-call(bf16[1024,768]{1,0:T(8,128)(2,1)} %constant_dynamic-update-slice_fusion.x_ref, bf16[1,768]{1,0:T(2,128)(2,1)} %reshape.106.g_ref, bf16[1,768]{1,0:T(2,128)(2,1)} %reshape.107.s_ref, bf16[768,1152]{1,0:T(8,128)(2,1)} %pad_maximum_fusion.w_ref, ...), custom_call_target="tpu_custom_call" | custom-call | tf_op jit(solution)/shard_map/qkv/pallas_call | solution.py:205
  20.6 0.0 copy-start.5
  20.6 0.0 copy-start.4
  20.7 26.8 %att.1 = (bf16[1024,384]{1,0:T(8,128)(2,1)}, f32[1024,384]{1,0:T(8,128)}) custom-call(bf16[1024,1152]{1,0:T(8,128)(2,1)} %get-tuple-element.53.qkv_ref, bf16[3,128,512]{2,1,0:T(8,128)(2,1)} %fusion.2.s_ref, f32[6,4,4,1024]{3,2,1,0:T(4,128)} %reshape_reshape.6.m_ref), custom_call_target="tpu_custom_call" | custom-call | tf_op jit(solution)/shard_map/att/pallas_call | solution.py:205
  47.5 0.0 collective-permute-start.2
  47.5 0.0 copy-done.8
  47.5 0.6 reshape.110.g_ref
  48.1 0.6 reshape.109.b_ref
  48.7 0.6 reshape.111.s_ref
  49.3 0.0 copy-done.5
  49.3 0.6 reshape.112.b_ref
  49.9 0.9 constant_dynamic-update-slice_fusion.3
  50.8 0.0 collective-permute-done.3
  50.8 2.1 constant_dynamic-update-slice_fusion.2.og_ref
  52.9 0.0 collective-permute-done.2
  52.9 0.1 fusion.7
  53.0 1.0 pad_maximum_fusion.2.other_ref
  54.0 7.3 %mix.1 = (f32[1024,768]{1,0:T(8,128)}, bf16[1024,768]{1,0:T(8,128)(2,1)}) custom-call(bf16[1024,768]{1,0:T(8,128)(2,1)} %constant_dynamic-update-slice_fusion.x_ref, bf16[1024,384]{1,0:T(8,128)(2,1)} %get-tuple-element.54.mine_ref.att_ref, bf16[1024,384]{1,0:T(8,128)(2,1)} %pad_maximum_fusion.2.other_ref, bf16[768,768]{1,0:T(8,128)(2,1)} %w_ref.3, ...), custom_call_target="tpu_custom_call" | custom-call | tf_op jit(solution)/shard_map/mix/pallas_call | solution.py:205
  61.3 17.9 %ff.1 = (bf16[1024,1536]{1,0:T(8,128)(2,1)}, bf16[1024,1536]{1,0:T(8,128)(2,1)}, bf16[1024,768]{1,0:T(8,128)(2,1)}, bf16[1024,768]{1,0:T(8,128)(2,1)}, f32[1,1536]{1,0:T(1,128)}) custom-call(bf16[1024,768]{1,0:T(8,128)(2,1)} %get-tuple-element.55.h_ref, bf16[1024,768]{1,0:T(8,128)(2,1)} %constant_dynamic-update-slice_fusion.2.og_ref, ...), custom_call_target="tpu_custom_call" | custom-call | tf_op jit(solution)/shard_map/ff/pallas_call | solution.py:205
  79.2 0.5 collective-permute-start.4
  79.7 2.1 slice.37
  81.7 0.0 collective-permute-start.5
  81.7 0.6 reshape.113.bd_ref
  82.3 0.1 copy.43
  82.4 0.3 broadcast_in_dim.5
  82.7 1.1 reshape_reshape.7.m_ref
  83.8 10.4 %ffw.1 = (bf16[16,48,1536]{2,1,0:T(8,128)(2,1)}, bf16[16,48,1536]{2,1,0:T(8,128)(2,1)}) custom-call(bf16[1024,768]{1,0:T(8,128)(2,1)} %get-tuple-element.55.h_ref, bf16[1024,768]{1,0:T(8,128)(2,1)} %constant_dynamic-update-slice_fusion.2.og_ref, bf16[1024,1536]{1,0:T(8,128)(2,1)} %get-tuple-element.64.act_ref, bf16[1024,1536]{1,0:T(8,128)(2,1)} %get-tuple-element.65.gp_ref), custom_call_target="tpu_custom_call" | custom-call | tf_op jit(solution)/shard_map/ffw/pallas_call | solution.py:205
  94.2 0.0 collective-permute-done.4
  94.2 1.5 fusion.6
  95.7 1.2 pad_maximum_fusion.1.gho_ref
  96.9 0.0 collective-permute-done.5.hido_ref
  96.9 0.9 copy-done.3
  97.9 12.4 %outb.1 = (f32[512,768]{1,0:T(8,128)}, f32[1024,384]{1,0:T(8,128)}, bf16[16,48,384]{2,1,0:T(8,128)(2,1)}, bf16[512,768]{1,0:T(8,128)(2,1)}, f32[8,768]{1,0:T(8,128)}) custom-call(bf16[1024,768]{1,0:T(8,128)(2,1)} %get-tuple-element.56.gh_ref, bf16[1024,768]{1,0:T(8,128)(2,1)} %pad_maximum_fusion.1.gho_ref, f32[1024,768]{1,0:T(8,128)} %get-tuple-element.57.mixed_ref, ...), custom_call_target="tpu_custom_call" | custom-call | tf_op jit(solution)/shard_map/outb/pallas_call | solution.py:205
  110.3 105.8 %back.1 = (f32[512,768]{1,0:T(8,128)}, f32[48,1536]{1,0:T(8,128)}, f32[48,1536]{1,0:T(8,128)}, f32[24,768]{1,0:T(8,128)}, f32[24,2304]{1,0:T(8,128)}, /*index=5*...) custom-call(bf16[1024,1152]{1,0:T(8,128)(2,1)} %get-tuple-element.53.qkv_ref, bf16[3,128,512]{2,1,0:T(8,128)(2,1)} %fusion.2.s_ref, ...), custom_call_target="tpu_custom_call" | custom-call | tf_op jit(solution)/shard_map/back/pallas_call | solution.py:205
  216.1 0.0 copy-start.1
  216.1 3.5 %emit.1 = (f32[512,768]{1,0:T(8,128)}, f32[48,1536]{1,0:T(8,128)}, f32[1536,48]{1,0:T(8,128)}, f32[24,768]{1,0:T(8,128)}, f32[24,2304]{1,0:T(8,128)}, /*index=5*...) custom-call(f32[512,768]{1,0:T(8,128)} %get-tuple-element.71.dx_ref,, ...), custom_call_target="tpu_custom_call" | custom-call | tf_op jit(solution)/shard_map/emit/pallas_call | solution.py:205
  219.6 2.1 copy.44
  (26 shorter events, 0.1 us)
Async XLA Ops:
  0.6 5.8 %copy-start = (s32[1,12,16,4]{2,3,1,0:T(4,128)S(1)}, s32[1,12,16,4]{2,3,1,0:T(4,128)}, u32[]{:S(2)}) copy-start(s32[1,12,16,4]{2,3,1,0:T(4,128)} %param.31) | copy-start | bytes 9220
  0.7 12.1 %collective-permute-start = (bf16[512,768]{1,0:T(8,128)(2,1)}, bf16[512,768]{1,0:T(8,128)(2,1)S(1)}, u32[]{:S(2)}, u32[]{:S(2)}) collective-permute-start(bf16[512,768]{1,0:T(8,128)(2,1)} %x_ref.1), channel_id=1, source_target_pairs={{0,1},{1,0},{2,3},{3,2},{4,5},{5,4},{6,7},{7,6},{8,9},{9,8},{10,11... | collective-permute-start | bytes 2359304 | tf_op jit(solution)/shard_map/ppermute | solution.py:677
  2.9 8.0 %collective-permute-start.1 = (bf16[6,64,128]{2,1,0:T(8,128)(2,1)}, bf16[6,64,128]{2,1,0:T(8,128)(2,1)}, u32[]{:S(2)}, u32[]{:S(2)}) collective-permute-start(bf16[6,64,128]{2,1,0:T(8,128)(2,1)} %get-tuple-element.144), channel_id=1, source_target_pairs={{0,1},{1,0},{2,3},{3,2},{4,5},{5,4},{6,7},{7,6},{8,9},{9,8},{10,11... | collective-permute-start | bytes 294920 | tf_op jit(solution)/shard_map/ppermute | solution.py:677
  3.0 47.9 %collective-permute-start.3 = (bf16[512,768]{1,0:T(8,128)(2,1)}, bf16[512,768]{1,0:T(8,128)(2,1)}, u32[]{:S(2)}, u32[]{:S(2)}) collective-permute-start(bf16[512,768]{1,0:T(8,128)(2,1)} %param.33), channel_id=1, source_target_pairs={{0,1},{1,0},{2,3},{3,2},{4,5},{5,4},{6,7},{7,6},{8,9},{9,8},{10,11... | collective-permute-start | bytes 2359304 | tf_op jit(solution)/shard_map/ppermute | solution.py:677
  3.5 1.7 copy-start.12
  3.5 1.8 copy-start.6
  3.5 2.4 %copy-start.7 = (bf16[768]{0:T(1024)(128)(2,1)S(1)}, bf16[768]{0:T(1024)(128)(2,1)}, u32[]{:S(2)}) copy-start(bf16[768]{0:T(1024)(128)(2,1)} %param.19) | copy-start | bytes 4612
  3.5 3.0 %copy-start.13 = (s32[1,12,16]{2,0,1:T(1,128)S(1)}, s32[1,12,16]{2,0,1:T(1,128)}, u32[]{:S(2)}) copy-start(s32[1,12,16]{2,0,1:T(1,128)} %param.32) | copy-start | bytes 2308
  8.0 2.0 copy-start.2
  20.6 26.9 %copy-start.8 = (bf16[768]{0:T(1024)(128)(2,1)S(1)}, bf16[768]{0:T(1024)(128)(2,1)}, u32[]{:S(2)}) copy-start(bf16[768]{0:T(1024)(128)(2,1)} %param.24) | copy-start | bytes 4612
  20.6 27.5 %copy-start.9 = (bf16[768]{0:T(1024)(128)(2,1)S(1)}, bf16[768]{0:T(1024)(128)(2,1)}, u32[]{:S(2)}) copy-start(bf16[768]{0:T(1024)(128)(2,1)} %param.23) | copy-start | bytes 4612
  20.6 28.1 %copy-start.10 = (bf16[768]{0:T(1024)(128)(2,1)S(1)}, bf16[768]{0:T(1024)(128)(2,1)}, u32[]{:S(2)}) copy-start(bf16[768]{0:T(1024)(128)(2,1)} %param.25) | copy-start | bytes 4612
  20.6 28.7 %copy-start.5 = (bf16[1536]{0:T(1024)(128)(2,1)S(1)}, bf16[1536]{0:T(1024)(128)(2,1)}, u32[]{:S(2)}) copy-start(bf16[1536]{0:T(1024)(128)(2,1)} %param.27) | copy-start | bytes 9220
  20.6 29.2 %copy-start.4 = (bf16[512,768]{1,0:T(8,128)(2,1)S(1)}, bf16[512,768]{1,0:T(8,128)(2,1)}, u32[]{:S(2)}) copy-start(bf16[512,768]{1,0:T(8,128)(2,1)} %param.33) | copy-start | bytes 2359300
  47.5 5.4 %collective-permute-start.2 = (bf16[1024,384]{1,0:T(8,128)(2,1)}, bf16[1024,384]{1,0:T(8,128)(2,1)S(1)}, u32[]{:S(2)}, u32[]{:S(2)}) collective-permute-start(bf16[1024,384]{1,0:T(8,128)(2,1)} %get-tuple-element.54.mine_ref.att_ref), channel_id=1, source_target_pairs={{0,1},{1,0},{2,3},{3,2},{4,5},{5,4},{6,7},{7,6},{8,9},{9,8},{10,11... | collective-permute-start | bytes 2359304 | tf_op jit(solution)/shard_map/ppermute | solution.py:677
  79.2 2.6 %copy-start.11 = (bf16[768]{0:T(1024)(128)(2,1)S(1)}, bf16[768]{0:T(1024)(128)(2,1)}, u32[]{:S(2)}) copy-start(bf16[768]{0:T(1024)(128)(2,1)} %param.29) | copy-start | bytes 4612
  79.2 15.1 %collective-permute-start.4 = (bf16[1024,768]{1,0:T(8,128)(2,1)}, bf16[1024,768]{1,0:T(8,128)(2,1)}, u32[]{:S(2)}, u32[]{:S(2)}) collective-permute-start(bf16[1024,768]{1,0:T(8,128)(2,1)} %get-tuple-element.56.gh_ref), channel_id=1, source_target_pairs={{0,1},{1,0},{2,3},{3,2},{4,5},{5,4},{6,7},{7,6},{8,9},{9,8},{10,11... | collective-permute-start | bytes 4718600 | tf_op jit(solution)/shard_map/ppermute | solution.py:677
  81.7 15.2 %collective-permute-start.5 = (bf16[512,768]{1,0:T(8,128)(2,1)}, bf16[512,768]{1,0:T(8,128)(2,1)S(1)}, u32[]{:S(2)}, u32[]{:S(2)}) collective-permute-start(bf16[512,768]{1,0:T(8,128)(2,1)} %slice.37), channel_id=1, source_target_pairs={{0,1},{1,0},{2,3},{3,2},{4,5},{5,4},{6,7},{7,6},{8,9},{9,8},{10,11... | collective-permute-start | bytes 2359304 | tf_op jit(solution)/shard_map/ppermute | solution.py:677
  96.9 0.9 copy-start.3
  216.1 5.6 %copy-start.1 = (s32[1,12,16,4]{2,3,1,0:T(4,128)S(1)}, s32[1,12,16,4]{2,3,1,0:T(4,128)}, u32[]{:S(2)}) copy-start(s32[1,12,16,4]{2,3,1,0:T(4,128)} %param.31) | copy-start | bytes 9220

commit v4 on v3

--- a/solution.py
+++ b/solution.py
@@ -17,6 +17,8 @@
 F32 = jnp.float32
 EPS = 1e-05
 TILE = 256
+ATILE = 512
+BTILE = 512
 GELU_A = math.sqrt(2.0 / math.pi)
 GELU_B = 0.044715
 MESH = pl.DeviceIdType.MESH
@@ -269,11 +271,11 @@
         v_one = jnp.where(mine, qkv_ref[:, cols(2)], jnp.ones((), BF))
 
         def step(i, _):
-            rows = ds(i, TILE)
+            rows = ds(i, ATILE)
             q = jnp.where(mine, qkv_ref[rows, cols(0)] * BF(HEAD_DIM ** (-0.5)), zero)
             ex = jnp.exp(nt(q, qkv_ref[:, cols(1)]))
             low = nt(pq_ref[rows, :], pk_ref[...])
-            per = TILE // BLOCK
+            per = ATILE // BLOCK
             marks = m_ref[h, i]
             probs = jnp.concatenate(
                 [
@@ -294,13 +296,13 @@
             den_ref[rows, out_cols] = jnp.where(mine, den, den_ref[rows, out_cols])
             return 0
 
-        lax.fori_loop(0, qkv_ref.shape[0] // TILE, step, 0)
+        lax.fori_loop(0, qkv_ref.shape[0] // ATILE, step, 0)
         return 0
 
     lax.fori_loop(0, qkv_ref.shape[1] // (3 * HEAD_DIM), head, 0)
 
 
-def mix_body(x_ref, mine_ref, other_ref, w_ref, b_ref, g_ref, s_ref, mixed_ref, h_ref):
+def mix_tiles(x_ref, mine_ref, other_ref, w_ref, b_ref, g_ref, s_ref, mixed_ref, h_ref):
     f = lax.axis_index("feat")
     half = mine_ref.shape[1]
 
@@ -320,11 +322,13 @@
     lax.fori_loop(0, x_ref.shape[0] // TILE, step, 0)
 
 
-def ff_body(h_ref, og_ref, up_ref, down_ref, b_ref, act_ref, gp_ref, hid_ref, gh_ref, db_ref):
+def ff_tiles(h_ref, og_ref, up_ref, down_ref, b_ref, act_ref, gp_ref, hid_ref, gh_ref, db_ref, send):
+    tiles = h_ref.shape[0] // TILE
     db_ref[...] = jnp.zeros_like(db_ref)
 
     def step(i, _):
-        rows = ds(i, TILE)
+        tile = lax.rem(i + tiles // 2, tiles)
+        rows = ds(tile, TILE)
         v = nn(h_ref[rows, :], up_ref[...]) + b_ref[...].astype(F32)
         vv = v * v
         th = jnp.tanh(GELU_A * v * (1.0 + GELU_B * vv))
@@ -338,9 +342,10 @@
         gp_ref[rows, :] = gpl
         db_ref[...] += jnp.sum(gpl.astype(F32), axis=0, keepdims=True)
         gh_ref[rows, :] = nt(gpl, up_ref[...]).astype(BF)
+        send(i, tile)
         return 0
 
-    lax.fori_loop(0, h_ref.shape[0] // TILE, step, 0)
+    lax.fori_loop(0, tiles, step, 0)
 
 
 def put_chunks(out_ref, first, value, net):
@@ -349,7 +354,7 @@
         out_ref[net.place(first + i)] = value[i * rows : (i + 1) * rows].astype(BF)
 
 
-def ffw_body(n, h_ref, og_ref, act_ref, gp_ref, up_ref, down_ref):
+def ff_weights(n, h_ref, og_ref, act_ref, gp_ref, up_ref, down_ref):
     net = Net(n)
     wide = h_ref.shape[1] // 2
     per = wide // up_ref.shape[1]
@@ -363,7 +368,7 @@
     lax.fori_loop(0, 2, step, 0)
 
 
-def outb_body(
+def out_back(
     n, gh_ref, gho_ref, mixed_ref, og_ref, hid_ref, hido_ref, bd_ref, g_ref, w_ref, mine_ref, other_ref,
     gm_ref, gatt_ref, dw_ref, y_ref, vec_ref, gb_ref,
 ):
@@ -404,6 +409,60 @@
     put_chunks(dw_ref, (1 - f) * per, tn(other_ref[...], gb_own), net)
 
 
+def mid_body(
+    n, x_ref, att_ref, wout_ref, bout_ref, g_ref, s_ref, og_own_ref, up_ref, down_ref, bup_ref, bdown_ref,
+    gm_ref, gatt_ref, dout_ref, y_ref, vec_ref, dup_ref, ddown_ref, dbup_ref,
+    far, og, mixed, h, act, gp, hid, gh, hid_got, gh_got, gb, send, recv,
+):
+    rows = og_own_ref.shape[0]
+    tiles = h.shape[0] // TILE
+    other = {"feat": 1 - lax.axis_index("feat")}
+
+    def copy(k, src, dst):
+        return pltpu.make_async_remote_copy(
+            src_ref=src, dst_ref=dst, send_sem=send.at[k], recv_sem=recv.at[k], device_id=other, device_id_type=MESH
+        )
+
+    barrier = pltpu.get_barrier_semaphore()
+    pl.semaphore_signal(barrier, inc=1, device_id=other, device_id_type=MESH)
+    pl.semaphore_wait(barrier, 1)
+    low, high = pl.ds(0, rows), pl.ds(rows, rows)
+    atts = [copy(0, att_ref.at[low], far.at[high]), copy(1, att_ref.at[high], far.at[low])]
+    og_copy = copy(2, og_own_ref, og.at[high])
+    for c in atts:
+        c.start()
+    og_copy.start()
+    og[low, :] = og_own_ref[...]
+    for c in atts:
+        c.wait()
+    mix_tiles(x_ref, att_ref, far, wout_ref, bout_ref, g_ref, s_ref, mixed, h)
+    og_copy.wait()
+
+    def gh_copy(i, tile):
+        return copy(3 + i, gh.at[ds(tile, TILE)], gh_got.at[ds(i, TILE)])
+
+    def hid_copy(i, tile):
+        return copy(3 + tiles + i, hid.at[ds(tile, TILE)], hid_got.at[ds(i, TILE)])
+
+    def send_tile(i, tile):
+        gh_copy(i, tile).start()
+
+        @pl.when(i < tiles // 2)
+        def _():
+            hid_copy(i, tile).start()
+
+    ff_tiles(h, og, up_ref, down_ref, bup_ref, act, gp, hid, gh, dbup_ref, send_tile)
+    ff_weights(n, h, og, act, gp, dup_ref, ddown_ref)
+    for i in range(tiles):
+        gh_copy(i, (i + tiles // 2) % tiles).wait()
+    for i in range(tiles // 2):
+        hid_copy(i, i + tiles // 2).wait()
+    out_back(
+        n, gh, gh_got, mixed, og, hid, hid_got, bdown_ref, g_ref, wout_ref, att_ref, far,
+        gm_ref, gatt_ref, dout_ref, y_ref, vec_ref, gb,
+    )
+
+
 def heads_back(
     qkv_ref, s_ref, m_ref, att_ref, den_ref, gatt_ref, gqkv_ref, pq_ref, pk_ref, gn_ref, gq_ref, gpq_ref, after
 ):
@@ -439,7 +498,7 @@
             gqkv_ref[rows, cols(part)] = jnp.where(mine, value.astype(BF), gqkv_ref[rows, cols(part)])
 
         def step(i, _):
-            rows = ds(i, TILE)
+            rows = ds(i, BTILE)
             k = jnp.where(mine, qkv_ref[rows, cols(1)] * BF(scale), zero)
             v_one = jnp.where(mine, qkv_ref[rows, cols(2)], jnp.ones((), BF))
             q_all = qkv_ref[:, cols(0)]
@@ -447,7 +506,7 @@
             ex = jnp.exp(nt(k, q_all))
             low = nt(pk, pq_ref[...])
             da = nt(v_one, gn_ref[...])
-            per = TILE // BLOCK
+            per = BTILE // BLOCK
             marks = m_ref[h, i]
             probs, dl, gs = [], [], []
             for j in range(per):
@@ -468,7 +527,7 @@
             gq_ref[...] += tn(gs, k)
             return 0
 
-        lax.fori_loop(0, rows_all // TILE, step, 0)
+        lax.fori_loop(0, rows_all // BTILE, step, 0)
 
         def last(i, _):
             rows = ds(i, TILE)
@@ -680,7 +739,6 @@
         return a.reshape(1, -1)
 
     x = jnp.concatenate([layer_input, swap(layer_input)], axis=0)
-    og = jnp.concatenate([out_grad, swap(out_grad)], axis=0)
     signs = (2 * feature_signs - 1).astype(BF)
     own_signs = lax.dynamic_slice_in_dim(signs, f * half_heads, half_heads, 0)
     far_signs = swap(lax.dynamic_slice_in_dim(signs, (1 - f) * half_heads, half_heads, 0))
@@ -701,9 +759,11 @@
     block = (jnp.arange(NB, dtype=jnp.int32) + shift) % NB
     matched = jnp.any(used[..., None] & (lists[..., None] == block), axis=2)
     matched = jnp.where(f == 0, matched, jnp.roll(matched, NB // 2, axis=1)).astype(F32)
-    tiled = (half_heads, tokens // TILE, TILE // BLOCK, tokens)
-    marks = jnp.repeat(matched, BLOCK, axis=2).reshape(tiled)
-    marks_t = jnp.repeat(matched.transpose(0, 2, 1), BLOCK, axis=2).reshape(tiled)
+
+    def spread(a, tile):
+        return jnp.repeat(a, BLOCK, axis=2).reshape(half_heads, tokens // tile, tile // BLOCK, tokens)
+
+    marks, marks_t = spread(matched, ATILE), spread(matched.transpose(0, 2, 1), BTILE)
 
     def own_cols(a):
         return jnp.concatenate(
@@ -720,32 +780,22 @@
         att_body, [((tokens, half_width), BF), ((tokens, half_width), F32)], [qkv, table, marks],
         scratch=[phi, phi], name="att",
     )
-    far = swap(att)
-    att_far = jnp.concatenate([far[rows:], far[:rows]], axis=0)
-    mixed, h2 = call(
-        mix_body, [((tokens, width), F32), ((tokens, width), BF)],
-        [x, att, att_far, w_out, row(b_out), row(ln2_gain), row(ln2_bias)], name="mix",
-    )
-    act, gp, hid, gh2, d_bup = call(
-        ff_body,
-        [((tokens, hidden), BF), ((tokens, hidden), BF), ((tokens, width), BF), ((tokens, width), BF), ((1, hidden), F32)],
-        [h2, og, w_up, w_down, row(b_up)], name="ff",
-    )
-    gh_far = swap(gh2)
-    gh_far = jnp.concatenate([gh_far[rows:], gh_far[:rows]], axis=0)
-    hid_far = swap(hid[rows:])
-    d_up, d_down = call(
-        functools.partial(ffw_body, n), [((n, chunk, hidden), BF), ((n, chunk, hidden), BF)], [h2, og, act, gp],
-        name="ffw",
-    )
-    gm, gatt, d_out, y, vec2 = call(
-        functools.partial(outb_body, n),
+    big, wide = pltpu.VMEM((tokens, width), BF), pltpu.VMEM((tokens, hidden), BF)
+    pair_sems = pltpu.SemaphoreType.DMA((3 + tokens // TILE + rows // TILE,))
+    gm, gatt, d_out, y, vec2, d_up, d_down, d_bup = call(
+        functools.partial(mid_body, n),
         [
-            ((rows, width), F32), ((tokens, half_width), F32), ((n, chunk, half_width), BF),
-            ((rows, width), BF), ((8, width), F32),
+            ((rows, width), F32), ((tokens, half_width), F32), ((n, chunk, half_width), BF), ((rows, width), BF),
+            ((8, width), F32), ((n, chunk, hidden), BF), ((n, chunk, hidden), BF), ((1, hidden), F32),
         ],
-        [gh2, gh_far, mixed, og, hid, hid_far, row(b_down), row(ln2_gain), w_out, att, att_far],
-        scratch=[pltpu.VMEM((tokens, width), BF)], name="outb",
+        [
+            x, att, w_out, row(b_out), row(ln2_gain), row(ln2_bias), out_grad, w_up, w_down, row(b_up), row(b_down),
+        ],
+        scratch=[
+            pltpu.VMEM((tokens, half_width), BF), big, pltpu.VMEM((tokens, width), F32), big, wide, wide, big, big,
+            pltpu.VMEM((rows, width), BF), big, big, pair_sems, pair_sems,
+        ],
+        name="mid", net=2,
     )
     slots = sum(split(n)) + split(n)[0] - 3 + 1
     bufs = []

time: 222 us -> 201 us (0.905)
  Pallas kernels: 191 us -> 177 us
  local copies, waits for them, and re-layouts: 20.9 us -> 16.2 us
    pallas_call x8 -> x5, Pallas kernels: 191 us -> 177 us  [call(): pl.pallas_call(body, out_shape=[jax.ShapeDtypeStruct(s, d) for s, d in ou...]
    slice x3 -> x0, local copies, waits for them, and re-layouts: 3.61 us -> none  [the longest x1 2.06 us: body(): hid_far = swap(hid[rows:])]
    concatenate x2 -> x0, other arithmetic: 2.23 us -> none  [the longest x1 1.24 us: body(): gh_far = jnp.concatenate([gh_far[rows:], gh_far[:rows]], axis=0)]
    unnamed x32 -> x24, local copies, waits for them, and re-layouts: 4.96 us -> 3.96 us
  transfers between devices with their start and end apart: 6 -> 2, of which waited for: 0 -> 0; matrix products, arithmetic and copies ran while one was open for 11% -> 9% of each run, Pallas kernels for 20% -> 0%
where the time goes in v4:
time: 201 us
  Pallas kernels  177 us (88%)
  local copies, waits for them, and re-layouts  16.2 us (8%)
  other arithmetic  5.67 us (3%)
    pallas_call x5, Pallas kernels, call(): pl.pallas_call(body, out_shape=[jax.ShapeDtypeStruct(s, d) for s, d in ou...  177 us
    reshape x7, local copies, waits for them, and re-layouts, row(): return a.reshape(1, -1)  5.47 us
  transfers between devices with their start and end apart: 2, of which 0 were waited for; matrix products, arithmetic and copies ran while one was open for 9% of the time, Pallas kernels for 0%

profile of v4, /device:TPU:0, one launch (start us, length us, event | category | flops | bytes accessed | tf_op | source)
XLA Modules:
  0.0 200.7 jit_solution(16312281622207500072)
XLA Ops:
  0.6 0.0 copy-start
  0.7 0.6 collective-permute-start
  1.2 1.1 add_convert_fusion
  2.3 0.7 constant_dynamic-slice_fusion.2
  2.9 0.0 collective-permute-start.1
  3.0 1.3 reshape.105.g_ref
  4.2 1.3 reshape.106.s_ref
  5.5 0.0 copy-start.8
  5.5 0.0 copy-start.9
  5.5 1.6 constant_dynamic-slice_fusion.5
  7.1 0.0 copy-done.8
  7.1 0.0 copy-start.4
  7.1 0.0 copy-start.5
  7.2 0.0 copy-start.6
  7.2 0.0 copy-start.3
  7.2 0.0 copy-start.7
  7.2 0.1 fusion.7
  7.3 0.0 copy-done
  7.4 0.0 copy-done.9
  7.4 0.2 and_reduce_fusion
  7.6 0.6 fusion.5
  8.2 0.3 broadcast_in_dim.4
  8.5 1.0 reshape_reshape.6.m_ref
  9.5 0.0 copy-done.4
  9.5 0.6 reshape.108.bout_ref
  10.1 0.0 copy-done.5
  10.1 0.6 reshape.109.g_ref
  10.7 0.0 copy-done.6
  10.7 0.6 reshape.110.s_ref
  11.3 0.0 copy-done.3
  11.3 0.6 reshape.111.bup_ref
  11.9 0.0 copy-done.7
  11.9 0.6 reshape.112.bdown_ref
  12.5 0.9 copy.43
  13.4 0.3 broadcast_in_dim.5
  13.6 1.0 reshape_reshape.7.m_ref
  14.6 0.0 copy-start.1
  14.6 1.5 pad_maximum_fusion.w_ref
  16.1 0.6 pad_maximum_fusion.2.b_ref
  16.7 0.0 copy-done.1
  16.7 0.9 constant_dynamic-update-slice_fusion.1
  17.6 0.0 collective-permute-done.1
  17.6 0.9 pad_maximum_fusion.1
  18.6 0.8 fusion.2.s_ref
  19.4 0.0 collective-permute-done
  19.4 0.9 constant_dynamic-update-slice_fusion.x_ref
  20.3 7.0 %qkv.1 = (bf16[1024,768]{1,0:T(8,128)(2,1)}, bf16[1024,1152]{1,0:T(8,128)(2,1)}) custom-call(bf16[1024,768]{1,0:T(8,128)(2,1)} %constant_dynamic-update-slice_fusion.x_ref, bf16[1,768]{1,0:T(2,128)(2,1)} %reshape.105.g_ref, bf16[1,768]{1,0:T(2,128)(2,1)} %reshape.106.s_ref, bf16[768,1152]{1,0:T(8,128)(2,1)} %pad_maximum_fusion.w_ref, ...), custom_call_target="tpu_custom_call" | custom-call | tf_op jit(solution)/shard_map/qkv/pallas_call | solution.py:207
  27.3 25.6 %att.1 = (bf16[1024,384]{1,0:T(8,128)(2,1)}, f32[1024,384]{1,0:T(8,128)}) custom-call(bf16[1024,1152]{1,0:T(8,128)(2,1)} %get-tuple-element.47.qkv_ref, bf16[3,128,512]{2,1,0:T(8,128)(2,1)} %fusion.2.s_ref, f32[6,2,8,1024]{3,2,1,0:T(8,128)} %reshape_reshape.6.m_ref), custom_call_target="tpu_custom_call" | custom-call | tf_op jit(solution)/shard_map/att/pallas_call | solution.py:207
  52.9 36.3 %mid.1 = (f32[512,768]{1,0:T(8,128)}, f32[1024,384]{1,0:T(8,128)}, bf16[16,48,384]{2,1,0:T(8,128)(2,1)}, bf16[512,768]{1,0:T(8,128)(2,1)}, f32[8,768]{1,0:T(8,12...) custom-call(bf16[1024,768]{1,0:T(8,128)(2,1)} %constant_dynamic-update-slice_fusion.x_ref, ...), custom_call_target="tpu_custom_call" | custom-call | tf_op jit(solution)/shard_map/mid/pallas_call | solution.py:207
  89.2 104.9 %back.1 = (f32[512,768]{1,0:T(8,128)}, f32[48,1536]{1,0:T(8,128)}, f32[48,1536]{1,0:T(8,128)}, f32[24,768]{1,0:T(8,128)}, f32[24,2304]{1,0:T(8,128)}, /*index=5*...) custom-call(bf16[1024,1152]{1,0:T(8,128)(2,1)} %get-tuple-element.47.qkv_ref, bf16[3,128,512]{2,1,0:T(8,128)(2,1)} %fusion.2.s_ref, ...), custom_call_target="tpu_custom_call" | custom-call | tf_op jit(solution)/shard_map/back/pallas_call | solution.py:207
  194.1 0.0 copy-start.2
  194.1 3.5 %emit.1 = (f32[512,768]{1,0:T(8,128)}, f32[48,1536]{1,0:T(8,128)}, f32[1536,48]{1,0:T(8,128)}, f32[24,768]{1,0:T(8,128)}, f32[24,2304]{1,0:T(8,128)}, /*index=5*...) custom-call(f32[512,768]{1,0:T(8,128)} %get-tuple-element.59.dx_ref,, ...), custom_call_target="tpu_custom_call" | custom-call | tf_op jit(solution)/shard_map/emit/pallas_call | solution.py:207
  197.7 2.1 %copy.44 = f32[1536,48]{0,1:T(8,128)} copy(f32[1536,48]{1,0:T(8,128)} %get-tuple-element.120) | data formatting | bytes 589824
  199.8 0.0 copy-done.2
  199.8 0.9 copy.52
  (10 shorter events, 0.1 us)
Async XLA Ops:
  0.6 6.7 %copy-start = (s32[1,12,16,4]{2,3,1,0:T(4,128)S(1)}, s32[1,12,16,4]{2,3,1,0:T(4,128)}, u32[]{:S(2)}) copy-start(s32[1,12,16,4]{2,3,1,0:T(4,128)} %param.31) | copy-start | bytes 9220
  0.7 18.7 %collective-permute-start = (bf16[512,768]{1,0:T(8,128)(2,1)}, bf16[512,768]{1,0:T(8,128)(2,1)S(1)}, u32[]{:S(2)}, u32[]{:S(2)}) collective-permute-start(bf16[512,768]{1,0:T(8,128)(2,1)} %x_ref.1), channel_id=1, source_target_pairs={{0,1},{1,0},{2,3},{3,2},{4,5},{5,4},{6,7},{7,6},{8,9},{9,8},{10,11... | collective-permute-start | bytes 2359304 | tf_op jit(solution)/shard_map/ppermute | solution.py:736
  2.9 14.7 %collective-permute-start.1 = (bf16[6,64,128]{2,1,0:T(8,128)(2,1)}, bf16[6,64,128]{2,1,0:T(8,128)(2,1)}, u32[]{:S(2)}, u32[]{:S(2)}) collective-permute-start(bf16[6,64,128]{2,1,0:T(8,128)(2,1)} %get-tuple-element.128), channel_id=1, source_target_pairs={{0,1},{1,0},{2,3},{3,2},{4,5},{5,4},{6,7},{7,6},{8,9},{9,8},{10,11... | collective-permute-start | bytes 294920 | tf_op jit(solution)/shard_map/ppermute | solution.py:736
  5.5 1.6 copy-start.8
  5.5 1.9 copy-start.9
  7.1 2.4 %copy-start.4 = (bf16[768]{0:T(1024)(128)(2,1)S(1)}, bf16[768]{0:T(1024)(128)(2,1)}, u32[]{:S(2)}) copy-start(bf16[768]{0:T(1024)(128)(2,1)} %param.23) | copy-start | bytes 4612
  7.1 3.0 %copy-start.5 = (bf16[768]{0:T(1024)(128)(2,1)S(1)}, bf16[768]{0:T(1024)(128)(2,1)}, u32[]{:S(2)}) copy-start(bf16[768]{0:T(1024)(128)(2,1)} %param.24) | copy-start | bytes 4612
  7.2 3.5 %copy-start.6 = (bf16[768]{0:T(1024)(128)(2,1)S(1)}, bf16[768]{0:T(1024)(128)(2,1)}, u32[]{:S(2)}) copy-start(bf16[768]{0:T(1024)(128)(2,1)} %param.25) | copy-start | bytes 4612
  7.2 4.1 %copy-start.3 = (bf16[1536]{0:T(1024)(128)(2,1)S(1)}, bf16[1536]{0:T(1024)(128)(2,1)}, u32[]{:S(2)}) copy-start(bf16[1536]{0:T(1024)(128)(2,1)} %param.27) | copy-start | bytes 9220
  7.2 4.7 %copy-start.7 = (bf16[768]{0:T(1024)(128)(2,1)S(1)}, bf16[768]{0:T(1024)(128)(2,1)}, u32[]{:S(2)}) copy-start(bf16[768]{0:T(1024)(128)(2,1)} %param.29) | copy-start | bytes 4612
  14.6 2.1 %copy-start.1 = (bf16[512,768]{1,0:T(8,128)(2,1)S(1)}, bf16[512,768]{1,0:T(8,128)(2,1)}, u32[]{:S(2)}) copy-start(bf16[512,768]{1,0:T(8,128)(2,1)} %x_ref.1) | copy-start | bytes 2359300
  194.1 5.6 %copy-start.2 = (bf16[512,768]{1,0:T(8,128)(2,1)S(1)}, bf16[512,768]{1,0:T(8,128)(2,1)}, u32[]{:S(2)}) copy-start(bf16[512,768]{1,0:T(8,128)(2,1)} %get-tuple-element.150) | copy-start | bytes 2359300

commit v5 on v4

--- a/solution.py
+++ b/solution.py
@@ -21,6 +21,7 @@
 BTILE = 512
 GELU_A = math.sqrt(2.0 / math.pi)
 GELU_B = 0.044715
+GAIN1, BIAS1, BOUT, GAIN2, BIAS2, BDOWN, BQKV, BUP = 0, 1, 2, 3, 4, 5, 6, 9
 MESH = pl.DeviceIdType.MESH
 VMEM = pl.BlockSpec(memory_space=pltpu.VMEM)
 ANY = pl.BlockSpec(memory_space=pl.ANY)
@@ -217,10 +218,12 @@
     )(*ins)
 
 
-def qkv_body(x_ref, g_ref, s_ref, w_ref, b_ref, h_ref, qkv_ref):
-    gain = g_ref[...].astype(F32)
-    shift = s_ref[...].astype(F32)
-    bias = b_ref[...].astype(F32)
+def qkv_tiles(first, last, x_ref, p_ref, w_ref, h_ref, qkv_ref):
+    width = x_ref.shape[1]
+    f = lax.axis_index("feat")
+    gain = p_ref[GAIN1 : GAIN1 + 1, :]
+    shift = p_ref[BIAS1 : BIAS1 + 1, :]
+    bias = jnp.concatenate([p_ref[BQKV + i : BQKV + i + 1, ds(f, width // 2)] for i in range(3)], axis=1)
 
     def step(i, _):
         rows = ds(i, TILE)
@@ -230,7 +233,88 @@
         qkv_ref[rows, :] = (nn(h, w_ref[...]) + bias).astype(BF)
         return 0
 
-    lax.fori_loop(0, x_ref.shape[0] // TILE, step, 0)
+    lax.fori_loop(first, last, step, 0)
+
+
+def matches(list_ref, count_ref, h):
+    at = lax.axis_index("feat") * (HEADS // 2) + h
+    lists, count = list_ref[0, at], count_ref[0, pl.ds(at, 1), :]
+    block = lax.broadcasted_iota(jnp.int32, (NB, NB), 0)
+    found = jnp.zeros((NB, NB), F32)
+    for j in range(lists.shape[0]):
+        found = jnp.where((lists[j : j + 1] == block) & (count > j), 1.0, found)
+    return found.astype(BF)
+
+
+def fill_spread(e_ref):
+    shift = lax.axis_index("feat") * (NB // 2)
+    block = lax.broadcasted_iota(jnp.int32, e_ref.shape, 0)
+    token = lax.broadcasted_iota(jnp.int32, e_ref.shape, 1)
+    start = lax.rem(block + shift, NB) * BLOCK
+    e_ref[...] = jnp.where((token >= start) & (token < start + BLOCK), 1.0, 0.0).astype(BF)
+
+
+def local_marks(mk_ref, i, tile):
+    assert tile * 2 == SEQLEN
+    return mk_ref[ds(lax.rem(i + lax.axis_index("feat"), 2), tile // BLOCK), :]
+
+
+def front_body(
+    x_own_ref, w_all_ref, fs_ref, list_ref, count_ref, g1, b1, bo, g2, b2, bd, bqkv, bup,
+    p_ref, x_ref, h_ref, qkv_ref, table_ref, w_ref, att_ref, den_ref, s_send, s_got, e_ref, mk_ref, pq_ref, pk_ref, send, recv, local,
+):
+    rows, width = x_own_ref.shape
+    own = width // 2
+    f = lax.axis_index("feat")
+    other = {"feat": 1 - f}
+
+    def copy(k, src, dst):
+        return pltpu.make_async_remote_copy(
+            src_ref=src, dst_ref=dst, send_sem=send.at[k], recv_sem=recv.at[k], device_id=other, device_id_type=MESH
+        )
+
+    loads = [
+        pltpu.make_async_copy(w_all_ref.at[:, ds(2 * i + f, own)], w_ref.at[:, pl.ds(i * own, own)], local.at[i])
+        for i in range(3)
+    ]
+    for c in loads:
+        c.start()
+    barrier = pltpu.get_barrier_semaphore()
+    pl.semaphore_signal(barrier, inc=1, device_id=other, device_id_type=MESH)
+    pl.semaphore_wait(barrier, 1)
+    x_copy = copy(0, x_own_ref, x_ref.at[pl.ds(rows, rows)])
+    x_copy.start()
+    heads, dim, feats = s_send.shape
+    line = 0
+    for vector in (g1, b1, bo, g2, b2, bd, bqkv, bup):
+        for i in range(vector.shape[0] // width):
+            p_ref[line : line + 1, :] = vector[i * width : (i + 1) * width].astype(F32).reshape(1, width)
+            line += 1
+
+    def sign(i):
+        return (2.0 * fs_ref[i].astype(F32) - 1.0).astype(BF)
+
+    for i in range(heads):
+        s_send[i] = sign((1 - f) * heads + i)
+    s_copy = copy(1, s_send, s_got)
+    s_copy.start()
+    x_ref[0:rows, :] = x_own_ref[...]
+    table_ref[...] = jnp.zeros_like(table_ref)
+    for i in range(heads):
+        e = i % 2
+        table_ref[i // 2, e * dim : (e + 1) * dim, 2 * e * feats : (2 * e + 1) * feats] = sign(f * heads + i)
+    fill_spread(e_ref)
+    for c in loads:
+        c.wait()
+    tiles = rows // TILE
+    qkv_tiles(0, tiles, x_ref, p_ref, w_ref, h_ref, qkv_ref)
+    s_copy.wait()
+    for i in range(heads):
+        e = i % 2
+        table_ref[i // 2, e * dim : (e + 1) * dim, (2 * e + 1) * feats : (2 * e + 2) * feats] = s_got[i]
+    x_copy.wait()
+    qkv_tiles(tiles, 2 * tiles, x_ref, p_ref, w_ref, h_ref, qkv_ref)
+    att_heads(qkv_ref, table_ref, list_ref, count_ref, e_ref, mk_ref, att_ref, den_ref, pq_ref, pk_ref)
 
 
 def head_parts(qkv_ref, h):
@@ -263,9 +347,10 @@
     lax.fori_loop(0, qkv_ref.shape[0] // TILE, step, 0)
 
 
-def att_body(qkv_ref, s_ref, m_ref, att_ref, den_ref, pq_ref, pk_ref):
+def att_heads(qkv_ref, s_ref, list_ref, count_ref, e_ref, mk_ref, att_ref, den_ref, pq_ref, pk_ref):
     def head(h, _):
         p, e, lane, mine, cols = head_parts(qkv_ref, h)
+        mk_ref[...] = tn(matches(list_ref, count_ref, h), e_ref[...])
         lift_all(qkv_ref, s_ref, h, pq_ref, pk_ref)
         zero = jnp.zeros((), BF)
         v_one = jnp.where(mine, qkv_ref[:, cols(2)], jnp.ones((), BF))
@@ -276,7 +361,7 @@
             ex = jnp.exp(nt(q, qkv_ref[:, cols(1)]))
             low = nt(pq_ref[rows, :], pk_ref[...])
             per = ATILE // BLOCK
-            marks = m_ref[h, i]
+            marks = local_marks(mk_ref, i, ATILE)
             probs = jnp.concatenate(
                 [
                     jnp.where(
@@ -322,14 +407,14 @@
     lax.fori_loop(0, x_ref.shape[0] // TILE, step, 0)
 
 
-def ff_tiles(h_ref, og_ref, up_ref, down_ref, b_ref, act_ref, gp_ref, hid_ref, gh_ref, db_ref, send):
+def ff_tiles(h_ref, og_ref, up_ref, down_ref, bias, act_ref, gp_ref, hid_ref, gh_ref, db_ref, send):
     tiles = h_ref.shape[0] // TILE
     db_ref[...] = jnp.zeros_like(db_ref)
 
     def step(i, _):
         tile = lax.rem(i + tiles // 2, tiles)
         rows = ds(tile, TILE)
-        v = nn(h_ref[rows, :], up_ref[...]) + b_ref[...].astype(F32)
+        v = nn(h_ref[rows, :], up_ref[...]) + bias
         vv = v * v
         th = jnp.tanh(GELU_A * v * (1.0 + GELU_B * vv))
         half = 0.5 + 0.5 * th
@@ -354,15 +439,12 @@
         out_ref[net.place(first + i)] = value[i * rows : (i + 1) * rows].astype(BF)
 
 
-def ff_weights(n, h_ref, og_ref, act_ref, gp_ref, up_ref, down_ref):
-    net = Net(n)
-    wide = h_ref.shape[1] // 2
-    per = wide // up_ref.shape[1]
+def ff_weight(net, lhs_ref, rhs_ref, out_ref):
+    wide = lhs_ref.shape[1] // 2
+    per = wide // out_ref.shape[1]
 
     def step(i, _):
-        rows = ds(i, wide)
-        put_chunks(up_ref, i * per, tn(h_ref[:, rows], gp_ref[...]), net)
-        put_chunks(down_ref, i * per, tn(og_ref[:, rows], act_ref[...]), net)
+        put_chunks(out_ref, i * per, tn(lhs_ref[:, ds(i, wide)], rhs_ref[...]), net)
         return 0
 
     lax.fori_loop(0, 2, step, 0)
@@ -410,10 +492,14 @@
 
 
 def mid_body(
-    n, x_ref, att_ref, wout_ref, bout_ref, g_ref, s_ref, og_own_ref, up_ref, down_ref, bup_ref, bdown_ref,
+    n, x_ref, att_ref, wout_ref, p_ref, og_own_ref, up_ref, down_ref,
     gm_ref, gatt_ref, dout_ref, y_ref, vec_ref, dup_ref, ddown_ref, dbup_ref,
-    far, og, mixed, h, act, gp, hid, gh, hid_got, gh_got, gb, send, recv,
+    far, og, mixed, h, act, gp, hid, gh, hid_got, gh_got, gb, ddown, ddown_got, send, recv, down_send, down_recv,
 ):
+    net = Net(n)
+    down = Scatter(net, ddown, [ddown_got, ddown_ref, None, None, None], down_send, down_recv)
+    bout_ref, g_ref, s_ref, bdown_ref = [p_ref.at[i : i + 1] for i in (BOUT, GAIN2, BIAS2, BDOWN)]
+    bup = jnp.concatenate([p_ref[i : i + 1, :] for i in range(BUP, p_ref.shape[0])], axis=1)
     rows = og_own_ref.shape[0]
     tiles = h.shape[0] // TILE
     other = {"feat": 1 - lax.axis_index("feat")}
@@ -423,9 +509,7 @@
             src_ref=src, dst_ref=dst, send_sem=send.at[k], recv_sem=recv.at[k], device_id=other, device_id_type=MESH
         )
 
-    barrier = pltpu.get_barrier_semaphore()
-    pl.semaphore_signal(barrier, inc=1, device_id=other, device_id_type=MESH)
-    pl.semaphore_wait(barrier, 1)
+    net.barrier()
     low, high = pl.ds(0, rows), pl.ds(rows, rows)
     atts = [copy(0, att_ref.at[low], far.at[high]), copy(1, att_ref.at[high], far.at[low])]
     og_copy = copy(2, og_own_ref, og.at[high])
@@ -451,8 +535,10 @@
         def _():
             hid_copy(i, tile).start()
 
-    ff_tiles(h, og, up_ref, down_ref, bup_ref, act, gp, hid, gh, dbup_ref, send_tile)
-    ff_weights(n, h, og, act, gp, dup_ref, ddown_ref)
+    ff_tiles(h, og, up_ref, down_ref, bup, act, gp, hid, gh, dbup_ref, send_tile)
+    ff_weight(net, og, act, ddown)
+    down.start(0)
+    ff_weight(net, h, gp, dup_ref)
     for i in range(tiles):
         gh_copy(i, (i + tiles // 2) % tiles).wait()
     for i in range(tiles // 2):
@@ -461,10 +547,11 @@
         n, gh, gh_got, mixed, og, hid, hid_got, bdown_ref, g_ref, wout_ref, att_ref, far,
         gm_ref, gatt_ref, dout_ref, y_ref, vec_ref, gb,
     )
+    down.finish(0)
 
 
 def heads_back(
-    qkv_ref, s_ref, m_ref, att_ref, den_ref, gatt_ref, gqkv_ref, pq_ref, pk_ref, gn_ref, gq_ref, gpq_ref, after
+    qkv_ref, s_ref, list_ref, count_ref, e_ref, mk_ref, att_ref, den_ref, gatt_ref, gqkv_ref, pq_ref, pk_ref, gn_ref, gq_ref, gpq_ref, after
 ):
     rows_all = qkv_ref.shape[0]
     scale = HEAD_DIM ** (-0.5)
@@ -473,6 +560,7 @@
         p, e, lane, mine, cols = head_parts(qkv_ref, h)
         feats = pq_ref.shape[1]
         zero = jnp.zeros((), BF)
+        mk_ref[...] = nn(matches(list_ref, count_ref, h), e_ref[...])
         lift_all(qkv_ref, s_ref, h, pq_ref, pk_ref)
         first_other = (1 - e) * HEAD_DIM
 
@@ -507,7 +595,7 @@
             low = nt(pk, pq_ref[...])
             da = nt(v_one, gn_ref[...])
             per = BTILE // BLOCK
-            marks = m_ref[h, i]
+            marks = local_marks(mk_ref, i, BTILE)
             probs, dl, gs = [], [], []
             for j in range(per):
                 part = slice(j * BLOCK, (j + 1) * BLOCK)
@@ -544,17 +632,17 @@
 
 
 def back_body(
-    n, qkv_ref, s_ref, m_ref, att_ref, den_ref, gatt_ref, h_ref, w_ref, x_ref, g_ref, gm_ref, up_ref, down_ref, out_ref,
+    n, qkv_ref, s_ref, list_ref, count_ref, att_ref, den_ref, gatt_ref, h_ref, w_ref, x_ref, p_ref, gm_ref, up_ref, down_ref, out_ref,
     vec_ref, bup_ref, dx_ref, oup_ref, odown_ref, oout_ref, oqkv_ref, orows_ref, obqkv_ref, obup_ref, *scratch,
 ):
     net = Net(n)
-    bufs, tail = scratch[:30], scratch[30:]
-    pq, pk, gn, gq, gpq, gqkv, gw, gh_send, gh_got, sout, rout, sqkv, rqkv, vrows, vbqkv, vbup, send, recv = tail
+    bufs, tail = (None, down_ref) + scratch[:28], scratch[28:]
+    e_ref, mk_ref, pq, pk, gn, gq, gpq, gqkv, gw, gh_send, gh_got, sout, rout, sqkv, rqkv, vrows, vbqkv, vbup, send, recv = tail
     f = net.f
     other = {"feat": 1 - f}
     parts = [
         Scatter(net, src, bufs[5 * i : 5 * i + 5], send.at[i], recv.at[i])
-        for i, src in enumerate((down_ref, up_ref, out_ref, gw.at[0], gw.at[1], gw.at[2]))
+        for i, src in enumerate((None, up_ref, out_ref, gw.at[0], gw.at[1], gw.at[2]))
     ]
     down, up, out = parts[:3]
     pairs = parts[3:]
@@ -595,30 +683,32 @@
             put_chunks(gw.at[p], i * per, tn(h_ref[:, i * own : (i + 1) * own], g), net)
         pairs[p].start(0)
 
+    fill_spread(e_ref)
     net.barrier()
-    for part in (down, up, out):
-        part.start(0)
+    down.start(1)
+    up.start(0)
+    out.start(0)
 
     def after1():
-        move(down, 0)
+        move(down, 1)
         weight(0)
 
     def after2():
         move(up, 0)
         move(out, 0)
+        move(pairs[0], 0)
 
     def after3():
-        move(down, 1)
-        move(pairs[0], 0)
-        weight(1)
-
-    def after4():
         move(up, 1)
         move(out, 1)
+        weight(1)
+
+    def after4():
+        down.finish(2, whole(odown_ref))
         move(pairs[0], 1)
 
     heads_back(
-        qkv_ref, s_ref, m_ref, att_ref, den_ref, gatt_ref, gqkv, pq, pk, gn, gq, gpq,
+        qkv_ref, s_ref, list_ref, count_ref, e_ref, mk_ref, att_ref, den_ref, gatt_ref, gqkv, pq, pk, gn, gq, gpq,
         {1: after1, 2: after2, 3: after3, 4: after4},
     )
     weight(2)
@@ -642,7 +732,6 @@
     for i in range(3):
         vbqkv[0, :, ds(2 * i + f, own)] = total[:, i * own : (i + 1) * own]
     vbup[0] = bup_ref[...]
-    down.finish(2, whole(odown_ref))
     out.finish(2, halves(sout))
     out_swap = swap(2, sout.at[1 - f], rout)
     out_swap.start()
@@ -650,7 +739,7 @@
     move(pairs[1], 1)
     move(pairs[2], 0)
     gh_swap.wait()
-    gain = g_ref[...].astype(F32)
+    gain = p_ref[GAIN1 : GAIN1 + 1, :]
     vrows[0] = vec_ref[...]
 
     def norm1(i, _):
@@ -707,14 +796,15 @@
     obqkv_ref[...] = cut(bqkv, bqkv.shape[1] // (2 * n), where, bqkv.shape[1])
 
 
-def emit_body(dx_ref, up_ref, down_ref, out_ref, qkv_ref, rows_ref, bqkv_ref, bup_ref, *outs):
-    odx, oup, odown, oout, oqkv, obqkv, obup = outs[:7]
+def emit_body(y_ref, dx_ref, up_ref, down_ref, out_ref, qkv_ref, rows_ref, bqkv_ref, bup_ref, *outs):
+    oy, odx, oup, odown, oout, oqkv, obqkv, obup = outs[:8]
+    oy[...] = y_ref[...]
     odx[...], oup[...], oout[...], oqkv[...] = dx_ref[...], up_ref[...], out_ref[...], qkv_ref[...]
     down = down_ref[...]
     odown[...] = down if odown.shape == down.shape else down.T
     obqkv[...] = bqkv_ref[:, : obqkv.shape[1]]
     obup[...] = bup_ref[:, : obup.shape[1]]
-    for i, ref in enumerate(outs[7:]):
+    for i, ref in enumerate(outs[8:]):
         ref[...] = rows_ref[i : i + 1, : ref.shape[1]]
 
 
@@ -732,74 +822,50 @@
     chunk = width // n
     assert lax.axis_size("feat") == 2 and match_blocks.shape[0] == 1 and tokens == SEQLEN
 
-    def swap(a):
-        return lax.ppermute(a, "feat", [(0, 1), (1, 0)])
-
-    def row(a):
-        return a.reshape(1, -1)
-
-    x = jnp.concatenate([layer_input, swap(layer_input)], axis=0)
-    signs = (2 * feature_signs - 1).astype(BF)
-    own_signs = lax.dynamic_slice_in_dim(signs, f * half_heads, half_heads, 0)
-    far_signs = swap(lax.dynamic_slice_in_dim(signs, (1 - f) * half_heads, half_heads, 0))
-    signs = jnp.concatenate([own_signs, far_signs], axis=2)
-    feats = signs.shape[2]
-    pairs = signs.reshape(half_heads // 2, 2, HEAD_DIM, feats)
-    table = jnp.concatenate(
+    lists = match_blocks.transpose(0, 1, 3, 2)
+    vectors = [ln1_gain, ln1_bias, b_out, ln2_gain, ln2_bias, b_down, b_qkv, b_up]
+    lines = sum(a.shape[0] for a in vectors) // width
+    feats = 2 * feature_signs.shape[2]
+    phi = pltpu.VMEM((tokens, feats), BF)
+    masks = [pltpu.VMEM((NB, tokens), BF), pltpu.VMEM((NB, tokens), F32)]
+    sign_half = pltpu.VMEM((half_heads, HEAD_DIM, feats // 2), BF)
+    two = pltpu.SemaphoreType.DMA((2,))
+    params, x, h1, qkv, table, w_own, att, den = call(
+        front_body,
         [
-            jnp.pad(pairs[:, 0], ((0, 0), (0, HEAD_DIM), (0, 0))),
-            jnp.pad(pairs[:, 1], ((0, 0), (HEAD_DIM, 0), (0, 0))),
+            ((lines, width), F32),
+            ((tokens, width), BF), ((tokens, width), BF), ((tokens, 3 * half_width), BF),
+            ((half_heads // 2, 2 * HEAD_DIM, 2 * feats), BF), ((width, 3 * half_width), BF),
+            ((tokens, half_width), BF), ((tokens, half_width), F32),
         ],
-        axis=2,
-    )
-    lists = lax.dynamic_slice_in_dim(match_blocks[0], f * half_heads, half_heads, 0)
-    counts = lax.dynamic_slice_in_dim(match_count[0], f * half_heads, half_heads, 0)
-    used = jnp.arange(lists.shape[2], dtype=jnp.int32) < counts[..., None]
-    shift = f * (NB // 2)
-    block = (jnp.arange(NB, dtype=jnp.int32) + shift) % NB
-    matched = jnp.any(used[..., None] & (lists[..., None] == block), axis=2)
-    matched = jnp.where(f == 0, matched, jnp.roll(matched, NB // 2, axis=1)).astype(F32)
-
-    def spread(a, tile):
-        return jnp.repeat(a, BLOCK, axis=2).reshape(half_heads, tokens // tile, tile // BLOCK, tokens)
-
-    marks, marks_t = spread(matched, ATILE), spread(matched.transpose(0, 2, 1), BTILE)
-
-    def own_cols(a):
-        return jnp.concatenate(
-            [lax.dynamic_slice_in_dim(a, i * width + f * half_width, half_width, 1) for i in range(3)], axis=1
-        )
-
-    w_own, b_own = own_cols(w_qkv), own_cols(row(b_qkv))
-    h1, qkv = call(
-        qkv_body, [((tokens, width), BF), ((tokens, 3 * half_width), BF)],
-        [x, row(ln1_gain), row(ln1_bias), w_own, b_own], name="qkv",
-    )
-    phi = pltpu.VMEM((tokens, feats), BF)
-    att, den = call(
-        att_body, [((tokens, half_width), BF), ((tokens, half_width), F32)], [qkv, table, marks],
-        scratch=[phi, phi], name="att",
+        [layer_input, w_qkv, feature_signs, lists, match_count] + vectors,
+        specs=[VMEM, ANY] + [VMEM] * (3 + len(vectors)),
+        scratch=[sign_half, sign_half] + masks + [phi, phi, two, two, pltpu.SemaphoreType.DMA((3,))],
+        name="front", net=3,
     )
     big, wide = pltpu.VMEM((tokens, width), BF), pltpu.VMEM((tokens, hidden), BF)
+    down_bufs = scatter_bufs(n, chunk, hidden)
+    down_sems = pltpu.SemaphoreType.DMA((split(n)[0] - 1,))
     pair_sems = pltpu.SemaphoreType.DMA((3 + tokens // TILE + rows // TILE,))
     gm, gatt, d_out, y, vec2, d_up, d_down, d_bup = call(
         functools.partial(mid_body, n),
         [
             ((rows, width), F32), ((tokens, half_width), F32), ((n, chunk, half_width), BF), ((rows, width), BF),
-            ((8, width), F32), ((n, chunk, hidden), BF), ((n, chunk, hidden), BF), ((1, hidden), F32),
+            ((8, width), F32), ((n, chunk, hidden), BF), (down_bufs[1].shape, BF), ((1, hidden), F32),
         ],
         [
-            x, att, w_out, row(b_out), row(ln2_gain), row(ln2_bias), out_grad, w_up, w_down, row(b_up), row(b_down),
+            x, att, w_out, params, out_grad, w_up, w_down,
         ],
         scratch=[
             pltpu.VMEM((tokens, half_width), BF), big, pltpu.VMEM((tokens, width), F32), big, wide, wide, big, big,
-            pltpu.VMEM((rows, width), BF), big, big, pair_sems, pair_sems,
+            pltpu.VMEM((rows, width), BF), big, big, pltpu.VMEM((n, chunk, hidden), BF), down_bufs[0],
+            pair_sems, pair_sems, down_sems, down_sems,
         ],
         name="mid", net=2,
     )
     slots = sum(split(n)) + split(n)[0] - 3 + 1
-    bufs = []
-    for cols in (hidden, hidden, half_width, half_width, half_width, half_width):
+    bufs = down_bufs[2:]
+    for cols in (hidden, half_width, half_width, half_width, half_width):
         bufs += scatter_bufs(n, chunk, cols)
     half_chunk = chunk // 2
     sems = pltpu.SemaphoreType.DMA((10, slots))
@@ -810,9 +876,9 @@
             ((half_chunk, 3 * width), F32), ((8, 128), F32), ((1, 128), F32), ((1, 128), F32),
         ],
         [
-            qkv, table, marks_t, att, den, gatt, h1, w_own, layer_input, row(ln1_gain), gm, d_up, d_down, d_out, vec2, d_bup,
+            qkv, table, lists, match_count, att, den, gatt, h1, w_own, layer_input, params, gm, d_up, d_down, d_out, vec2, d_bup,
         ],
-        scratch=bufs + [
+        scratch=bufs + masks + [
             phi, phi, pltpu.VMEM((tokens, 128), BF), pltpu.VMEM((tokens, 128), F32), pltpu.VMEM((tokens, feats), F32),
             pltpu.VMEM((tokens, 3 * half_width), BF), pltpu.VMEM((3, n, chunk, half_width), BF),
             pltpu.VMEM((rows, width), BF), pltpu.VMEM((rows, width), BF),
@@ -824,14 +890,15 @@
         name="back", net=1,
     )
     own = width // (2 * n)
-    turn = chunk % 8 == 0
-    dx, up, down, out, full, d_b, d_bup, *vec = call(
+    turn = False
+    y, dx, up, down, out, full, d_b, d_bup, *vec = call(
         emit_body,
         [
+            ((rows, width), BF),
             ((rows, width), F32), ((chunk, hidden), F32), ((hidden, chunk) if turn else (chunk, hidden), F32),
             ((half_chunk, width), F32), ((half_chunk, 3 * width), F32), ((1, 3 * own), F32), ((1, hidden // n), F32),
         ] + [((1, own), F32)] * 6,
-        sums, name="emit",
+        [y] + list(sums), name="emit",
     )
     vec = [v.reshape(-1) for v in vec]
     return (

time: 201 us -> 171 us (0.85)
  local copies, waits for them, and re-layouts: 16.2 us -> 1.29 us
  Pallas kernels: 177 us -> 169 us
  other arithmetic: 5.67 us -> 0 us
    pallas_call x5 -> x4, Pallas kernels: 177 us -> 169 us  [call(): pl.pallas_call(body, out_shape=[jax.ShapeDtypeStruct(s, d) for s, d in ou...]
    reshape x7 -> x0, local copies, waits for them, and re-layouts: 5.47 us -> none  [row(): return a.reshape(1, -1)]
    concatenate x4 -> x0, other arithmetic: 3.79 us -> none  [the longest x2 2.05 us: own_cols(): jnp.concatenate([lax.dynamic_slice_in_dim(a, i * width + f * half_width,...]
    unnamed x24 -> x1, local copies, waits for them, and re-layouts: 3.96 us -> 1.29 us
    dynamic_slice x6 -> x0, local copies, waits for them, and re-layouts: 2.31 us -> none  [the longest x4 1.64 us: own_cols(): lax.dynamic_slice_in_dim(a, i * width + f * half_width, half_width, 1)]
    another operation x3 -> x0, local copies, waits for them, and re-layouts: 2.13 us -> none  [the longest x2 2.02 us: spread(): jnp.repeat(a, BLOCK, axis=2)]
  transfers between devices with their start and end apart: 2 -> 0, of which waited for: 0 -> 0; matrix products, arithmetic and copies ran while one was open for 9% -> 0% of each run, Pallas kernels for 0% -> 0%
where the time goes in v5:
time: 171 us
  Pallas kernels  169 us (99%)
    pallas_call x4, Pallas kernels, call(): pl.pallas_call(body, out_shape=[jax.ShapeDtypeStruct(s, d) for s, d in ou...  169 us

profile of v5, /device:TPU:0, one launch (start us, length us, event | category | flops | bytes accessed | tf_op | source)
XLA Modules:
  0.0 171.0 jit_solution(3603452691777088647)
XLA Ops:
  0.6 1.3 copy.31.count_ref
  1.9 33.6 %front.1 = (f32[11,768]{1,0:T(8,128)}, bf16[1024,768]{1,0:T(8,128)(2,1)}, bf16[1024,768]{1,0:T(8,128)(2,1)}, bf16[1024,1152]{1,0:T(8,128)(2,1)}, bf16[3,128,512]...) custom-call(bf16[512,768]{1,0:T(8,128)(2,1)} %x_ref.1, ...), custom_call_target="tpu_custom_call" | custom-call | tf_op jit(solution)/shard_map/front/pallas_call | solution.py:208
  35.5 47.9 %mid.1 = (f32[512,768]{1,0:T(8,128)}, f32[1024,384]{1,0:T(8,128)}, bf16[16,48,384]{2,1,0:T(8,128)(2,1)}, bf16[512,768]{1,0:T(8,128)(2,1)}, f32[8,768]{1,0:T(8,12...) custom-call(bf16[1024,768]{1,0:T(8,128)(2,1)} %get-tuple-element.52.x_ref, ...), custom_call_target="tpu_custom_call" | custom-call | tf_op jit(solution)/shard_map/mid/pallas_call | solution.py:208
  83.4 83.7 %back.1 = (f32[512,768]{1,0:T(8,128)}, f32[48,1536]{1,0:T(8,128)}, f32[48,1536]{1,0:T(8,128)}, f32[24,768]{1,0:T(8,128)}, f32[24,2304]{1,0:T(8,128)}, /*index=5*...) custom-call(bf16[1024,1152]{1,0:T(8,128)(2,1)} %get-tuple-element.56.qkv_ref, ...), custom_call_target="tpu_custom_call" | custom-call | tf_op jit(solution)/shard_map/back/pallas_call | solution.py:208
  167.1 3.7 %emit.1 = (bf16[512,768]{1,0:T(8,128)(2,1)}, f32[512,768]{1,0:T(8,128)}, f32[48,1536]{1,0:T(8,128)}, f32[48,1536]{1,0:T(8,128)}, f32[24,768]{1,0:T(8,128)}, /*in...) custom-call(bf16[512,768]{1,0:T(8,128)(2,1)} %get-tuple-element.55.y, ...), custom_call_target="tpu_custom_call" | custom-call | tf_op jit(solution)/shard_map/emit/pallas_call | solution.py:208

commit v6 on v5

--- a/solution.py
+++ b/solution.py
@@ -21,6 +21,7 @@
 BTILE = 512
 GELU_A = math.sqrt(2.0 / math.pi)
 GELU_B = 0.044715
+LOG2E = math.log2(math.e)
 GAIN1, BIAS1, BOUT, GAIN2, BIAS2, BDOWN, BQKV, BUP = 0, 1, 2, 3, 4, 5, 6, 9
 MESH = pl.DeviceIdType.MESH
 VMEM = pl.BlockSpec(memory_space=pltpu.VMEM)
@@ -204,12 +205,12 @@
         return total
 
 
-def call(body, outs, ins, specs=None, scratch=(), name=None, net=None):
+def call(body, outs, ins, specs=None, out_specs=None, scratch=(), name=None, net=None):
     return pl.pallas_call(
         body,
         out_shape=[jax.ShapeDtypeStruct(s, d) for s, d in outs],
         in_specs=specs or [VMEM] * len(ins),
-        out_specs=[VMEM] * len(outs),
+        out_specs=out_specs or [VMEM] * len(outs),
         scratch_shapes=list(scratch),
         compiler_params=pltpu.CompilerParams(
             vmem_limit_bytes=64000 * 1024, collective_id=net, has_side_effects=net is not None
@@ -261,7 +262,7 @@
 
 def front_body(
     x_own_ref, w_all_ref, fs_ref, list_ref, count_ref, g1, b1, bo, g2, b2, bd, bqkv, bup,
-    p_ref, x_ref, h_ref, qkv_ref, table_ref, w_ref, att_ref, den_ref, s_send, s_got, e_ref, mk_ref, pq_ref, pk_ref, send, recv, local,
+    p_ref, x_ref, h_ref, qkv_ref, table_ref, w_ref, att_ref, den_ref, kept_ref, s_send, s_got, e_ref, mk_ref, pq_ref, pk_ref, keep_ref, acc_ref, send, recv, local, keep_sems,
 ):
     rows, width = x_own_ref.shape
     own = width // 2
@@ -314,7 +315,10 @@
         table_ref[i // 2, e * dim : (e + 1) * dim, (2 * e + 1) * feats : (2 * e + 2) * feats] = s_got[i]
     x_copy.wait()
     qkv_tiles(tiles, 2 * tiles, x_ref, p_ref, w_ref, h_ref, qkv_ref)
-    att_heads(qkv_ref, table_ref, list_ref, count_ref, e_ref, mk_ref, att_ref, den_ref, pq_ref, pk_ref)
+    att_heads(
+        qkv_ref, table_ref, list_ref, count_ref, e_ref, mk_ref, att_ref, den_ref, kept_ref, pq_ref, pk_ref, keep_ref,
+        acc_ref, keep_sems,
+    )
 
 
 def head_parts(qkv_ref, h):
@@ -339,28 +343,41 @@
         for part, out in ((0, pq_ref), (1, pk_ref)):
             t = qkv_ref[rows, cols(part)]
             w = jnp.where(mine, t.astype(F32), 0.0)
-            sq = jnp.sum(w * w, axis=-1, keepdims=True) * (0.5 * HEAD_DIM ** (-0.5))
-            lifted = nn(t, signs) * HEAD_DIM ** (-0.25)
-            out[rows, :] = (jnp.exp(lifted - sq) * feats ** (-0.5)).astype(BF)
+            sq = jnp.sum(w * w, axis=-1, keepdims=True) * (LOG2E * 0.5 * HEAD_DIM ** (-0.5)) + 0.5 * math.log2(feats)
+            out[rows, :] = jnp.exp2(nn(t, signs) * (LOG2E * HEAD_DIM ** (-0.25)) - sq).astype(BF)
         return 0
 
     lax.fori_loop(0, qkv_ref.shape[0] // TILE, step, 0)
 
 
-def att_heads(qkv_ref, s_ref, list_ref, count_ref, e_ref, mk_ref, att_ref, den_ref, pq_ref, pk_ref):
+def att_heads(
+    qkv_ref, s_ref, list_ref, count_ref, e_ref, mk_ref, att_ref, den_ref, kept_ref, pq_ref, pk_ref, p_ref, acc_ref, sems
+):
+    heads = qkv_ref.shape[1] // (3 * HEAD_DIM)
+
+    def keep(h):
+        slot = lax.rem(h, 2)
+        return pltpu.make_async_copy(p_ref.at[slot], kept_ref.at[h], sems.at[slot])
+
     def head(h, _):
         p, e, lane, mine, cols = head_parts(qkv_ref, h)
-        mk_ref[...] = tn(matches(list_ref, count_ref, h), e_ref[...])
+        slot = lax.rem(h, 2)
+        mk_ref[...] = nn(matches(list_ref, count_ref, h), e_ref[...])
         lift_all(qkv_ref, s_ref, h, pq_ref, pk_ref)
         zero = jnp.zeros((), BF)
-        v_one = jnp.where(mine, qkv_ref[:, cols(2)], jnp.ones((), BF))
+
+        @pl.when(h >= 2)
+        def _():
+            keep(h - 2).wait()
+
+        acc_ref[...] = jnp.zeros_like(acc_ref)
 
         def step(i, _):
             rows = ds(i, ATILE)
-            q = jnp.where(mine, qkv_ref[rows, cols(0)] * BF(HEAD_DIM ** (-0.5)), zero)
-            ex = jnp.exp(nt(q, qkv_ref[:, cols(1)]))
-            low = nt(pq_ref[rows, :], pk_ref[...])
-            per = ATILE // BLOCK
+            k = jnp.where(mine, qkv_ref[rows, cols(1)] * BF(HEAD_DIM ** (-0.5)), zero)
+            v_one = jnp.where(mine, qkv_ref[rows, cols(2)], jnp.ones((), BF))
+            ex = jnp.exp(nt(k, qkv_ref[:, cols(0)]))
+            low = nt(pk_ref[rows, :], pq_ref[...])
             marks = local_marks(mk_ref, i, ATILE)
             probs = jnp.concatenate(
                 [
@@ -369,11 +386,20 @@
                         ex[j * BLOCK : (j + 1) * BLOCK],
                         low[j * BLOCK : (j + 1) * BLOCK],
                     )
-                    for j in range(per)
+                    for j in range(ATILE // BLOCK)
                 ],
                 axis=0,
             ).astype(BF)
-            both = nn(probs, v_one)
+            p_ref[slot, rows, :] = probs
+            acc_ref[...] += tn(probs, v_one)
+            return 0
+
+        lax.fori_loop(0, qkv_ref.shape[0] // ATILE, step, 0)
+        keep(h).start()
+
+        def last(i, _):
+            rows = ds(i, TILE)
+            both = acc_ref[rows, :]
             den = pltpu.roll(both, HEAD_DIM, 1)
             out_cols = ds(p, 128)
             att = (both / den).astype(BF)
@@ -381,10 +407,12 @@
             den_ref[rows, out_cols] = jnp.where(mine, den, den_ref[rows, out_cols])
             return 0
 
-        lax.fori_loop(0, qkv_ref.shape[0] // ATILE, step, 0)
+        lax.fori_loop(0, qkv_ref.shape[0] // TILE, last, 0)
         return 0
 
-    lax.fori_loop(0, qkv_ref.shape[1] // (3 * HEAD_DIM), head, 0)
+    lax.fori_loop(0, heads, head, 0)
+    keep(heads - 2).wait()
+    keep(heads - 1).wait()
 
 
 def mix_tiles(x_ref, mine_ref, other_ref, w_ref, b_ref, g_ref, s_ref, mixed_ref, h_ref):
@@ -407,9 +435,8 @@
     lax.fori_loop(0, x_ref.shape[0] // TILE, step, 0)
 
 
-def ff_tiles(h_ref, og_ref, up_ref, down_ref, bias, act_ref, gp_ref, hid_ref, gh_ref, db_ref, send):
+def ff_forward(h_ref, up_ref, down_ref, bias, act_ref, slope_ref, hid_ref, send):
     tiles = h_ref.shape[0] // TILE
-    db_ref[...] = jnp.zeros_like(db_ref)
 
     def step(i, _):
         tile = lax.rem(i + tiles // 2, tiles)
@@ -419,14 +446,26 @@
         th = jnp.tanh(GELU_A * v * (1.0 + GELU_B * vv))
         half = 0.5 + 0.5 * th
         act = (v * half).astype(BF)
-        slope = half + (0.5 * GELU_A) * v * (1.0 - th * th) * (1.0 + (3.0 * GELU_B) * vv)
+        slope_ref[rows, :] = half + (0.5 * GELU_A) * v * (1.0 - th * th) * (1.0 + (3.0 * GELU_B) * vv)
         act_ref[rows, :] = act
         hid_ref[rows, :] = nn(act, down_ref[...]).astype(BF)
-        gp = nt(og_ref[rows, :], down_ref[...]) * slope
-        gpl = gp.astype(BF)
-        gp_ref[rows, :] = gpl
-        db_ref[...] += jnp.sum(gpl.astype(F32), axis=0, keepdims=True)
-        gh_ref[rows, :] = nt(gpl, up_ref[...]).astype(BF)
+        send(i, tile)
+        return 0
+
+    lax.fori_loop(0, tiles, step, 0)
+
+
+def ff_backward(og_ref, up_ref, down_ref, slope_ref, gp_ref, gh_ref, db_ref, send):
+    tiles = og_ref.shape[0] // TILE
+    db_ref[...] = jnp.zeros_like(db_ref)
+
+    def step(i, _):
+        tile = lax.rem(i + tiles // 2, tiles)
+        rows = ds(tile, TILE)
+        gp = (nt(og_ref[rows, :], down_ref[...]) * slope_ref[rows, :]).astype(BF)
+        gp_ref[rows, :] = gp
+        db_ref[...] += jnp.sum(gp.astype(F32), axis=0, keepdims=True)
+        gh_ref[rows, :] = nt(gp, up_ref[...]).astype(BF)
         send(i, tile)
         return 0
 
@@ -439,12 +478,14 @@
         out_ref[net.place(first + i)] = value[i * rows : (i + 1) * rows].astype(BF)
 
 
-def ff_weight(net, lhs_ref, rhs_ref, out_ref):
+def ff_weight(net, lhs_ref, rhs_ref, outs):
     wide = lhs_ref.shape[1] // 2
-    per = wide // out_ref.shape[1]
+    per = wide // outs[0].shape[1]
 
     def step(i, _):
-        put_chunks(out_ref, i * per, tn(lhs_ref[:, ds(i, wide)], rhs_ref[...]), net)
+        value = tn(lhs_ref[:, ds(i, wide)], rhs_ref[...])
+        for j, out in enumerate(outs):
+            put_chunks(out, i * per, value[:, j * out.shape[2] : (j + 1) * out.shape[2]], net)
         return 0
 
     lax.fori_loop(0, 2, step, 0)
@@ -494,7 +535,7 @@
 def mid_body(
     n, x_ref, att_ref, wout_ref, p_ref, og_own_ref, up_ref, down_ref,
     gm_ref, gatt_ref, dout_ref, y_ref, vec_ref, dup_ref, ddown_ref, dbup_ref,
-    far, og, mixed, h, act, gp, hid, gh, hid_got, gh_got, gb, ddown, ddown_got, send, recv, down_send, down_recv,
+    far, og, mixed, h, act, gp, hid, gh, hid_got, gh_got, gb, ddown, ddown_got, slope, send, recv, down_send, down_recv,
 ):
     net = Net(n)
     down = Scatter(net, ddown, [ddown_got, ddown_ref, None, None, None], down_send, down_recv)
@@ -520,7 +561,6 @@
     for c in atts:
         c.wait()
     mix_tiles(x_ref, att_ref, far, wout_ref, bout_ref, g_ref, s_ref, mixed, h)
-    og_copy.wait()
 
     def gh_copy(i, tile):
         return copy(3 + i, gh.at[ds(tile, TILE)], gh_got.at[ds(i, TILE)])
@@ -528,17 +568,20 @@
     def hid_copy(i, tile):
         return copy(3 + tiles + i, hid.at[ds(tile, TILE)], hid_got.at[ds(i, TILE)])
 
-    def send_tile(i, tile):
+    def send_gh(i, tile):
         gh_copy(i, tile).start()
 
+    def send_hid(i, tile):
         @pl.when(i < tiles // 2)
         def _():
             hid_copy(i, tile).start()
 
-    ff_tiles(h, og, up_ref, down_ref, bup, act, gp, hid, gh, dbup_ref, send_tile)
-    ff_weight(net, og, act, ddown)
+    ff_forward(h, up_ref, down_ref, bup, act, slope, hid, send_hid)
+    og_copy.wait()
+    ff_weight(net, og, act, [ddown])
     down.start(0)
-    ff_weight(net, h, gp, dup_ref)
+    ff_backward(og, up_ref, down_ref, slope, gp, gh, dbup_ref, send_gh)
+    ff_weight(net, h, gp, [dup_ref.at[0], dup_ref.at[1]])
     for i in range(tiles):
         gh_copy(i, (i + tiles // 2) % tiles).wait()
     for i in range(tiles // 2):
@@ -551,12 +594,26 @@
 
 
 def heads_back(
-    qkv_ref, s_ref, list_ref, count_ref, e_ref, mk_ref, att_ref, den_ref, gatt_ref, gqkv_ref, pq_ref, pk_ref, gn_ref, gq_ref, gpq_ref, after
+    qkv_ref, s_ref, list_ref, count_ref, kept_ref, p_ref, sems, e_ref, mk_ref, att_ref, den_ref, gatt_ref, gqkv_ref, pq_ref, pk_ref, gn_ref, gq_ref, gpq_ref, after
 ):
     rows_all = qkv_ref.shape[0]
     scale = HEAD_DIM ** (-0.5)
 
+    heads = qkv_ref.shape[1] // (3 * HEAD_DIM)
+
+    def fetch(h):
+        slot = lax.rem(h, 2)
+        return pltpu.make_async_copy(kept_ref.at[h], p_ref.at[slot], sems.at[slot])
+
+    fetch(0).start()
+
     def head(h, _):
+        slot = lax.rem(h, 2)
+
+        @pl.when(h + 1 < heads)
+        def _():
+            fetch(h + 1).start()
+
         p, e, lane, mine, cols = head_parts(qkv_ref, h)
         feats = pq_ref.shape[1]
         zero = jnp.zeros((), BF)
@@ -585,26 +642,24 @@
         def put(part, rows, value):
             gqkv_ref[rows, cols(part)] = jnp.where(mine, value.astype(BF), gqkv_ref[rows, cols(part)])
 
+        fetch(h).wait()
+
         def step(i, _):
             rows = ds(i, BTILE)
             k = jnp.where(mine, qkv_ref[rows, cols(1)] * BF(scale), zero)
             v_one = jnp.where(mine, qkv_ref[rows, cols(2)], jnp.ones((), BF))
             q_all = qkv_ref[:, cols(0)]
             pk = pk_ref[rows, :]
-            ex = jnp.exp(nt(k, q_all))
-            low = nt(pk, pq_ref[...])
+            probs = p_ref[slot, rows, :]
             da = nt(v_one, gn_ref[...])
-            per = BTILE // BLOCK
             marks = local_marks(mk_ref, i, BTILE)
-            probs, dl, gs = [], [], []
-            for j in range(per):
+            dl, gs = [], []
+            for j in range(BTILE // BLOCK):
                 part = slice(j * BLOCK, (j + 1) * BLOCK)
                 on = marks[j : j + 1, :] > 0.5
-                exj, daj = ex[part], da[part]
-                probs.append(jnp.where(on, exj, low[part]))
+                daj = da[part]
                 dl.append(jnp.where(on, 0.0, daj))
-                gs.append(jnp.where(on, daj * exj, 0.0))
-            probs = jnp.concatenate(probs, axis=0).astype(BF)
+                gs.append(jnp.where(on, daj * probs[part].astype(F32), 0.0))
             dl = jnp.concatenate(dl, axis=0).astype(BF)
             gs = jnp.concatenate(gs, axis=0).astype(BF)
             put(2, rows, nn(probs, gn_ref[...]))
@@ -632,20 +687,20 @@
 
 
 def back_body(
-    n, qkv_ref, s_ref, list_ref, count_ref, att_ref, den_ref, gatt_ref, h_ref, w_ref, x_ref, p_ref, gm_ref, up_ref, down_ref, out_ref,
+    n, qkv_ref, s_ref, list_ref, count_ref, kept_ref, att_ref, den_ref, gatt_ref, h_ref, w_ref, x_ref, p_ref, gm_ref, up_ref, down_ref, out_ref,
     vec_ref, bup_ref, dx_ref, oup_ref, odown_ref, oout_ref, oqkv_ref, orows_ref, obqkv_ref, obup_ref, *scratch,
 ):
     net = Net(n)
-    bufs, tail = (None, down_ref) + scratch[:28], scratch[28:]
-    e_ref, mk_ref, pq, pk, gn, gq, gpq, gqkv, gw, gh_send, gh_got, sout, rout, sqkv, rqkv, vrows, vbqkv, vbup, send, recv = tail
+    bufs, tail = (None, down_ref) + scratch[:33], scratch[33:]
+    kept_buf, keep_sems, e_ref, mk_ref, pq, pk, gn, gq, gpq, gqkv, gw, gh_send, gh_got, sout, rout, sqkv, rqkv, vrows, vbqkv, vbup, send, recv = tail
     f = net.f
     other = {"feat": 1 - f}
-    parts = [
-        Scatter(net, src, bufs[5 * i : 5 * i + 5], send.at[i], recv.at[i])
-        for i, src in enumerate((None, up_ref, out_ref, gw.at[0], gw.at[1], gw.at[2]))
+    sources = (None, up_ref.at[0], out_ref, gw.at[0], gw.at[1], gw.at[2], up_ref.at[1])
+    lanes_of = (0, 1, 2, 3, 4, 5, 10)
+    down, up_low, out, *pairs, up_high = [
+        Scatter(net, src, bufs[5 * i : 5 * i + 5], send.at[k], recv.at[k])
+        for i, (src, k) in enumerate(zip(sources, lanes_of))
     ]
-    down, up, out = parts[:3]
-    pairs = parts[3:]
     vectors = [Vector(net, ref, send.at[6 + i], recv.at[6 + i]) for i, ref in enumerate((vrows, vbqkv, vbup))]
     last = net.slots() - 1
     half = sout.shape[1]
@@ -686,29 +741,33 @@
     fill_spread(e_ref)
     net.barrier()
     down.start(1)
-    up.start(0)
+    up_low.start(0)
+    up_high.start(0)
     out.start(0)
 
     def after1():
         move(down, 1)
+        move(up_low, 0)
         weight(0)
 
     def after2():
-        move(up, 0)
+        move(up_high, 0)
+        move(up_low, 1)
+
+    def after3():
         move(out, 0)
         move(pairs[0], 0)
-
-    def after3():
-        move(up, 1)
-        move(out, 1)
+        move(up_high, 1)
         weight(1)
 
     def after4():
         down.finish(2, whole(odown_ref))
+        move(out, 1)
         move(pairs[0], 1)
+        move(pairs[1], 0)
 
     heads_back(
-        qkv_ref, s_ref, list_ref, count_ref, e_ref, mk_ref, att_ref, den_ref, gatt_ref, gqkv, pq, pk, gn, gq, gpq,
+        qkv_ref, s_ref, list_ref, count_ref, kept_ref, kept_buf, keep_sems, e_ref, mk_ref, att_ref, den_ref, gatt_ref, gqkv, pq, pk, gn, gq, gpq,
         {1: after1, 2: after2, 3: after3, 4: after4},
     )
     weight(2)
@@ -722,7 +781,7 @@
     total = lax.fori_loop(0, tiles, far, jnp.zeros((1, 3 * own), F32))
     gh_swap = swap(9, gh_send, gh_got)
     gh_swap.start()
-    move(pairs[1], 0)
+    move(pairs[1], 1)
 
     def sums(i, total):
         return total + jnp.sum(gqkv[ds(i, TILE), :].astype(F32), axis=0, keepdims=True)
@@ -732,12 +791,12 @@
     for i in range(3):
         vbqkv[0, :, ds(2 * i + f, own)] = total[:, i * own : (i + 1) * own]
     vbup[0] = bup_ref[...]
+    up_low.finish(2, whole(oup_ref.at[:, 0 : oup_ref.shape[1] // 2]))
     out.finish(2, halves(sout))
     out_swap = swap(2, sout.at[1 - f], rout)
     out_swap.start()
-    up.finish(2, whole(oup_ref))
-    move(pairs[1], 1)
     move(pairs[2], 0)
+    up_high.finish(2, whole(oup_ref.at[:, oup_ref.shape[1] // 2 :]))
     gh_swap.wait()
     gain = p_ref[GAIN1 : GAIN1 + 1, :]
     vrows[0] = vec_ref[...]
@@ -830,17 +889,21 @@
     masks = [pltpu.VMEM((NB, tokens), BF), pltpu.VMEM((NB, tokens), F32)]
     sign_half = pltpu.VMEM((half_heads, HEAD_DIM, feats // 2), BF)
     two = pltpu.SemaphoreType.DMA((2,))
-    params, x, h1, qkv, table, w_own, att, den = call(
+    params, x, h1, qkv, table, w_own, att, den, kept = call(
         front_body,
         [
             ((lines, width), F32),
             ((tokens, width), BF), ((tokens, width), BF), ((tokens, 3 * half_width), BF),
             ((half_heads // 2, 2 * HEAD_DIM, 2 * feats), BF), ((width, 3 * half_width), BF),
-            ((tokens, half_width), BF), ((tokens, half_width), F32),
+            ((tokens, half_width), BF), ((tokens, half_width), F32), ((half_heads, tokens, tokens), BF),
         ],
         [layer_input, w_qkv, feature_signs, lists, match_count] + vectors,
         specs=[VMEM, ANY] + [VMEM] * (3 + len(vectors)),
-        scratch=[sign_half, sign_half] + masks + [phi, phi, two, two, pltpu.SemaphoreType.DMA((3,))],
+        scratch=[sign_half, sign_half] + masks + [
+            phi, phi, pltpu.VMEM((2, tokens, tokens), BF), pltpu.VMEM((tokens, 128), F32), two, two,
+            pltpu.SemaphoreType.DMA((3,)), two,
+        ],
+        out_specs=[VMEM] * 8 + [ANY],
         name="front", net=3,
     )
     big, wide = pltpu.VMEM((tokens, width), BF), pltpu.VMEM((tokens, hidden), BF)
@@ -851,7 +914,7 @@
         functools.partial(mid_body, n),
         [
             ((rows, width), F32), ((tokens, half_width), F32), ((n, chunk, half_width), BF), ((rows, width), BF),
-            ((8, width), F32), ((n, chunk, hidden), BF), (down_bufs[1].shape, BF), ((1, hidden), F32),
+            ((8, width), F32), ((2, n, chunk, hidden // 2), BF), (down_bufs[1].shape, BF), ((1, hidden), F32),
         ],
         [
             x, att, w_out, params, out_grad, w_up, w_down,
@@ -859,16 +922,16 @@
         scratch=[
             pltpu.VMEM((tokens, half_width), BF), big, pltpu.VMEM((tokens, width), F32), big, wide, wide, big, big,
             pltpu.VMEM((rows, width), BF), big, big, pltpu.VMEM((n, chunk, hidden), BF), down_bufs[0],
-            pair_sems, pair_sems, down_sems, down_sems,
+            pltpu.VMEM((tokens, hidden), F32), pair_sems, pair_sems, down_sems, down_sems,
         ],
         name="mid", net=2,
     )
     slots = sum(split(n)) + split(n)[0] - 3 + 1
     bufs = down_bufs[2:]
-    for cols in (hidden, half_width, half_width, half_width, half_width):
+    for cols in (hidden // 2, half_width, half_width, half_width, half_width, hidden // 2):
         bufs += scatter_bufs(n, chunk, cols)
     half_chunk = chunk // 2
-    sems = pltpu.SemaphoreType.DMA((10, slots))
+    sems = pltpu.SemaphoreType.DMA((11, slots))
     sums = call(
         functools.partial(back_body, n),
         [
@@ -876,9 +939,10 @@
             ((half_chunk, 3 * width), F32), ((8, 128), F32), ((1, 128), F32), ((1, 128), F32),
         ],
         [
-            qkv, table, lists, match_count, att, den, gatt, h1, w_own, layer_input, params, gm, d_up, d_down, d_out, vec2, d_bup,
+            qkv, table, lists, match_count, kept, att, den, gatt, h1, w_own, layer_input, params, gm, d_up, d_down, d_out, vec2, d_bup,
         ],
-        scratch=bufs + masks + [
+        specs=[VMEM] * 4 + [ANY] + [VMEM] * 13,
+        scratch=bufs + [pltpu.VMEM((2, tokens, tokens), BF), two] + masks + [
             phi, phi, pltpu.VMEM((tokens, 128), BF), pltpu.VMEM((tokens, 128), F32), pltpu.VMEM((tokens, feats), F32),
             pltpu.VMEM((tokens, 3 * half_width), BF), pltpu.VMEM((3, n, chunk, half_width), BF),
             pltpu.VMEM((rows, width), BF), pltpu.VMEM((rows, width), BF),

time: 171 us -> 163 us (0.953)
  Pallas kernels: 169 us -> 160 us
    pallas_call x4, Pallas kernels: 169 us -> 160 us  [call(): pl.pallas_call(body, out_shape=[jax.ShapeDtypeStruct(s, d) for s, d in ou...]
where the time goes in v6:
time: 163 us; the launch traced here: 162 us
  Pallas kernels  160 us (98%)
    pallas_call x4, Pallas kernels, call(): pl.pallas_call(body, out_shape=[jax.ShapeDtypeStruct(s, d) for s, d in ou...  160 us

profile of v6, /device:TPU:0, one launch (start us, length us, event | category | flops | bytes accessed | tf_op | source)
XLA Modules:
  0.0 162.5 jit_solution(3245879955677020538)
XLA Ops:
  0.6 1.3 copy.31.count_ref
  1.9 33.3 %front.1 = (f32[11,768]{1,0:T(8,128)}, bf16[1024,768]{1,0:T(8,128)(2,1)}, bf16[1024,768]{1,0:T(8,128)(2,1)}, bf16[1024,1152]{1,0:T(8,128)(2,1)}, bf16[3,128,512]...) custom-call(bf16[512,768]{1,0:T(8,128)(2,1)} %x_ref.1, ...), custom_call_target="tpu_custom_call" | custom-call | tf_op jit(solution)/shard_map/front/pallas_call | solution.py:209
  35.2 43.7 %mid.1 = (f32[512,768]{1,0:T(8,128)}, f32[1024,384]{1,0:T(8,128)}, bf16[16,48,384]{2,1,0:T(8,128)(2,1)}, bf16[512,768]{1,0:T(8,128)(2,1)}, f32[8,768]{1,0:T(8,12...) custom-call(bf16[1024,768]{1,0:T(8,128)(2,1)} %get-tuple-element.53.x_ref, ...), custom_call_target="tpu_custom_call" | custom-call | tf_op jit(solution)/shard_map/mid/pallas_call | solution.py:209
  78.9 79.8 %back.1 = (f32[512,768]{1,0:T(8,128)}, f32[48,1536]{1,0:T(8,128)}, f32[48,1536]{1,0:T(8,128)}, f32[24,768]{1,0:T(8,128)}, f32[24,2304]{1,0:T(8,128)}, /*index=5*...) custom-call(bf16[1024,1152]{1,0:T(8,128)(2,1)} %get-tuple-element.57.qkv_ref, ...), custom_call_target="tpu_custom_call" | custom-call | tf_op jit(solution)/shard_map/back/pallas_call | solution.py:209
  158.7 3.7 %emit.1 = (bf16[512,768]{1,0:T(8,128)(2,1)}, f32[512,768]{1,0:T(8,128)}, f32[48,1536]{1,0:T(8,128)}, f32[48,1536]{1,0:T(8,128)}, f32[24,768]{1,0:T(8,128)}, /*in...) custom-call(bf16[512,768]{1,0:T(8,128)(2,1)} %get-tuple-element.56.y, ...), custom_call_target="tpu_custom_call" | custom-call | tf_op jit(solution)/shard_map/emit/pallas_call | solution.py:209

commit v7 on v6

--- a/solution.py
+++ b/solution.py
@@ -262,7 +262,9 @@
 
 def front_body(
     x_own_ref, w_all_ref, fs_ref, list_ref, count_ref, g1, b1, bo, g2, b2, bd, bqkv, bup,
-    p_ref, x_ref, h_ref, qkv_ref, table_ref, w_ref, att_ref, den_ref, kept_ref, s_send, s_got, e_ref, mk_ref, pq_ref, pk_ref, keep_ref, acc_ref, send, recv, local, keep_sems,
+    p_ref, x_out, h_out, qkv_out, table_ref, att_ref, den_ref, kept_ref,
+    x_ref, h_ref, qkv_ref, w_ref, s_send, s_got, e_ref, mk_ref, pq_ref, pk_ref, keep_ref, acc_ref,
+    send, recv, local, keep_sems, store,
 ):
     rows, width = x_own_ref.shape
     own = width // 2
@@ -315,10 +317,16 @@
         table_ref[i // 2, e * dim : (e + 1) * dim, (2 * e + 1) * feats : (2 * e + 2) * feats] = s_got[i]
     x_copy.wait()
     qkv_tiles(tiles, 2 * tiles, x_ref, p_ref, w_ref, h_ref, qkv_ref)
+    pairs = ((x_ref, x_out), (h_ref, h_out), (qkv_ref, qkv_out))
+    stores = [pltpu.make_async_copy(src, dst, store.at[i]) for i, (src, dst) in enumerate(pairs)]
+    for c in stores:
+        c.start()
     att_heads(
         qkv_ref, table_ref, list_ref, count_ref, e_ref, mk_ref, att_ref, den_ref, kept_ref, pq_ref, pk_ref, keep_ref,
         acc_ref, keep_sems,
     )
+    for c in stores:
+        c.wait()
 
 
 def head_parts(qkv_ref, h):
@@ -533,9 +541,9 @@
 
 
 def mid_body(
-    n, x_ref, att_ref, wout_ref, p_ref, og_own_ref, up_ref, down_ref,
+    n, x_ref, att_ref, wout_ref, p_ref, og_own_ref, up_all, down_all,
     gm_ref, gatt_ref, dout_ref, y_ref, vec_ref, dup_ref, ddown_ref, dbup_ref,
-    far, og, mixed, h, act, gp, hid, gh, hid_got, gh_got, gb, ddown, ddown_got, slope, send, recv, down_send, down_recv,
+    far, og, mixed, h, act, gp, hid, gh, hid_got, gh_got, gb, ddown, ddown_got, slope, up_ref, down_ref, send, recv, down_send, down_recv, local,
 ):
     net = Net(n)
     down = Scatter(net, ddown, [ddown_got, ddown_ref, None, None, None], down_send, down_recv)
@@ -550,6 +558,9 @@
             src_ref=src, dst_ref=dst, send_sem=send.at[k], recv_sem=recv.at[k], device_id=other, device_id_type=MESH
         )
 
+    loads = [pltpu.make_async_copy(a, b, local.at[i]) for i, (a, b) in enumerate(((up_all, up_ref), (down_all, down_ref)))]
+    for c in loads:
+        c.start()
     net.barrier()
     low, high = pl.ds(0, rows), pl.ds(rows, rows)
     atts = [copy(0, att_ref.at[low], far.at[high]), copy(1, att_ref.at[high], far.at[low])]
@@ -576,6 +587,8 @@
         def _():
             hid_copy(i, tile).start()
 
+    for c in loads:
+        c.wait()
     ff_forward(h, up_ref, down_ref, bup, act, slope, hid, send_hid)
     og_copy.wait()
     ff_weight(net, og, act, [ddown])
@@ -687,12 +700,12 @@
 
 
 def back_body(
-    n, qkv_ref, s_ref, list_ref, count_ref, kept_ref, att_ref, den_ref, gatt_ref, h_ref, w_ref, x_ref, p_ref, gm_ref, up_ref, down_ref, out_ref,
+    n, qkv_ref, s_ref, list_ref, count_ref, kept_ref, att_ref, den_ref, gatt_ref, h_all, w_all, x_all, p_ref, gm_all, up_ref, down_ref, out_ref,
     vec_ref, bup_ref, dx_ref, oup_ref, odown_ref, oout_ref, oqkv_ref, orows_ref, obqkv_ref, obup_ref, *scratch,
 ):
     net = Net(n)
     bufs, tail = (None, down_ref) + scratch[:33], scratch[33:]
-    kept_buf, keep_sems, e_ref, mk_ref, pq, pk, gn, gq, gpq, gqkv, gw, gh_send, gh_got, sout, rout, sqkv, rqkv, vrows, vbqkv, vbup, send, recv = tail
+    kept_buf, keep_sems, h_ref, w_ref, x_ref, gm_ref, local, e_ref, mk_ref, pq, pk, gn, gq, gpq, gqkv, gw, gh_send, gh_got, sout, rout, sqkv, rqkv, vrows, vbqkv, vbup, send, recv = tail
     f = net.f
     other = {"feat": 1 - f}
     sources = (None, up_ref.at[0], out_ref, gw.at[0], gw.at[1], gw.at[2], up_ref.at[1])
@@ -738,6 +751,15 @@
             put_chunks(gw.at[p], i * per, tn(h_ref[:, i * own : (i + 1) * own], g), net)
         pairs[p].start(0)
 
+    loads = [
+        pltpu.make_async_copy(a, b, local.at[i])
+        for i, (a, b) in enumerate(((h_all, h_ref), (x_all, x_ref), (gm_all, gm_ref)))
+    ] + [
+        pltpu.make_async_copy(w_all.at[:, ds(2 * i + f, own)], w_ref.at[:, pl.ds(i * own, own)], local.at[3 + i])
+        for i in range(3)
+    ]
+    for c in loads:
+        c.start()
     fill_spread(e_ref)
     net.barrier()
     down.start(1)
@@ -748,6 +770,7 @@
     def after1():
         move(down, 1)
         move(up_low, 0)
+        loads[0].wait()
         weight(0)
 
     def after2():
@@ -771,6 +794,8 @@
         {1: after1, 2: after2, 3: after3, 4: after4},
     )
     weight(2)
+    for c in loads[1:]:
+        c.wait()
     tiles = rows // TILE
 
     def far(i, total):
@@ -888,22 +913,24 @@
     phi = pltpu.VMEM((tokens, feats), BF)
     masks = [pltpu.VMEM((NB, tokens), BF), pltpu.VMEM((NB, tokens), F32)]
     sign_half = pltpu.VMEM((half_heads, HEAD_DIM, feats // 2), BF)
-    two = pltpu.SemaphoreType.DMA((2,))
-    params, x, h1, qkv, table, w_own, att, den, kept = call(
+    two, three = pltpu.SemaphoreType.DMA((2,)), pltpu.SemaphoreType.DMA((3,))
+    full, qkv_buf = pltpu.VMEM((tokens, width), BF), pltpu.VMEM((tokens, 3 * half_width), BF)
+    w_buf = pltpu.VMEM((width, 3 * half_width), BF)
+    params, x, h1, qkv, table, att, den, kept = call(
         front_body,
         [
             ((lines, width), F32),
             ((tokens, width), BF), ((tokens, width), BF), ((tokens, 3 * half_width), BF),
-            ((half_heads // 2, 2 * HEAD_DIM, 2 * feats), BF), ((width, 3 * half_width), BF),
+            ((half_heads // 2, 2 * HEAD_DIM, 2 * feats), BF),
             ((tokens, half_width), BF), ((tokens, half_width), F32), ((half_heads, tokens, tokens), BF),
         ],
         [layer_input, w_qkv, feature_signs, lists, match_count] + vectors,
         specs=[VMEM, ANY] + [VMEM] * (3 + len(vectors)),
-        scratch=[sign_half, sign_half] + masks + [
+        scratch=[full, full, qkv_buf, w_buf, sign_half, sign_half] + masks + [
             phi, phi, pltpu.VMEM((2, tokens, tokens), BF), pltpu.VMEM((tokens, 128), F32), two, two,
-            pltpu.SemaphoreType.DMA((3,)), two,
+            three, two, three,
         ],
-        out_specs=[VMEM] * 8 + [ANY],
+        out_specs=[VMEM, ANY, ANY, ANY, VMEM, VMEM, VMEM, ANY],
         name="front", net=3,
     )
     big, wide = pltpu.VMEM((tokens, width), BF), pltpu.VMEM((tokens, hidden), BF)
@@ -919,10 +946,12 @@
         [
             x, att, w_out, params, out_grad, w_up, w_down,
         ],
+        specs=[VMEM] * 5 + [ANY] * 2,
         scratch=[
             pltpu.VMEM((tokens, half_width), BF), big, pltpu.VMEM((tokens, width), F32), big, wide, wide, big, big,
             pltpu.VMEM((rows, width), BF), big, big, pltpu.VMEM((n, chunk, hidden), BF), down_bufs[0],
-            pltpu.VMEM((tokens, hidden), F32), pair_sems, pair_sems, down_sems, down_sems,
+            pltpu.VMEM((tokens, hidden), F32), pltpu.VMEM((width, hidden), BF), pltpu.VMEM((hidden, width), BF),
+            pair_sems, pair_sems, down_sems, down_sems, two,
         ],
         name="mid", net=2,
     )
@@ -939,10 +968,13 @@
             ((half_chunk, 3 * width), F32), ((8, 128), F32), ((1, 128), F32), ((1, 128), F32),
         ],
         [
-            qkv, table, lists, match_count, kept, att, den, gatt, h1, w_own, layer_input, params, gm, d_up, d_down, d_out, vec2, d_bup,
+            qkv, table, lists, match_count, kept, att, den, gatt, h1, w_qkv, layer_input, params, gm, d_up, d_down, d_out, vec2, d_bup,
         ],
-        specs=[VMEM] * 4 + [ANY] + [VMEM] * 13,
-        scratch=bufs + [pltpu.VMEM((2, tokens, tokens), BF), two] + masks + [
+        specs=[VMEM] * 4 + [ANY] + [VMEM] * 3 + [ANY] * 3 + [VMEM, ANY] + [VMEM] * 5,
+        scratch=bufs + [
+            pltpu.VMEM((2, tokens, tokens), BF), two, full, w_buf, pltpu.VMEM((rows, width), BF),
+            pltpu.VMEM((rows, width), F32), pltpu.SemaphoreType.DMA((6,)),
+        ] + masks + [
             phi, phi, pltpu.VMEM((tokens, 128), BF), pltpu.VMEM((tokens, 128), F32), pltpu.VMEM((tokens, feats), F32),
             pltpu.VMEM((tokens, 3 * half_width), BF), pltpu.VMEM((3, n, chunk, half_width), BF),
             pltpu.VMEM((rows, width), BF), pltpu.VMEM((rows, width), BF),

time: 163 us -> 158 us (0.969)
  Pallas kernels: 160 us -> 155 us
    pallas_call x4, Pallas kernels: 160 us -> 155 us  [call(): pl.pallas_call(body, out_shape=[jax.ShapeDtypeStruct(s, d) for s, d in ou...]
where the time goes in v7:
time: 158 us; the launch traced here: 157 us
  Pallas kernels  155 us (98%)
    pallas_call x4, Pallas kernels, call(): pl.pallas_call(body, out_shape=[jax.ShapeDtypeStruct(s, d) for s, d in ou...  155 us

profile of v7, /device:TPU:0, one launch (start us, length us, event | category | flops | bytes accessed | tf_op | source)
XLA Modules:
  0.0 157.3 jit_solution(6409138965397080762)
XLA Ops:
  0.6 1.3 copy.31.count_ref
  1.9 31.0 %front.1 = (f32[11,768]{1,0:T(8,128)}, bf16[1024,768]{1,0:T(8,128)(2,1)}, bf16[1024,768]{1,0:T(8,128)(2,1)}, bf16[1024,1152]{1,0:T(8,128)(2,1)}, bf16[3,128,512]...) custom-call(bf16[512,768]{1,0:T(8,128)(2,1)} %x_all.1, ...), custom_call_target="tpu_custom_call" | custom-call | tf_op jit(solution)/shard_map/front/pallas_call | solution.py:209
  33.0 42.4 %mid.1 = (f32[512,768]{1,0:T(8,128)}, f32[1024,384]{1,0:T(8,128)}, bf16[16,48,384]{2,1,0:T(8,128)(2,1)}, bf16[512,768]{1,0:T(8,128)(2,1)}, f32[8,768]{1,0:T(8,12...) custom-call(bf16[1024,768]{1,0:T(8,128)(2,1)} %get-tuple-element.52.x_ref, ...), custom_call_target="tpu_custom_call" | custom-call | tf_op jit(solution)/shard_map/mid/pallas_call | solution.py:209
  75.3 78.2 %back.1 = (f32[512,768]{1,0:T(8,128)}, f32[48,1536]{1,0:T(8,128)}, f32[48,1536]{1,0:T(8,128)}, f32[24,768]{1,0:T(8,128)}, f32[24,2304]{1,0:T(8,128)}, /*index=5*...) custom-call(bf16[1024,1152]{1,0:T(8,128)(2,1)} %get-tuple-element.56.qkv_ref, ...), custom_call_target="tpu_custom_call" | custom-call | tf_op jit(solution)/shard_map/back/pallas_call | solution.py:209
  153.5 3.7 %emit.1 = (bf16[512,768]{1,0:T(8,128)(2,1)}, f32[512,768]{1,0:T(8,128)}, f32[48,1536]{1,0:T(8,128)}, f32[48,1536]{1,0:T(8,128)}, f32[24,768]{1,0:T(8,128)}, /*in...) custom-call(bf16[512,768]{1,0:T(8,128)(2,1)} %get-tuple-element.55.y, ...), custom_call_target="tpu_custom_call" | custom-call | tf_op jit(solution)/shard_map/emit/pallas_call | solution.py:209

commit v8 on v7

--- a/solution.py
+++ b/solution.py
@@ -19,6 +19,7 @@
 TILE = 256
 ATILE = 512
 BTILE = 512
+WTILE = 512
 GELU_A = math.sqrt(2.0 / math.pi)
 GELU_B = 0.044715
 LOG2E = math.log2(math.e)
@@ -347,7 +348,7 @@
     signs = s_ref[p, :, ds(e, feats)]
 
     def step(i, _):
-        rows = ds(i, TILE)
+        rows = ds(i, WTILE)
         for part, out in ((0, pq_ref), (1, pk_ref)):
             t = qkv_ref[rows, cols(part)]
             w = jnp.where(mine, t.astype(F32), 0.0)
@@ -355,7 +356,7 @@
             out[rows, :] = jnp.exp2(nn(t, signs) * (LOG2E * HEAD_DIM ** (-0.25)) - sq).astype(BF)
         return 0
 
-    lax.fori_loop(0, qkv_ref.shape[0] // TILE, step, 0)
+    lax.fori_loop(0, qkv_ref.shape[0] // WTILE, step, 0)
 
 
 def att_heads(
@@ -635,14 +636,14 @@
         first_other = (1 - e) * HEAD_DIM
 
         def prep(i, _):
-            rows = ds(i, TILE)
+            rows = ds(i, WTILE)
             inv = 1.0 / den_ref[rows, ds(p, 128)]
             ga = jnp.where(mine, gatt_ref[rows, ds(p, 128)] * inv, 0.0)
             gd = -jnp.sum(ga * att_ref[rows, ds(p, 128)].astype(F32), axis=-1, keepdims=True)
             gn_ref[rows, :] = jnp.where(lane == first_other, gd, ga).astype(BF)
             return 0
 
-        lax.fori_loop(0, rows_all // TILE, prep, 0)
+        lax.fori_loop(0, rows_all // WTILE, prep, 0)
         gq_ref[...] = jnp.zeros_like(gq_ref)
         gpq_ref[...] = jnp.zeros_like(gpq_ref)
         signs = s_ref[p, :, ds(e, feats)]
@@ -686,12 +687,12 @@
         lax.fori_loop(0, rows_all // BTILE, step, 0)
 
         def last(i, _):
-            rows = ds(i, TILE)
+            rows = ds(i, WTILE)
             gq = gq_ref[rows, :] + lift_back(qkv_ref[rows, cols(0)], pq_ref[rows, :], gpq_ref[rows, :])
             put(0, rows, gq)
             return 0
 
-        lax.fori_loop(0, rows_all // TILE, last, 0)
+        lax.fori_loop(0, rows_all // WTILE, last, 0)
         for k, then in after.items():
             pl.when(h == k)(then)
         return 0
@@ -768,26 +769,26 @@
     out.start(0)
 
     def after1():
+        loads[0].wait()
+        weight(0)
+
+    def after2():
         move(down, 1)
         move(up_low, 0)
-        loads[0].wait()
-        weight(0)
-
-    def after2():
+
+    def after3():
         move(up_high, 0)
         move(up_low, 1)
-
-    def after3():
         move(out, 0)
         move(pairs[0], 0)
+        weight(1)
+
+    def after4():
         move(up_high, 1)
-        weight(1)
-
-    def after4():
-        down.finish(2, whole(odown_ref))
         move(out, 1)
         move(pairs[0], 1)
         move(pairs[1], 0)
+        down.finish(2, whole(odown_ref))
 
     heads_back(
         qkv_ref, s_ref, list_ref, count_ref, kept_ref, kept_buf, keep_sems, e_ref, mk_ref, att_ref, den_ref, gatt_ref, gqkv, pq, pk, gn, gq, gpq,

time: 158 us -> 155 us (0.981)
  Pallas kernels: 155 us -> 152 us
    pallas_call x4, Pallas kernels: 155 us -> 152 us  [call(): pl.pallas_call(body, out_shape=[jax.ShapeDtypeStruct(s, d) for s, d in ou...]
where the time goes in v8:
time: 155 us; the launch traced here: 154 us
  Pallas kernels  152 us (98%)
    pallas_call x4, Pallas kernels, call(): pl.pallas_call(body, out_shape=[jax.ShapeDtypeStruct(s, d) for s, d in ou...  152 us

profile of v8, /device:TPU:0, one launch (start us, length us, event | category | flops | bytes accessed | tf_op | source)
XLA Modules:
  0.0 154.5 jit_solution(15099841527527189209)
XLA Ops:
  0.6 1.3 copy.31.count_ref
  1.9 29.6 %front.1 = (f32[11,768]{1,0:T(8,128)}, bf16[1024,768]{1,0:T(8,128)(2,1)}, bf16[1024,768]{1,0:T(8,128)(2,1)}, bf16[1024,1152]{1,0:T(8,128)(2,1)}, bf16[3,128,512]...) custom-call(bf16[512,768]{1,0:T(8,128)(2,1)} %x_all.1, ...), custom_call_target="tpu_custom_call" | custom-call | tf_op jit(solution)/shard_map/front/pallas_call | solution.py:210
  31.5 42.4 %mid.1 = (f32[512,768]{1,0:T(8,128)}, f32[1024,384]{1,0:T(8,128)}, bf16[16,48,384]{2,1,0:T(8,128)(2,1)}, bf16[512,768]{1,0:T(8,128)(2,1)}, f32[8,768]{1,0:T(8,12...) custom-call(bf16[1024,768]{1,0:T(8,128)(2,1)} %get-tuple-element.52.x_ref, ...), custom_call_target="tpu_custom_call" | custom-call | tf_op jit(solution)/shard_map/mid/pallas_call | solution.py:210
  73.9 76.8 %back.1 = (f32[512,768]{1,0:T(8,128)}, f32[48,1536]{1,0:T(8,128)}, f32[48,1536]{1,0:T(8,128)}, f32[24,768]{1,0:T(8,128)}, f32[24,2304]{1,0:T(8,128)}, /*index=5*...) custom-call(bf16[1024,1152]{1,0:T(8,128)(2,1)} %get-tuple-element.56.qkv_ref, ...), custom_call_target="tpu_custom_call" | custom-call | tf_op jit(solution)/shard_map/back/pallas_call | solution.py:210
  150.7 3.7 %emit.1 = (bf16[512,768]{1,0:T(8,128)(2,1)}, f32[512,768]{1,0:T(8,128)}, f32[48,1536]{1,0:T(8,128)}, f32[48,1536]{1,0:T(8,128)}, f32[24,768]{1,0:T(8,128)}, /*in...) custom-call(bf16[512,768]{1,0:T(8,128)(2,1)} %get-tuple-element.55.y, ...), custom_call_target="tpu_custom_call" | custom-call | tf_op jit(solution)/shard_map/emit/pallas_call | solution.py:210

commit v9 on v8

--- a/solution.py
+++ b/solution.py
@@ -543,8 +543,8 @@
 
 def mid_body(
     n, x_ref, att_ref, wout_ref, p_ref, og_own_ref, up_all, down_all,
-    gm_ref, gatt_ref, dout_ref, y_ref, vec_ref, dup_ref, ddown_ref, dbup_ref,
-    far, og, mixed, h, act, gp, hid, gh, hid_got, gh_got, gb, ddown, ddown_got, slope, up_ref, down_ref, send, recv, down_send, down_recv, local,
+    gm_ref, gatt_ref, dout_ref, y_ref, vec_ref, dup_out, ddown_ref, dbup_ref,
+    far, og, mixed, h, act, gp, hid, gh, hid_got, gh_got, gb, ddown, ddown_got, slope, up_ref, down_ref, dup_ref, send, recv, down_send, down_recv, local,
 ):
     net = Net(n)
     down = Scatter(net, ddown, [ddown_got, ddown_ref, None, None, None], down_send, down_recv)
@@ -596,6 +596,8 @@
     down.start(0)
     ff_backward(og, up_ref, down_ref, slope, gp, gh, dbup_ref, send_gh)
     ff_weight(net, h, gp, [dup_ref.at[0], dup_ref.at[1]])
+    dup_store = pltpu.make_async_copy(dup_ref, dup_out, local.at[2])
+    dup_store.start()
     for i in range(tiles):
         gh_copy(i, (i + tiles // 2) % tiles).wait()
     for i in range(tiles // 2):
@@ -605,6 +607,7 @@
         gm_ref, gatt_ref, dout_ref, y_ref, vec_ref, gb,
     )
     down.finish(0)
+    dup_store.wait()
 
 
 def heads_back(
@@ -948,11 +951,12 @@
             x, att, w_out, params, out_grad, w_up, w_down,
         ],
         specs=[VMEM] * 5 + [ANY] * 2,
+        out_specs=[VMEM] * 5 + [ANY] + [VMEM] * 2,
         scratch=[
             pltpu.VMEM((tokens, half_width), BF), big, pltpu.VMEM((tokens, width), F32), big, wide, wide, big, big,
             pltpu.VMEM((rows, width), BF), big, big, pltpu.VMEM((n, chunk, hidden), BF), down_bufs[0],
             pltpu.VMEM((tokens, hidden), F32), pltpu.VMEM((width, hidden), BF), pltpu.VMEM((hidden, width), BF),
-            pair_sems, pair_sems, down_sems, down_sems, two,
+            pltpu.VMEM((2, n, chunk, hidden // 2), BF), pair_sems, pair_sems, down_sems, down_sems, three,
         ],
         name="mid", net=2,
     )

time: 155 us -> 154 us (level)
  no operation moved by 1% of the time
where the time goes in v9:
time: 154 us
  Pallas kernels  152 us (99%)
    pallas_call x4, Pallas kernels, call(): pl.pallas_call(body, out_shape=[jax.ShapeDtypeStruct(s, d) for s, d in ou...  152 us

profile of v9, /device:TPU:0, one launch (start us, length us, event | category | flops | bytes accessed | tf_op | source)
XLA Modules:
  0.0 153.7 jit_solution(17420817998426778633)
XLA Ops:
  0.6 1.3 copy.31.count_ref
  1.9 29.6 %front.1 = (f32[11,768]{1,0:T(8,128)}, bf16[1024,768]{1,0:T(8,128)(2,1)}, bf16[1024,768]{1,0:T(8,128)(2,1)}, bf16[1024,1152]{1,0:T(8,128)(2,1)}, bf16[3,128,512]...) custom-call(bf16[512,768]{1,0:T(8,128)(2,1)} %x_all.1, ...), custom_call_target="tpu_custom_call" | custom-call | tf_op jit(solution)/shard_map/front/pallas_call | solution.py:210
  31.5 41.6 %mid.1 = (f32[512,768]{1,0:T(8,128)}, f32[1024,384]{1,0:T(8,128)}, bf16[16,48,384]{2,1,0:T(8,128)(2,1)}, bf16[512,768]{1,0:T(8,128)(2,1)}, f32[8,768]{1,0:T(8,12...) custom-call(bf16[1024,768]{1,0:T(8,128)(2,1)} %get-tuple-element.52.x_ref, ...), custom_call_target="tpu_custom_call" | custom-call | tf_op jit(solution)/shard_map/mid/pallas_call | solution.py:210
  73.1 76.8 %back.1 = (f32[512,768]{1,0:T(8,128)}, f32[48,1536]{1,0:T(8,128)}, f32[48,1536]{1,0:T(8,128)}, f32[24,768]{1,0:T(8,128)}, f32[24,2304]{1,0:T(8,128)}, /*index=5*...) custom-call(bf16[1024,1152]{1,0:T(8,128)(2,1)} %get-tuple-element.56.qkv_ref, ...), custom_call_target="tpu_custom_call" | custom-call | tf_op jit(solution)/shard_map/back/pallas_call | solution.py:210
  149.9 3.7 %emit.1 = (bf16[512,768]{1,0:T(8,128)(2,1)}, f32[512,768]{1,0:T(8,128)}, f32[48,1536]{1,0:T(8,128)}, f32[48,1536]{1,0:T(8,128)}, f32[24,768]{1,0:T(8,128)}, /*in...) custom-call(bf16[512,768]{1,0:T(8,128)(2,1)} %get-tuple-element.55.y, ...), custom_call_target="tpu_custom_call" | custom-call | tf_op jit(solution)/shard_map/emit/pallas_call | solution.py:210
